TPU v7x, 32 devices: a whole 2x2x4 slice. The times are simulated.
32 devices in a mesh: wide: 8 (over z, x), narrow: 4 (over y, core).
Axes of the slice: x: 2, y: 2, z: 4, core: 2. Of those that a mesh axis runs over, the one named last changes fastest.
Arguments:
- tokens: bfloat16 [4096, 2048], P('wide', 'narrow'), may hold values from -6 to 6
- cotangent: bfloat16 [4096, 2048], P('wide', 'narrow'), may hold values from -6 to 6
- block_ids: int32 [8, 512], P('wide'), may hold values from 0 to 2, never falling along the last dimension, each value on 1 to 256 neighbouring positions
- routes: int32 [4096, 8], P('wide'), may hold values from 0 to 15, all different within a row; in each aligned block of 512 rows (0 to 511, 512 to 1023, ...) at most 272 rows name the same one
- norm_attn: bfloat16 [2048], P('narrow'), may hold values from 0.5 to 1.5
- w_query: bfloat16 [2048, 2048], P('wide', 'narrow'), may hold values from -0.125 to 0.125
- w_key: bfloat16 [2048, 2048], P('wide', 'narrow'), may hold values from -0.125 to 0.125
- w_value: bfloat16 [2048, 2048], P('wide', 'narrow'), may hold values from -0.125 to 0.125
- norm_query: bfloat16 [2048], P('narrow'), may hold values from 0.5 to 1.5
- norm_key: bfloat16 [2048], P('narrow'), may hold values from 0.5 to 1.5
- w_out: bfloat16 [2048, 2048], P('wide', 'narrow'), may hold values from -1 to 1
- norm_ffn: bfloat16 [2048], P('narrow'), may hold values from 0.5 to 1.5
- w_router: bfloat16 [2048, 16], replicated, may hold values from -0.0625 to 0.0625
- w_gate: bfloat16 [2048, 16, 1024], P('wide', None, 'narrow'), may hold values from -0.125 to 0.125
- w_up: bfloat16 [2048, 16, 1024], P('wide', None, 'narrow'), may hold values from -0.125 to 0.125
- w_down: bfloat16 [2048, 16, 1024], P('wide', None, 'narrow'), may hold values from -1.5 to 1.5
Outputs:
- block_out: bfloat16 [4096, 2048], P('wide', 'narrow')
- grad_tokens: float32 [4096, 2048], P('wide', 'narrow')
- grad_norm_attn: float32 [2048], P('narrow')
- grad_query: float32 [2048, 2048], P('wide', 'narrow')
- grad_key: float32 [2048, 2048], P('wide', 'narrow')
- grad_value: float32 [2048, 2048], P('wide', 'narrow')
- grad_norm_query: float32 [2048], P('narrow')
- grad_norm_key: float32 [2048], P('narrow')
- grad_out: float32 [2048, 2048], P('wide', 'narrow')
- grad_norm_ffn: float32 [2048], P('narrow')
- grad_router: float32 [2048, 16], replicated
- grad_gate: float32 [2048, 16, 1024], P('wide', None, 'narrow')
- grad_up: float32 [2048, 16, 1024], P('wide', None, 'narrow')
- grad_down: float32 [2048, 16, 1024], P('wide', None, 'narrow')
Inputs may be any that keep to these rules, and one draw needn't show every extreme that they name: `block_ids`: block numbers never fall along a sequence; each block has 1 to 256 tokens and some block exactly 256. `routes`: each row names 8 different experts; among the tokens of one sequence no expert is named more than 272 times, a bound that some block reaches.
All inputs are finite; a program needn't handle non-finite values.
Results may differ from a plain program's by a relative error of at most 0.025.
Values may be sent and summed in bfloat16 or wider, within the bound.
No kernel may reach another device: no remote copies, remote signals or barrier semaphores. Data moves between devices by JAX's collectives and lax.ppermute only.
A program may use at most 384 MiB of HBM per device.

v0:
```python
import jax
import jax.numpy as jnp
from jax import lax
from jax.sharding import PartitionSpec as P

HD = 128
EXPERTS = 16
TOP = 8
CAP = 272


EPS = 1e-05
query_rows = 512


def rms_scale(values, scales):
    return values * lax.rsqrt(jnp.mean(values * values, axis=-1, keepdims=True) + EPS) * scales


def rope_tables(length, head_dim):
    exponent = jnp.arange(0, head_dim, 2, dtype=jnp.float32) / head_dim
    angles = jnp.arange(length, dtype=jnp.float32)[:, None] * (10000.0 ** (-exponent))[None, :]
    angles = jnp.concatenate([angles, angles], axis=-1)
    return (jnp.cos(angles)[:, None, :], jnp.sin(angles)[:, None, :])


def rotate_half(values, cosines, sine_table):
    middle = values.shape[-1] // 2
    turned = jnp.concatenate([-values[..., middle:], values[..., :middle]], axis=-1)
    return values * cosines + turned * sine_table


def slot_tables(routes, experts, capacity):
    token_count, top_count = routes.shape
    flat_routes = routes.reshape(-1)
    onehot = (flat_routes[:, None] == jnp.arange(experts, dtype=jnp.int32)[None, :]).astype(
        jnp.int32
    )
    earlier = jnp.cumsum(onehot, axis=0) - onehot
    within = jnp.sum(earlier * onehot, axis=1)
    destination = flat_routes * capacity + within
    pair_ids = jnp.arange(token_count * top_count, dtype=jnp.int32)
    owners = (
        jnp.full((experts * capacity,), token_count * top_count, jnp.int32)
        .at[destination]
        .set(pair_ids)
    )
    return (destination.reshape(token_count, top_count), owners)


def swiglu(gate_in, up_in):
    return jax.nn.silu(gate_in) * up_in


def per_device(
    tokens,
    cotangent,
    block_ids,
    routes,
    norm_attn,
    w_query,
    w_key,
    w_value,
    norm_query,
    norm_key,
    w_out,
    norm_ffn,
    w_router,
    w_gate,
    w_up,
    w_down,
):
    lane_index = lax.axis_index("narrow")
    rows_full, cot_full, gain_attn, gain_ffn = (
        lax.all_gather(tokens, "narrow", axis=1, tiled=True),
        lax.all_gather(cotangent, "narrow", axis=1, tiled=True),
        lax.all_gather(norm_attn, "narrow", axis=0, tiled=True),
        lax.all_gather(norm_ffn, "narrow", axis=0, tiled=True),
    )
    length, model_width = rows_full.shape
    head_cols = w_query.shape[1]
    heads_here = head_cols // HD
    score_scale = HD ** (-0.5)
    rows_float = rows_full.astype(jnp.float32)
    cot_float = cot_full.astype(jnp.float32)
    attn_gain = gain_attn.astype(jnp.float32)
    ffn_gain = gain_ffn.astype(jnp.float32)
    normed = rms_scale(rows_float, attn_gain).astype(jnp.bfloat16)
    query_full, key_full, value_full = (
        lax.all_gather(w_query, "wide", axis=0, tiled=True),
        lax.all_gather(w_key, "wide", axis=0, tiled=True),
        lax.all_gather(w_value, "wide", axis=0, tiled=True),
    )
    query_raw = jnp.dot(normed, query_full, preferred_element_type=jnp.float32)
    key_raw = jnp.dot(normed, key_full, preferred_element_type=jnp.float32)
    value_raw = jnp.dot(normed, value_full, preferred_element_type=jnp.float32)
    square_query, square_key = lax.psum(
        (jnp.sum(query_raw * query_raw, axis=1), jnp.sum(key_raw * key_raw, axis=1)), "narrow"
    )
    query_scale = lax.rsqrt(square_query / model_width + EPS)[:, None]
    key_scale = lax.rsqrt(square_key / model_width + EPS)[:, None]
    query_gain = norm_query.astype(jnp.float32)
    key_gain = norm_key.astype(jnp.float32)
    cosines, sine_table = rope_tables(length, HD)
    query_normed = query_raw * query_scale * query_gain
    key_normed = key_raw * key_scale * key_gain

    def rotate_both(query_in, key_in):
        return (
            rotate_half(query_in.reshape(length, heads_here, HD), cosines, sine_table),
            rotate_half(key_in.reshape(length, heads_here, HD), cosines, sine_table),
        )

    (query_rot, key_rot), rotate_pull = jax.vjp(rotate_both, query_normed, key_normed)
    query_bf = query_rot.astype(jnp.bfloat16)
    key_bf = key_rot.astype(jnp.bfloat16)
    value_bf = value_raw.astype(jnp.bfloat16).reshape(length, heads_here, HD)
    seq_blocks = block_ids[0]
    step_rows = min(query_rows, length)

    def block_scores(offset):
        scores = (
            jnp.einsum("qhd,khd->hqk", query_bf, key_bf, preferred_element_type=jnp.float32)
            * score_scale
        )
        allowed = seq_blocks[None, :] <= seq_blocks[offset : offset + step_rows, None]
        return jnp.where(allowed[None], scores, -1e30)

    offset = 0
    scores = block_scores(offset)
    highest = jnp.max(scores, axis=-1, keepdims=True)
    shifted = jnp.exp(scores - highest)
    totals = jnp.sum(shifted, axis=-1, keepdims=True)
    attn_probs = (shifted / totals).astype(jnp.bfloat16)
    attended_parts = jnp.einsum(
        "hqk,khd->qhd", attn_probs, value_bf, preferred_element_type=jnp.float32
    ).astype(jnp.bfloat16)
    total_parts = highest + jnp.log(totals)
    attended = attended_parts.reshape(length, head_cols)
    out_full = lax.all_gather(w_out, "wide", axis=0, tiled=True)
    out_partial = jnp.einsum("td,cd->tc", attended, out_full, preferred_element_type=jnp.float32)
    residual = rows_float + lax.psum(out_partial, "narrow")
    ffn_in = rms_scale(residual, ffn_gain).astype(jnp.bfloat16)
    logits = jnp.dot(ffn_in, w_router, preferred_element_type=jnp.float32)

    def route_gates(logit_values):
        return jnp.take_along_axis(jax.nn.softmax(logit_values, axis=-1), routes, axis=1)

    gate_values, gate_pull = jax.vjp(route_gates, logits)
    destination, owners = slot_tables(routes, EXPERTS, CAP)
    slot_tokens = owners // TOP
    slot_gates = jnp.concatenate([gate_values.reshape(-1), jnp.zeros((1,), jnp.float32)], axis=0)[
        owners
    ]
    padded_in = jnp.concatenate([ffn_in, jnp.zeros((1, model_width), jnp.bfloat16)], axis=0)
    expert_rows = padded_in[slot_tokens].reshape(EXPERTS, CAP, model_width)
    padded_cot = jnp.concatenate([cot_float, jnp.zeros((1, model_width), jnp.float32)], axis=0)
    slot_cot = padded_cot[slot_tokens]
    gate_full, up_full = (
        lax.all_gather(w_gate, "wide", axis=0, tiled=True),
        lax.all_gather(w_up, "wide", axis=0, tiled=True),
    )
    gate_pre = jnp.einsum(
        "ecd,def->ecf", expert_rows, gate_full, preferred_element_type=jnp.float32
    )
    up_pre = jnp.einsum("ecd,def->ecf", expert_rows, up_full, preferred_element_type=jnp.float32)
    hidden_float, swiglu_pull = jax.vjp(swiglu, gate_pre, up_pre)
    hidden_bf = hidden_float.astype(jnp.bfloat16)
    down_full = lax.all_gather(w_down, "wide", axis=0, tiled=True)
    expert_out = jnp.einsum(
        "ecf,def->ecd", hidden_bf, down_full, preferred_element_type=jnp.float32
    ).reshape(EXPERTS * CAP, model_width)
    moe_partial = (
        jnp.zeros((length + 1, model_width), jnp.float32)
        .at[slot_tokens]
        .add(slot_gates[:, None] * expert_out)[:length]
    )
    slot_dots = jnp.concatenate(
        [jnp.sum(expert_out * slot_cot, axis=1), jnp.zeros((1,), jnp.float32)], axis=0
    )
    dots_partial = slot_dots[destination]
    expert_cot = (
        (slot_gates[:, None] * slot_cot).astype(jnp.bfloat16).reshape(EXPERTS, CAP, model_width)
    )
    hidden_grad = jnp.einsum(
        "ecd,def->ecf", expert_cot, down_full, preferred_element_type=jnp.float32
    )
    gate_grad, up_grad = swiglu_pull(hidden_grad)
    gate_grad_bf = gate_grad.astype(jnp.bfloat16)
    up_grad_bf = up_grad.astype(jnp.bfloat16)
    rows_grad = jnp.einsum(
        "ecf,def->ecd", gate_grad_bf, gate_full, preferred_element_type=jnp.float32
    ) + jnp.einsum("ecf,def->ecd", up_grad_bf, up_full, preferred_element_type=jnp.float32)
    input_partial = (
        jnp.zeros((length + 1, model_width), jnp.float32)
        .at[slot_tokens]
        .add(rows_grad.reshape(EXPERTS * CAP, model_width))[:length]
    )
    pair_dots, input_sum, moe_sum = (
        lax.psum(dots_partial.astype(jnp.bfloat16), "narrow").astype(jnp.float32),
        lax.psum(input_partial.astype(jnp.bfloat16), "narrow").astype(jnp.float32),
        lax.psum(moe_partial.astype(jnp.bfloat16), "narrow").astype(jnp.float32),
    )
    block_rows = residual + moe_sum
    block_out = lax.dynamic_slice_in_dim(block_rows, lane_index * head_cols, head_cols, 1).astype(
        jnp.bfloat16
    )
    logit_grad = gate_pull(pair_dots)[0].astype(jnp.bfloat16)
    ffn_grad = input_sum + jnp.einsum(
        "te,de->td", logit_grad, w_router, preferred_element_type=jnp.float32
    )
    router_grad = jnp.einsum("td,te->de", ffn_in, logit_grad, preferred_element_type=jnp.float32)
    _, ffn_norm_pull = jax.vjp(rms_scale, residual, ffn_gain)
    residual_norm_grad, ffn_gain_grad = ffn_norm_pull(ffn_grad)
    residual_grad = cot_float + residual_norm_grad
    out_cot = residual_grad.astype(jnp.bfloat16)
    attended_grad = (
        jnp.einsum("tc,cd->td", out_cot, out_full, preferred_element_type=jnp.float32)
        .astype(jnp.bfloat16)
        .reshape(length, heads_here, HD)
    )
    offset = 0
    scores = block_scores(offset)
    attn_probs = jnp.exp(scores - total_parts)
    prob_grad = jnp.einsum(
        "qhd,khd->hqk", attended_grad, value_bf, preferred_element_type=jnp.float32
    )
    centre = jnp.sum(attn_probs * prob_grad, axis=-1, keepdims=True)
    score_grad = (attn_probs * (prob_grad - centre)).astype(jnp.bfloat16)
    query_grad_parts = (
        jnp.einsum("hqk,khd->qhd", score_grad, key_bf, preferred_element_type=jnp.float32)
        * score_scale
    )
    key_grad = (
        jnp.einsum("hqk,qhd->khd", score_grad, query_bf, preferred_element_type=jnp.float32)
        * score_scale
    )
    value_grad = jnp.einsum(
        "hqk,qhd->khd",
        attn_probs.astype(jnp.bfloat16),
        attended_grad,
        preferred_element_type=jnp.float32,
    )
    query_normed_grad, key_normed_grad = rotate_pull((query_grad_parts, key_grad))
    dot_query, dot_key = lax.psum(
        (
            jnp.sum(query_gain * query_normed_grad * query_raw, axis=1),
            jnp.sum(key_gain * key_normed_grad * key_raw, axis=1),
        ),
        "narrow",
    )
    query_pre_grad = (
        query_scale * query_gain * query_normed_grad
        - query_raw * query_scale**3 * dot_query[:, None] / model_width
    )
    key_pre_grad = (
        key_scale * key_gain * key_normed_grad
        - key_raw * key_scale**3 * dot_key[:, None] / model_width
    )
    query_gain_grad = jnp.sum(query_normed_grad * query_raw * query_scale, axis=0)
    key_gain_grad = jnp.sum(key_normed_grad * key_raw * key_scale, axis=0)
    query_grad_bf = query_pre_grad.astype(jnp.bfloat16)
    key_grad_bf = key_pre_grad.astype(jnp.bfloat16)
    value_grad_bf = value_grad.reshape(length, head_cols).astype(jnp.bfloat16)
    normed_partial = jnp.einsum(
        "tc,dc->td", query_grad_bf, query_full, preferred_element_type=jnp.float32
    )
    normed_partial = normed_partial + jnp.einsum(
        "tc,dc->td", key_grad_bf, key_full, preferred_element_type=jnp.float32
    )
    normed_partial = normed_partial + jnp.einsum(
        "tc,dc->td", value_grad_bf, value_full, preferred_element_type=jnp.float32
    )
    normed_grad = lax.psum(normed_partial.astype(jnp.bfloat16), "narrow").astype(jnp.float32)
    _, attn_norm_pull = jax.vjp(rms_scale, rows_float, attn_gain)
    rows_norm_grad, attn_gain_grad = attn_norm_pull(normed_grad)
    grad_tokens = lax.dynamic_slice_in_dim(
        residual_grad + rows_norm_grad, lane_index * head_cols, head_cols, 1
    )
    small_terms = (
        router_grad,
        lax.dynamic_slice_in_dim(attn_gain_grad, lane_index * head_cols, head_cols, 0),
        lax.dynamic_slice_in_dim(ffn_gain_grad, lane_index * head_cols, head_cols, 0),
        query_gain_grad,
        key_gain_grad,
    )
    grad_router, grad_norm_attn, grad_norm_ffn, grad_norm_query, grad_norm_key = (
        lax.psum(small_terms[0].astype(jnp.bfloat16), "wide").astype(jnp.float32),
        lax.psum(small_terms[1].astype(jnp.bfloat16), "wide").astype(jnp.float32),
        lax.psum(small_terms[2].astype(jnp.bfloat16), "wide").astype(jnp.float32),
        lax.psum(small_terms[3].astype(jnp.bfloat16), "wide").astype(jnp.float32),
        lax.psum(small_terms[4].astype(jnp.bfloat16), "wide").astype(jnp.float32),
    )
    query_term = jnp.einsum("tc,tf->cf", normed, query_grad_bf, preferred_element_type=jnp.float32)
    key_term = jnp.einsum("tc,tf->cf", normed, key_grad_bf, preferred_element_type=jnp.float32)
    value_term = jnp.einsum("tc,tf->cf", normed, value_grad_bf, preferred_element_type=jnp.float32)
    out_term = jnp.einsum("tc,tf->cf", out_cot, attended, preferred_element_type=jnp.float32)
    gate_term = jnp.einsum(
        "ecd,ecf->def", expert_rows, gate_grad_bf, preferred_element_type=jnp.float32
    )
    up_term = jnp.einsum(
        "ecd,ecf->def", expert_rows, up_grad_bf, preferred_element_type=jnp.float32
    )
    down_term = jnp.einsum(
        "ecd,ecf->def", expert_cot, hidden_bf, preferred_element_type=jnp.float32
    )
    gate_term, up_term, down_term = (gate_term, up_term, down_term)
    grad_query, grad_key, grad_value, grad_out, grad_gate, grad_up, grad_down = (
        lax.psum_scatter(
            query_term.astype(jnp.bfloat16), "wide", scatter_dimension=0, tiled=True
        ).astype(jnp.float32),
        lax.psum_scatter(
            key_term.astype(jnp.bfloat16), "wide", scatter_dimension=0, tiled=True
        ).astype(jnp.float32),
        lax.psum_scatter(
            value_term.astype(jnp.bfloat16), "wide", scatter_dimension=0, tiled=True
        ).astype(jnp.float32),
        lax.psum_scatter(
            out_term.astype(jnp.bfloat16), "wide", scatter_dimension=0, tiled=True
        ).astype(jnp.float32),
        lax.psum_scatter(
            gate_term.astype(jnp.bfloat16), "wide", scatter_dimension=0, tiled=True
        ).astype(jnp.float32),
        lax.psum_scatter(
            up_term.astype(jnp.bfloat16), "wide", scatter_dimension=0, tiled=True
        ).astype(jnp.float32),
        lax.psum_scatter(
            down_term.astype(jnp.bfloat16), "wide", scatter_dimension=0, tiled=True
        ).astype(jnp.float32),
    )
    return (
        block_out,
        grad_tokens,
        grad_norm_attn,
        grad_query,
        grad_key,
        grad_value,
        grad_norm_query,
        grad_norm_key,
        grad_out,
        grad_norm_ffn,
        grad_router,
        grad_gate,
        grad_up,
        grad_down,
    )


def solution(mesh):
    placed = (
        P("wide", "narrow"),
        P("wide", "narrow"),
        P("wide", None),
        P("wide", None),
        P("narrow"),
        P("wide", "narrow"),
        P("wide", "narrow"),
        P("wide", "narrow"),
        P("narrow"),
        P("narrow"),
        P("wide", "narrow"),
        P("narrow"),
        P(),
        P("wide", None, "narrow"),
        P("wide", None, "narrow"),
        P("wide", None, "narrow"),
    )
    return jax.shard_map(
        per_device,
        mesh=mesh,
        in_specs=placed,
        out_specs=(
            P("wide", "narrow"),
            P("wide", "narrow"),
            P("narrow"),
            P("wide", "narrow"),
            P("wide", "narrow"),
            P("wide", "narrow"),
            P("narrow"),
            P("narrow"),
            P("wide", "narrow"),
            P("narrow"),
            P(),
            P("wide", None, "narrow"),
            P("wide", None, "narrow"),
            P("wide", None, "narrow"),
        ),
        check_vma=False,
    )
```

profile of v0, /device:TPU:0, one launch (start us, length us, event | category | flops | bytes accessed | tf_op | source)
XLA Modules:
  0.0 2680.0 jit_solution(7671028160317145200)
XLA Ops:
  37.0 49.3 %all-gather.16.cloned.1.call-done = bf16[2048,512]{1,0:T(8,128)(2,1)} async-done(((bf16[256,512]{1,0:T(8,128)(2,1)}), bf16[2048,512]{1,0:T(8,128)(2,1)}) %all-gather.16.cloned.1.call-update) | async-done | bytes 2097168 | tf_op jit(solution)/shard_map/all_gather | solution.py:90
  90.1 46.2 %all-gather.18.cloned.1.call-done = bf16[2048,512]{1,0:T(8,128)(2,1)} async-done(((bf16[256,512]{1,0:T(8,128)(2,1)}), bf16[2048,512]{1,0:T(8,128)(2,1)}) %all-gather.18.cloned.1.call-update) | async-done | bytes 2097168 | tf_op jit(solution)/shard_map/all_gather | solution.py:91
  152.6 33.5 %all-gather.14.cloned.1.call-done = bf16[2048,512]{1,0:T(8,128)(2,1)} async-done(((bf16[256,512]{1,0:T(8,128)(2,1)}), bf16[2048,512]{1,0:T(8,128)(2,1)}) %all-gather.14.cloned.1.call-update) | async-done | bytes 2097168 | tf_op jit(solution)/shard_map/all_gather | solution.py:92
  191.0 44.9 %all-gather.20.cloned.1.call-done = bf16[2048,512]{1,0:T(8,128)(2,1)} async-done(((bf16[256,512]{1,0:T(8,128)(2,1)}), bf16[2048,512]{1,0:T(8,128)(2,1)}) %all-gather.20.cloned.1.call-update) | async-done | bytes 2097168 | tf_op jit(solution)/shard_map/all_gather | solution.py:140
  287.1 34.3 %gather_fusion.2 = f32[4352,2048]{1,0:T(8,128)} fusion(f32[513,2048]{1,0:T(8,128)} %concatenate.34, s32[5120]{0:T(1024)S(1)} %pad_clamp_fusion), kind=kCustom, calls=%fused_computation.2 | custom fusion | bytes 71320576 | tf_op jit(solution)/shard_map/gather | solution.py:158
  322.0 24.9 all-reduce.15.cloned.1.call-done
  352.5 33.0 %gather_fusion.4 = f32[4096]{0:T(1024)S(1)} fusion(f32[512,16]{0,1:T(8,128)S(1)} %fusion.49, s32[4096]{0:T(1024)S(1)} %reshape.331), kind=kCustom, calls=%fused_computation.4 | custom fusion | bytes 65536 | tf_op jit(solution)/shard_map/jvp(jit(take_along_axis))/gather | solution.py:147
  386.2 22.8 gather_fusion
  429.2 147.9 %all-gather.22.cloned.1.call-done = bf16[2048,16,256]{2,0,1:T(8,128)(2,1)} async-done(((bf16[256,16,256]{2,0,1:T(8,128)(2,1)}), bf16[2048,16,256]{2,0,1:T(8,128)(2,1)}) %all-gather.22.cloned.1.call-update) | async-done | bytes 16777232 | tf_op jit(solution)/shard_map/all_gather | solution.py:160
  593.7 211.7 %all-gather.24.cloned.1.call-done = bf16[2048,16,256]{2,0,1:T(8,128)(2,1)} async-done(((bf16[256,16,256]{2,0,1:T(8,128)(2,1)}), bf16[2048,16,256]{2,0,1:T(8,128)(2,1)}) %all-gather.24.cloned.1.call-update) | async-done | bytes 16777232 | tf_op jit(solution)/shard_map/all_gather | solution.py:161
  821.9 211.5 %all-gather.26.cloned.1.call-done = bf16[2048,16,256]{2,0,1:T(8,128)(2,1)} async-done(((bf16[256,16,256]{2,0,1:T(8,128)(2,1)}), bf16[2048,16,256]{2,0,1:T(8,128)(2,1)}) %all-gather.26.cloned.1.call-update) | async-done | bytes 16777232 | tf_op jit(solution)/shard_map/all_gather | solution.py:169
  1033.4 34.2 %multiply_convert_fusion.3 = (bf16[16,272,256]{2,1,0:T(8,128)(2,1)}, bf16[16,272,256]{2,1,0:T(8,128)(2,1)S(1)}, bf16[16,272,256]{2,1,0:T(8,128)(2,1)}) fusion(f32[16,272,256]{2,1,0:T(8,128)} %fusion.67, f32[16,272,256]{2,1,0:T(8,128)} %fusion.68, bf16[2048,16,256]{2,0,1:T(8,128)(2,1)} %all-gather.26.cloned.1.call-done, f32[16,272,2048]{2,1,0:T(8,128)} %bitcast.142, ...), kind=kOutput, calls=%fused_computation.24 | convolution fusion | flops 4599054336 | bytes 68043776 | tf_op jit(solution)/shard_map/ecd,def->ecf/dot_general | solution.py:185
  1067.6 25.4 fusion.69
  1093.0 31.1 %convolution_add_fusion = f32[16,272,2048]{2,1,0:T(8,128)} fusion(f32[16,272,2048]{2,1,0:T(8,128)} %fusion.69, bf16[16,272,256]{2,1,0:T(8,128)(2,1)} %get-tuple-element.104, bf16[2048,16,256]{2,0,1:T(8,128)(2,1)} %all-gather.24.cloned.1.call-done), kind=kOutput, calls=%fused_computation.12 | convolution fusion | flops 4572315648 | bytes 90308608 | tf_op jit(solution)/shard_map/ecf,def->ecd/dot_general | solution.py:193
  1124.1 60.5 %scatter_custom_fusion.2 = f32[513,2048]{1,0:T(8,128)} fusion(s32[4352]{0:T(1024)} %copy-done.52, f32[4352,2048]{1,0:T(8,128)} %bitcast.149, f32[]{:T(128)} %constant.32.clone.1), kind=kCustom, calls=%fused_computation.56 | custom fusion | flops 8912896 | bytes 4203008 | tf_op jit(solution)/shard_map/scatter-add | solution.py:197
  1188.8 31.0 %multiply_reduce_fusion = (bf16[16,272]{1,0:T(8,128)(2,1)S(1)}, f32[16,272,2048]{2,1,0:T(8,128)}) fusion(f32[16,272,2048]{2,1,0:T(8,128)} %bitcast.143, bf16[16,272,256]{2,1,0:T(8,128)(2,1)S(1)} %copy-done.16, bf16[2048,16,256]{2,0,1:T(8,128)(2,1)} %all-gather.26.cloned.1.call-done), kind=kOutput, calls=%fused_computation.10 | convolution fusion | flops 4581224448 | bytes 90317312 | tf_op jit(solution)/shard_map/ecf,def->ecd/dot_general | solution.py:170
  1219.8 26.7 bitcast_multiply_fusion
  1246.7 25.6 gather_fusion.3
  1285.0 22.1 scatter_custom_fusion.3
  1307.2 60.9 %scatter_custom_fusion.1 = f32[513,2048]{1,0:T(8,128)} fusion(s32[4352]{0:T(1024)} %copy-done.52, f32[4352,2048]{1,0:T(8,128)} %bitcast_multiply_fusion, f32[]{:T(128)} %constant.32.clone.1), kind=kCustom, calls=%fused_computation.58 | custom fusion | flops 8912896 | bytes 4203008 | tf_op jit(solution)/shard_map/scatter-add | solution.py:176
  1420.0 20.4 convert_bitcast_fusion
  1440.5 18.9 convert_bitcast_fusion.2
  1459.7 19.0 convert_bitcast_fusion.1
  1482.9 44.9 %all-reduce.21.cloned.1.call-done = (bf16[512,2048]{1,0:T(8,128)(2,1)}, bf16[512,2048]{1,0:T(8,128)(2,1)}) async-done(((bf16[512,2048]{1,0:T(8,128)(2,1)}, bf16[512,2048]{1,0:T(8,128)(2,1)}), (bf16[512,2048]{1,0:T(8,128)(2,1)}, bf16[512,2048]{1,0:T(8,128)(2,1)})) %all-reduce.21.cloned.1.call-update) | async-done | bytes 4194320 | tf_op jit(solution)/shard_map/psum | solution.py:202
  1533.1 21.6 all-reduce.8
  1562.4 36.9 %reduce-scatter.12.cloned.1.call-done = bf16[256,512]{1,0:T(8,128)(2,1)} async-done(((bf16[2048,512]{1,0:T(8,128)(2,1)}), bf16[256,512]{1,0:T(8,128)(2,1)}) %reduce-scatter.12.cloned.1.call-update) | async-done | bytes 262160 | tf_op jit(solution)/shard_map/reduce_scatter | solution.py:315
  1601.1 68.6 %reduce-scatter.10.cloned.1.call-done = bf16[256,512]{1,0:T(8,128)(2,1)} async-done(((bf16[2048,512]{1,0:T(8,128)(2,1)}), bf16[256,512]{1,0:T(8,128)(2,1)}) %reduce-scatter.10.cloned.1.call-update) | async-done | bytes 262160 | tf_op jit(solution)/shard_map/reduce_scatter | solution.py:312
  1671.5 68.8 %reduce-scatter.8.cloned.1.call-done = bf16[256,512]{1,0:T(8,128)(2,1)} async-done(((bf16[2048,512]{1,0:T(8,128)(2,1)}), bf16[256,512]{1,0:T(8,128)(2,1)}) %reduce-scatter.8.cloned.1.call-update) | async-done | bytes 262160 | tf_op jit(solution)/shard_map/reduce_scatter | solution.py:309
  1742.1 68.6 %reduce-scatter.14.cloned.1.call-done = bf16[256,512]{1,0:T(8,128)(2,1)} async-done(((bf16[2048,512]{1,0:T(8,128)(2,1)}), bf16[256,512]{1,0:T(8,128)(2,1)}) %reduce-scatter.14.cloned.1.call-update) | async-done | bytes 262160 | tf_op jit(solution)/shard_map/reduce_scatter | solution.py:318
  1812.5 284.1 %reduce-scatter.20.cloned.1.call-done = bf16[256,16,256]{0,2,1:T(8,128)(2,1)} async-done(((bf16[2048,16,256]{0,2,1:T(8,128)(2,1)}), bf16[256,16,256]{0,2,1:T(8,128)(2,1)}) %reduce-scatter.20.cloned.1.call-update) | async-done | bytes 2097168 | tf_op jit(solution)/shard_map/reduce_scatter | solution.py:327
  2101.3 280.9 %reduce-scatter.16.cloned.1.call-done = bf16[256,16,256]{0,2,1:T(8,128)(2,1)} async-done(((bf16[2048,16,256]{0,2,1:T(8,128)(2,1)}), bf16[256,16,256]{0,2,1:T(8,128)(2,1)}) %reduce-scatter.16.cloned.1.call-update) | async-done | bytes 2097168 | tf_op jit(solution)/shard_map/reduce_scatter | solution.py:321
  2387.0 281.0 %reduce-scatter.18.cloned.1.call-done = bf16[256,16,256]{0,2,1:T(8,128)(2,1)} async-done(((bf16[2048,16,256]{0,2,1:T(8,128)(2,1)}), bf16[256,16,256]{0,2,1:T(8,128)(2,1)}) %reduce-scatter.18.cloned.1.call-update) | async-done | bytes 2097168 | tf_op jit(solution)/shard_map/reduce_scatter | solution.py:324
  (344 shorter events, 272.8 us)
Async XLA Ops:
  7.2 343.0 %copy-start = (bf16[2048,16]{0,1:T(8,128)(2,1)S(1)}, bf16[2048,16]{0,1:T(8,128)(2,1)}, u32[]{:S(2)}) copy-start(bf16[2048,16]{0,1:T(8,128)(2,1)} %param.28) | copy-start | bytes 196612
  7.2 27.7 %all-gather.12.cloned.1.call-start = ((), (), s32[]{:S(2)}) async-start(), calls=%async_computation.7 | async-start | bytes 2621440 | tf_op jit(solution)/shard_map/all_gather | solution.py:75
  7.9 78.4 %all-gather.16.cloned.1.call-start = ((), (), s32[]{:S(2)}) async-start(), calls=%async_computation.9 | async-start | bytes 2359296 | tf_op jit(solution)/shard_map/all_gather | solution.py:90
  8.7 127.6 %all-gather.18.cloned.1.call-start = ((), (), s32[]{:S(2)}) async-start(), calls=%async_computation.10 | async-start | bytes 2359296 | tf_op jit(solution)/shard_map/all_gather | solution.py:91
  9.4 176.7 %all-gather.14.cloned.1.call-start = ((), (), s32[]{:S(2)}) async-start(), calls=%async_computation.8 | async-start | bytes 2359296 | tf_op jit(solution)/shard_map/all_gather | solution.py:92
  10.0 225.9 %all-gather.20.cloned.1.call-start = ((), (), s32[]{:S(2)}) async-start(), calls=%async_computation.11 | async-start | bytes 2359296 | tf_op jit(solution)/shard_map/all_gather | solution.py:140
  10.6 272.3 %all-gather.28.cloned.1.call-start = ((), (), s32[]{:S(2)}) async-start(), calls=%async_computation.16 | async-start | bytes 2621440 | tf_op jit(solution)/shard_map/all_gather | solution.py:76
  11.2 335.8 %all-reduce.15.cloned.1.call-start = ((), (), s32[]{:S(2)}) async-start(), calls=%async_computation.12 | async-start | bytes 8388608 | tf_op jit(solution)/shard_map/psum | solution.py:142
  18.0 168.1 %copy-start.65 = (f32[4,1,512]{2,1,0:T(1,128)}, f32[4,1,512]{2,1,0:T(1,128)S(1)}, u32[]{:S(2)}) copy-start(f32[4,1,512]{2,1,0:T(1,128)S(1)} %convert_element_type.261) | copy-start | bytes 24580
  18.7 127.8 %copy-start.57 = (f32[512]{0:T(512)}, f32[512]{0:T(512)S(1)}, u32[]{:S(2)}) copy-start(f32[512]{0:T(512)S(1)} %convert_element_type.200) | copy-start | bytes 6148
  19.4 127.4 %copy-start.59 = (f32[512]{0:T(512)}, f32[512]{0:T(512)S(1)}, u32[]{:S(2)}) copy-start(f32[512]{0:T(512)S(1)} %convert_element_type.202) | copy-start | bytes 6148
  37.0 149.1 %copy-start.71 = (f32[512]{0:T(512)}, f32[512]{0:T(512)S(1)}, u32[]{:S(2)}) copy-start(f32[512]{0:T(512)S(1)} %fusion.58) | copy-start | bytes 6148
  240.8 336.3 %all-gather.22.cloned.1.call-start = ((), (), s32[]{:S(2)}) async-start(), calls=%async_computation.13 | async-start | bytes 18874368 | tf_op jit(solution)/shard_map/all_gather | solution.py:160
  244.7 560.6 %all-gather.24.cloned.1.call-start = ((), (), s32[]{:S(2)}) async-start(), calls=%async_computation.14 | async-start | bytes 18874368 | tf_op jit(solution)/shard_map/all_gather | solution.py:161
  248.6 784.8 %all-gather.26.cloned.1.call-start = ((), (), s32[]{:S(2)}) async-start(), calls=%async_computation.15 | async-start | bytes 18874368 | tf_op jit(solution)/shard_map/all_gather | solution.py:169
  252.4 1121.1 %all-reduce.17.cloned.1.call-start = ((), (), s32[]{:S(2)}) async-start(), calls=%async_computation.17 | async-start | bytes 4194304 | tf_op jit(solution)/shard_map/psum | solution.py:201
  258.1 91.7 %copy-start.47 = (f32[4,1,512]{2,1,0:T(1,128)}, f32[4,1,512]{2,1,0:T(1,128)S(1)}, u32[]{:S(2)}) copy-start(f32[4,1,512]{2,1,0:T(1,128)S(1)} %convert_element_type.262) | copy-start | bytes 24580
  352.5 76.2 %copy-start.55 = (f32[512]{0:T(512)}, f32[512]{0:T(512)S(1)}, u32[]{:S(2)}) copy-start(f32[512]{0:T(512)S(1)} %fusion.50) | copy-start | bytes 6148
  409.7 623.8 %copy-start.49 = (f32[16,272]{1,0:T(8,128)}, f32[16,272]{1,0:T(8,128)S(1)}, u32[]{:S(2)}) copy-start(f32[16,272]{1,0:T(8,128)S(1)} %mul.486) | copy-start | bytes 52228
  1188.7 292.6 %all-reduce.19.cloned.1.call-start = ((), (), s32[]{:S(2)}) async-start(), calls=%async_computation.22 | async-start | bytes 131072 | tf_op jit(solution)/shard_map/psum | solution.py:288
  1246.7 60.5 %copy-start.39 = (f32[512,16]{0,1:T(8,128)S(1)}, f32[512,16]{0,1:T(8,128)}, u32[]{:S(2)}) copy-start(f32[512,16]{0,1:T(8,128)} %copy-done.38) | copy-start | bytes 98308
  1246.7 60.5 %copy-start.54 = (f32[512]{0:T(512)S(1)}, f32[512]{0:T(512)}, u32[]{:S(2)}) copy-start(f32[512]{0:T(512)} %copy-done.53) | copy-start | bytes 6148
  1307.2 64.8 %copy-start.56 = (f32[512]{0:T(512)S(1)}, f32[512]{0:T(512)}, u32[]{:S(2)}) copy-start(f32[512]{0:T(512)} %copy-done.55) | copy-start | bytes 6148
  1307.2 64.8 %copy-start.8 = (bf16[512,2048]{1,0:T(8,128)(2,1)S(1)}, bf16[512,2048]{1,0:T(8,128)(2,1)}, u32[]{:S(2)}) copy-start(bf16[512,2048]{1,0:T(8,128)(2,1)} %copy-done.7) | copy-start | bytes 6291460
  1373.1 154.7 %all-reduce.21.cloned.1.call-start = ((), (), s32[]{:S(2)}) async-start(), calls=%async_computation.26 | async-start | bytes 8388608 | tf_op jit(solution)/shard_map/psum | solution.py:202
  1404.6 194.7 %reduce-scatter.12.cloned.1.call-start = ((), (), s32[]{:S(2)}) async-start(), calls=%async_computation.20 | async-start | bytes 2359296 | tf_op jit(solution)/shard_map/reduce_scatter | solution.py:315
  1409.0 260.7 %reduce-scatter.10.cloned.1.call-start = ((), (), s32[]{:S(2)}) async-start(), calls=%async_computation.19 | async-start | bytes 2359296 | tf_op jit(solution)/shard_map/reduce_scatter | solution.py:312
  1411.9 328.3 %reduce-scatter.8.cloned.1.call-start = ((), (), s32[]{:S(2)}) async-start(), calls=%async_computation.18 | async-start | bytes 2359296 | tf_op jit(solution)/shard_map/reduce_scatter | solution.py:309
  1414.9 395.8 %reduce-scatter.14.cloned.1.call-start = ((), (), s32[]{:S(2)}) async-start(), calls=%async_computation.21 | async-start | bytes 2359296 | tf_op jit(solution)/shard_map/reduce_scatter | solution.py:318
  1419.7 676.8 %reduce-scatter.20.cloned.1.call-start = ((), (), s32[]{:S(2)}) async-start(), calls=%async_computation.25 | async-start | bytes 18874368 | tf_op jit(solution)/shard_map/reduce_scatter | solution.py:327
  1440.5 941.7 %reduce-scatter.16.cloned.1.call-start = ((), (), s32[]{:S(2)}) async-start(), calls=%async_computation.23 | async-start | bytes 18874368 | tf_op jit(solution)/shard_map/reduce_scatter | solution.py:321
  1459.4 1208.6 %reduce-scatter.18.cloned.1.call-start = ((), (), s32[]{:S(2)}) async-start(), calls=%async_computation.24 | async-start | bytes 18874368 | tf_op jit(solution)/shard_map/reduce_scatter | solution.py:324
  (69 other events, 658.3 us)
Sparse Core Ops, SparseCore 0:
  9.6 25.2 all-gather.11
  37.0 49.2 all-gather.15
  88.5 47.7 all-gather.17
  138.3 47.7 all-gather.13
  188.1 47.7 all-gather.19
  237.3 21.0 all-gather.27
  261.4 85.5 all-reduce.14
  349.3 227.7 all-gather.21
  579.5 225.7 all-gather.23
  807.6 225.7 all-gather.25
  1188.8 49.5 all-reduce.16
  1373.2 66.4 all-reduce.18
  1442.1 85.6 all-reduce.20
  1531.5 67.7 reduce-scatter.11
  1603.1 66.5 reduce-scatter.9
  1673.5 66.7 reduce-scatter.7
  1744.1 66.5 reduce-scatter.13
  1814.8 281.7 reduce-scatter.19
  2100.3 281.8 reduce-scatter.15
  2386.3 281.6 reduce-scatter.17
where the time goes:
time: 2690 us; the launch traced here: 2680 us
  waiting for transfers between devices  1920 us (71%)
  matrix products  261 us (10%)
  other arithmetic  221 us (8%)
  local copies, waits for them, and re-layouts  205 us (8%)
  blocking collectives  56.7 us (2%)
    reduce_scatter x1, waiting for transfers between devices, per_device(): lax.psum_scatter(down_term.astype(jnp.bfloat16), 'wide', scatter_dimensio...  284 us
    reduce_scatter x1, waiting for transfers between devices, per_device(): lax.psum_scatter(up_term.astype(jnp.bfloat16), 'wide', scatter_dimension=...  281 us
    reduce_scatter x1, waiting for transfers between devices, per_device(): lax.psum_scatter(gate_term.astype(jnp.bfloat16), 'wide', scatter_dimensio...  281 us
    all_gather x1, waiting for transfers between devices, per_device(): lax.all_gather(w_up, 'wide', axis=0, tiled=True)  212 us
    all_gather x1, waiting for transfers between devices, per_device(): down_full = lax.all_gather(w_down, 'wide', axis=0, tiled=True)  211 us
    all_gather x1, waiting for transfers between devices, per_device(): lax.all_gather(w_gate, 'wide', axis=0, tiled=True)  148 us
    reduce_scatter x1, waiting for transfers between devices, per_device(): lax.psum_scatter(query_term.astype(jnp.bfloat16), 'wide', scatter_dimensi...  68.8 us
    reduce_scatter x1, waiting for transfers between devices, per_device(): lax.psum_scatter(key_term.astype(jnp.bfloat16), 'wide', scatter_dimension...  68.6 us
  transfers between devices with their start and end apart: 20, of which 17 were waited for; matrix products, arithmetic and copies ran while one was open for 19% of the time, Pallas kernels for 0%

commit v1 on v0

v1 whole, which is shorter than its diff:
```python
import jax
import jax.numpy as jnp
from jax import lax
from jax.sharding import Mesh
from jax.sharding import PartitionSpec as P

HD = 128
EPS = 1e-05
WIDE = ("t", "g", "p")
NARROW = ("y", "c")
GROUP = ("g", "p", "c")
ALL = ("t", "g", "p", "y", "c")
BF = jnp.bfloat16
F32 = jnp.float32


def rms_scale(values, scales):
    return values * lax.rsqrt(jnp.mean(values * values, axis=-1, keepdims=True) + EPS) * scales


def rope_tables(length, head_dim):
    exponent = jnp.arange(0, head_dim, 2, dtype=F32) / head_dim
    angles = jnp.arange(length, dtype=F32)[:, None] * (10000.0 ** (-exponent))[None, :]
    angles = jnp.concatenate([angles, angles], axis=-1)
    return (jnp.cos(angles)[:, None, :], jnp.sin(angles)[:, None, :])


def rotate_half(values, cosines, sine_table):
    middle = values.shape[-1] // 2
    turned = jnp.concatenate([-values[..., middle:], values[..., :middle]], axis=-1)
    return values * cosines + turned * sine_table


def dot(a, b, contract):
    return lax.dot_general(a, b, (contract, ((), ())), preferred_element_type=F32)


def swap(values, axis, step=1):
    count = lax.axis_size(axis)
    return lax.ppermute(values, axis, [(i, i ^ step) for i in range(count)])


def gather_four(block, axis):
    count = lax.axis_size("y") * lax.axis_size("c")
    size = block.shape[axis]
    here = lax.axis_index("y") * lax.axis_size("c") + lax.axis_index("c")
    other = swap(block, "y")
    near = swap(block, "c")
    far = swap(other, "c")
    shape = list(block.shape)
    shape[axis] = size * count
    whole = jnp.zeros(shape, block.dtype)
    for piece, place in ((block, 0), (near, 1), (other, 2), (far, 3)):
        whole = lax.dynamic_update_slice_in_dim(whole, piece, (here ^ place) * size, axis)
    return whole


def sum_four(partial):
    length, width = partial.shape
    rows = length // 4
    y, c = lax.axis_index("y"), lax.axis_index("c")
    parts = partial.reshape(2, 2, rows, width)
    mine = lax.dynamic_index_in_dim(parts, c, 1, False)
    theirs = lax.dynamic_index_in_dim(parts, 1 - c, 1, False)
    mine = mine + swap(theirs.astype(BF), "c").astype(F32)
    keep = lax.dynamic_index_in_dim(mine, y, 0, False)
    send = lax.dynamic_index_in_dim(mine, 1 - y, 0, False)
    return keep + swap(send.astype(BF), "y").astype(F32)


def spread(block):
    count = lax.axis_size("g")
    far = [block] + [swap(block, "g", step) for step in range(1, count)]
    near = [swap(piece, "p") for piece in far]
    first = jnp.concatenate(far + near, axis=0)
    return jnp.concatenate([first, swap(first, "c")], axis=0)


def collect(partial):
    count = lax.axis_size("g")
    rows = partial.shape[0] // (4 * count)
    parts = partial.reshape(2, 2, count, rows, partial.shape[1])
    halves = parts[0] + swap(parts[1].astype(BF), "c").astype(F32)
    total = None
    order = list(range(1, count)) + [0]
    quarters = {s: halves[0, s] + swap(halves[1, s].astype(BF), "p").astype(F32) for s in order}
    total = quarters[0]
    for s in order[:-1]:
        total = total + swap(quarters[s].astype(BF), "g", s).astype(F32)
    return total


def by_distance(values):
    count = lax.axis_size("g")
    tail = values.shape[1:]
    v = values.reshape((count // 2, 2, 2, 2) + tail)
    g, p, c = lax.axis_index("g"), lax.axis_index("p"), lax.axis_index("c")
    for axis, bit in enumerate((g // 2, g % 2, p, c)):
        v = jnp.where(bit == 1, jnp.flip(v, axis), v)
    return v


def to_experts(columns):
    sent = lax.all_to_all(columns.T, GROUP, 0, 0, tiled=True)
    v = by_distance(sent)
    v = jnp.transpose(v, (3, 2, 0, 1, 4))
    return v.reshape(-1)


def to_owners(values, rows):
    count = lax.axis_size("g")
    v = values.reshape(2, 2, count // 2, 2, rows)
    v = jnp.transpose(v, (2, 3, 1, 0, 4)).reshape(4 * count, rows)
    v = by_distance(v).reshape(4 * count, rows)
    return lax.all_to_all(v, GROUP, 0, 0, tiled=True).T


def own_expert(weight):
    depth, experts, units = weight.shape
    got = lax.all_to_all(jnp.transpose(weight, (1, 0, 2)), GROUP, 0, 0, tiled=True)
    both = jnp.stack([got, swap(got, "y")])
    both = both.reshape(2, experts // 2, 2, depth, units)
    whole = jnp.transpose(both, (1, 3, 0, 2, 4)).reshape(experts // 2 * depth, 4 * units)
    if lax.axis_size("t") > 1:
        whole = lax.all_gather(whole, "t", axis=0, tiled=True)
    return whole


def to_slices(grad, experts):
    model, hidden = grad.shape
    units = hidden // 4
    parts = grad.reshape(model, 2, 2 * units)
    mine = parts[:, 0] + swap(parts[:, 1].astype(BF), "y").astype(F32)
    if lax.axis_size("t") > 1:
        mine = lax.psum_scatter(mine.astype(BF), "t", scatter_dimension=0, tiled=True)
    depth = mine.shape[0] * 2 // experts
    mine = mine.astype(BF).reshape(experts // 2, depth, 2, units)
    sent = jnp.transpose(mine, (0, 2, 1, 3)).reshape(experts, depth, units)
    got = lax.all_to_all(sent, GROUP, 0, 0, tiled=True)
    return jnp.transpose(got, (1, 0, 2)).astype(F32)


def per_device(
    tokens,
    cotangent,
    block_ids,
    routes,
    norm_attn,
    w_query,
    w_key,
    w_value,
    norm_query,
    norm_key,
    w_out,
    norm_ffn,
    w_router,
    w_gate,
    w_up,
    w_down,
):
    experts = w_router.shape[1]
    lane_index = lax.axis_index("y") * lax.axis_size("c") + lax.axis_index("c")
    lanes = lax.axis_size("y") * lax.axis_size("c")
    length, head_cols = tokens.shape
    model_width = head_cols * lanes
    rows = length // lanes
    heads_here = head_cols // HD
    score_scale = HD ** (-0.5)

    rows_full = gather_four(tokens, 1)
    gains = lax.all_gather(jnp.stack([norm_attn, norm_ffn]), NARROW, axis=1, tiled=True)
    attn_gain = gains[0].astype(F32)
    ffn_gain = gains[1].astype(F32)
    qkv_full = lax.all_gather(
        jnp.concatenate([w_query, w_key, w_value], axis=1), WIDE, axis=0, tiled=True
    )
    query_full = qkv_full[:, :head_cols]
    key_full = qkv_full[:, head_cols : 2 * head_cols]
    value_full = qkv_full[:, 2 * head_cols :]
    out_full = lax.all_gather(w_out, WIDE, axis=0, tiled=True)

    cot_rows = lax.all_to_all(cotangent.reshape(lanes, rows, head_cols), NARROW, 0, 0, tiled=True)
    cot_rows = jnp.transpose(cot_rows, (1, 0, 2)).reshape(rows, model_width)
    cot_all = spread(cot_rows)

    gate_own = own_expert(w_gate)
    up_own = own_expert(w_up)
    down_own = own_expert(w_down)

    rows_float = rows_full.astype(F32)
    normed = rms_scale(rows_float, attn_gain).astype(BF)
    query_raw = jnp.dot(normed, query_full, preferred_element_type=F32)
    key_raw = jnp.dot(normed, key_full, preferred_element_type=F32)
    value_raw = jnp.dot(normed, value_full, preferred_element_type=F32)
    square_query, square_key = lax.psum(
        (jnp.sum(query_raw * query_raw, axis=1), jnp.sum(key_raw * key_raw, axis=1)), NARROW
    )
    query_scale = lax.rsqrt(square_query / model_width + EPS)[:, None]
    key_scale = lax.rsqrt(square_key / model_width + EPS)[:, None]
    query_gain = norm_query.astype(F32)
    key_gain = norm_key.astype(F32)
    cosines, sine_table = rope_tables(length, HD)
    query_normed = query_raw * query_scale * query_gain
    key_normed = key_raw * key_scale * key_gain

    def rotate_both(query_in, key_in):
        return (
            rotate_half(query_in.reshape(length, heads_here, HD), cosines, sine_table),
            rotate_half(key_in.reshape(length, heads_here, HD), cosines, sine_table),
        )

    (query_rot, key_rot), rotate_pull = jax.vjp(rotate_both, query_normed, key_normed)
    query_bf = query_rot.astype(BF)
    key_bf = key_rot.astype(BF)
    value_bf = value_raw.astype(BF).reshape(length, heads_here, HD)
    seq_blocks = block_ids[0]

    def block_scores():
        scores = (
            jnp.einsum("qhd,khd->hqk", query_bf, key_bf, preferred_element_type=F32) * score_scale
        )
        allowed = seq_blocks[None, :] <= seq_blocks[:, None]
        return jnp.where(allowed[None], scores, -1e30)

    scores = block_scores()
    highest = jnp.max(scores, axis=-1, keepdims=True)
    shifted = jnp.exp(scores - highest)
    totals = jnp.sum(shifted, axis=-1, keepdims=True)
    attn_probs = (shifted / totals).astype(BF)
    attended = (
        jnp.einsum("hqk,khd->qhd", attn_probs, value_bf, preferred_element_type=F32)
        .astype(BF)
        .reshape(length, head_cols)
    )
    log_totals = highest + jnp.log(totals)
    out_partial = dot(attended, out_full, ((1,), (1,)))

    first_row = lane_index * rows
    x_rows = lax.dynamic_slice_in_dim(rows_full, first_row, rows, 0).astype(F32)
    residual = x_rows + sum_four(out_partial)
    ffn_in = rms_scale(residual, ffn_gain).astype(BF)
    x_all = spread(ffn_in)
    logits = jnp.dot(ffn_in, w_router, preferred_element_type=F32)
    gate_probs = jax.nn.softmax(logits, axis=-1)
    routes_rows = lax.dynamic_slice_in_dim(routes, first_row, rows, 0)
    chosen = jnp.any(
        routes_rows[:, :, None] == jnp.arange(experts, dtype=jnp.int32)[None, None, :], axis=1
    )
    own_gate = to_experts(jnp.where(chosen, gate_probs, 0.0))[:, None]

    gate_pre = jnp.dot(x_all, gate_own, preferred_element_type=F32)
    up_pre = jnp.dot(x_all, up_own, preferred_element_type=F32)
    sig = jax.nn.sigmoid(gate_pre)
    hidden = gate_pre * sig * up_pre
    hidden_gated = (own_gate * hidden).astype(BF)
    down_grad = jnp.dot(cot_all, down_own, preferred_element_type=F32)
    own_dots = jnp.sum(hidden * down_grad, axis=1)
    hidden_grad = own_gate * down_grad
    gate_grad = (hidden_grad * up_pre * (sig * (1.0 + gate_pre * (1.0 - sig)))).astype(BF)
    up_grad = (hidden_grad * gate_pre * sig).astype(BF)
    input_partial = dot(gate_grad, gate_own, ((1,), (1,))) + dot(up_grad, up_own, ((1,), (1,)))
    input_sum = collect(input_partial)
    moe_partial = dot(hidden_gated, down_own, ((1,), (1,)))
    moe_sum = collect(moe_partial)
    pair_dots = jnp.where(chosen, to_owners(own_dots, rows), 0.0)

    grad_down = to_slices(dot(cot_all, hidden_gated, ((0,), (0,))), experts)
    grad_gate = to_slices(dot(x_all, gate_grad, ((0,), (0,))), experts)
    grad_up = to_slices(dot(x_all, up_grad, ((0,), (0,))), experts)

    block_rows = (residual + moe_sum).astype(BF)

    def to_features(values):
        parts = jnp.transpose(values.reshape(rows, lanes, head_cols), (1, 0, 2))
        return lax.all_to_all(parts, NARROW, 0, 0, tiled=True).reshape(length, head_cols)

    block_out = to_features(block_rows)

    logit_grad = (
        gate_probs * (pair_dots - jnp.sum(gate_probs * pair_dots, axis=1, keepdims=True))
    ).astype(BF)
    ffn_grad = input_sum + dot(logit_grad, w_router, ((1,), (1,)))
    router_grad = dot(logit_grad, ffn_in, ((0,), (0,)))
    _, ffn_norm_pull = jax.vjp(rms_scale, residual, ffn_gain)
    residual_norm_grad, ffn_gain_grad = ffn_norm_pull(ffn_grad)
    residual_grad = cot_rows.astype(F32) + residual_norm_grad
    out_cot = gather_four(residual_grad.astype(BF), 0)

    attended_grad = (
        jnp.dot(out_cot, out_full, preferred_element_type=F32)
        .astype(BF)
        .reshape(length, heads_here, HD)
    )
    out_term = dot(out_cot, attended, ((0,), (0,)))
    grad_out = lax.psum_scatter(out_term.astype(BF), WIDE, scatter_dimension=0, tiled=True)
    attn_probs = jnp.exp(block_scores() - log_totals)
    prob_grad = jnp.einsum("qhd,khd->hqk", attended_grad, value_bf, preferred_element_type=F32)
    centre = jnp.sum(attn_probs * prob_grad, axis=-1, keepdims=True)
    score_grad = (attn_probs * (prob_grad - centre)).astype(BF)
    query_grad = (
        jnp.einsum("hqk,khd->qhd", score_grad, key_bf, preferred_element_type=F32) * score_scale
    )
    key_grad = (
        jnp.einsum("hqk,qhd->khd", score_grad, query_bf, preferred_element_type=F32) * score_scale
    )
    value_grad = jnp.einsum(
        "hqk,qhd->khd", attn_probs.astype(BF), attended_grad, preferred_element_type=F32
    )
    query_normed_grad, key_normed_grad = rotate_pull((query_grad, key_grad))
    dot_query, dot_key = lax.psum(
        (
            jnp.sum(query_gain * query_normed_grad * query_raw, axis=1),
            jnp.sum(key_gain * key_normed_grad * key_raw, axis=1),
        ),
        NARROW,
    )
    query_pre_grad = (
        query_scale * query_gain * query_normed_grad
        - query_raw * query_scale**3 * dot_query[:, None] / model_width
    )
    key_pre_grad = (
        key_scale * key_gain * key_normed_grad
        - key_raw * key_scale**3 * dot_key[:, None] / model_width
    )
    query_gain_grad = jnp.sum(query_normed_grad * query_raw * query_scale, axis=0)
    key_gain_grad = jnp.sum(key_normed_grad * key_raw * key_scale, axis=0)
    qkv_grad = jnp.concatenate(
        [
            query_pre_grad.astype(BF),
            key_pre_grad.astype(BF),
            value_grad.reshape(length, head_cols).astype(BF),
        ],
        axis=1,
    )
    normed_grad = sum_four(dot(qkv_grad, qkv_full, ((1,), (1,))))
    qkv_term = dot(normed, qkv_grad, ((0,), (0,)))
    grad_qkv = lax.psum_scatter(qkv_term.astype(BF), WIDE, scatter_dimension=0, tiled=True)
    grad_query = grad_qkv[:, :head_cols]
    grad_key = grad_qkv[:, head_cols : 2 * head_cols]
    grad_value = grad_qkv[:, 2 * head_cols :]
    _, attn_norm_pull = jax.vjp(rms_scale, x_rows, attn_gain)
    rows_norm_grad, attn_gain_grad = attn_norm_pull(normed_grad)
    grad_tokens = to_features(residual_grad + rows_norm_grad)

    place = (jnp.arange(lanes) == lane_index).astype(F32)[:, None]
    small = jnp.concatenate(
        [
            router_grad,
            attn_gain_grad[None],
            ffn_gain_grad[None],
            (place * query_gain_grad[None]).reshape(1, model_width),
            (place * key_gain_grad[None]).reshape(1, model_width),
        ],
        axis=0,
    )
    small = lax.psum(small, ALL)
    grad_router = small[:experts].T
    four = lax.dynamic_slice_in_dim(small[experts:], lane_index * head_cols, head_cols, 1)
    return (
        block_out,
        grad_tokens,
        four[0],
        grad_query.astype(F32),
        grad_key.astype(F32),
        grad_value.astype(F32),
        four[2],
        four[3],
        grad_out.astype(F32),
        four[1],
        grad_router,
        grad_gate,
        grad_up,
        grad_down,
    )


def solution(mesh):
    wide, narrow = mesh.shape["wide"], mesh.shape["narrow"]
    near = 2
    middle = min(wide // near, 4)
    inner = Mesh(mesh.devices.reshape(wide // (near * middle), middle, near, narrow // 2, 2), ALL)
    both = P(WIDE, NARROW)
    cube = P(WIDE, None, NARROW)
    lane = P(NARROW)
    row = P(WIDE, None)
    return jax.shard_map(
        per_device,
        mesh=inner,
        in_specs=(
            both, both, row, row, lane, both, both, both, lane, lane, both, lane, P(),
            cube, cube, cube,
        ),
        out_specs=(
            both, both, lane, both, both, both, lane, lane, both, lane, P(), cube, cube, cube,
        ),
        check_vma=False,
    )
```

time: 2690 us -> 1210 us (0.45)
  waiting for transfers between devices: 1920 us -> 598 us
  other arithmetic: 221 us -> 84.8 us
  starting transfers between devices: 1.94 us -> 124 us
  matrix products: 261 us -> 180 us
  local copies, waits for them, and re-layouts: 205 us -> 168 us
  blocking collectives: 56.7 us -> 29.1 us
    reduce_scatter x7 -> x2, waiting for transfers between devices: 1090 us -> 15.1 us  [the longest x1 15.1 us: per_device(): lax.psum_scatter(qkv_term.astype(BF), WIDE, scatter_dimension=0, tiled=True)]
    all_gather x9 -> x2, waiting for transfers between devices: 757 us -> 163 us  [the longest x1 119 us: per_device(): lax.all_gather(jnp.concatenate([w_query, w_key, w_value], axis=1), WIDE,...]
    ppermute x0 -> x48, waiting for transfers between devices: none -> 415 us  [swap(): return lax.ppermute(values, axis, [(i, i ^ step) for i in range(count)])]
    gather x10 -> x0, local copies, waits for them, and re-layouts: 134 us -> none  [the longest x1 34.3 us: per_device(): slot_cot = padded_cot[slot_tokens]]
    scatter-add x2 -> x0, other arithmetic: 121 us -> none  [the longest x1 60.9 us: per_device(): moe_partial = jnp.zeros((length + 1, model_width), jnp.float32).at[slot_t...]
    dot_general x29 -> x25, matrix products: 260 us -> 179 us  [the longest x12 112 us: dot(): lax.dot_general(a, b, (contract, ((), ())), preferred_element_type=F32)]
    all_to_all x0 -> x11, starting transfers between devices: none -> 71.2 us  [the longest x3 27 us: to_slices(): got = lax.all_to_all(sent, GROUP, 0, 0, tiled=True)]
    psum x4 -> x1, waiting for transfers between devices: 69.8 us -> 0.01 us  [per_device(): small = lax.psum(small, ALL)]
  transfers between devices with their start and end apart: 20 -> 64, of which waited for: 17 -> 34; matrix products, arithmetic and copies ran while one was open for 19% -> 25% of each run, Pallas kernels for 0% -> 0%
where the time goes in v1:
time: 1210 us; the launch traced here: 1200 us
  waiting for transfers between devices  598 us (49%)
  matrix products  180 us (15%)
  local copies, waits for them, and re-layouts  168 us (14%)
  starting transfers between devices  124 us (10%)
  other arithmetic  84.8 us (7%)
  blocking collectives  29.1 us (2%)
  between operations  15.5 us (1%)
    ppermute x48, waiting for transfers between devices, swap(): return lax.ppermute(values, axis, [(i, i ^ step) for i in range(count)])  415 us
    all_gather x1, waiting for transfers between devices, per_device(): lax.all_gather(jnp.concatenate([w_query, w_key, w_value], axis=1), WIDE,...  119 us
    dot_general x12, matrix products, dot(): lax.dot_general(a, b, (contract, ((), ())), preferred_element_type=F32)  112 us
    unnamed x206, local copies, waits for them, and re-layouts  67.1 us
    ppermute x48, starting transfers between devices, swap(): return lax.ppermute(values, axis, [(i, i ^ step) for i in range(count)])  51.4 us
    all_gather x1, waiting for transfers between devices, per_device(): out_full = lax.all_gather(w_out, WIDE, axis=0, tiled=True)  44 us
    all_to_all x3, starting transfers between devices, to_slices(): got = lax.all_to_all(sent, GROUP, 0, 0, tiled=True)  27 us
    another operation x6, local copies, waits for them, and re-layouts, own_expert(): both = jnp.stack([got, swap(got, 'y')])  26 us
  transfers between devices with their start and end apart: 64, of which 34 were waited for; matrix products, arithmetic and copies ran while one was open for 25% of the time, Pallas kernels for 0%

profile of v1, /device:TPU:0, one launch (start us, length us, event | category | flops | bytes accessed | tf_op | source)
XLA Modules:
  0.0 1198.6 jit_solution(10731819214937716714)
XLA Ops:
  19.5 15.2 %all_gather.9 = bf16[2,2048]{1,0:T(2,128)(2,1)S(1)} all-gather(bf16[2,512]{1,0:T(2,128)(2,1)S(1)} %pad_maximum_fusion.8), channel_id=1, replica_groups=mesh['t'=1,'g'=4,'p'=2,'y'=2,'c'=2] {'y','c'}, dimensions={1}, use_global_device_ids=true | all-gather | bytes 10240 | tf_op jit(solution)/shard_map/all_gather | solution.py:171
  60.0 119.0 %all-gather.3.cloned.1.call-done = bf16[2048,1536]{1,0:T(8,128)(2,1)} async-done(((bf16[256,1536]{1,0:T(8,128)(2,1)}), bf16[2048,1536]{1,0:T(8,128)(2,1)}) %all-gather.3.cloned.1.call-update) | async-done | bytes 6291472 | tf_op jit(solution)/shard_map/all_gather | solution.py:174
  216.6 44.0 %all-gather.5.cloned.1.call-done = bf16[2048,512]{1,0:T(8,128)(2,1)} async-done(((bf16[256,512]{1,0:T(8,128)(2,1)}), bf16[2048,512]{1,0:T(8,128)(2,1)}) %all-gather.5.cloned.1.call-update) | async-done | bytes 2097168 | tf_op jit(solution)/shard_map/all_gather | solution.py:180
  294.8 19.4 %collective-permute-done.29 = bf16[128,2048]{1,0:T(8,128)(2,1)} collective-permute-done((bf16[128,2048]{1,0:T(8,128)(2,1)}, bf16[128,2048]{1,0:T(8,128)(2,1)}, u32[]{:S(2)}, u32[]{:S(2)}) %collective-permute-start.29) | collective-permute-done | bytes 524320 | tf_op jit(solution)/shard_map/ppermute | solution.py:40
  316.3 15.6 %collective-permute-done.30 = bf16[128,2048]{1,0:T(8,128)(2,1)} collective-permute-done((bf16[128,2048]{1,0:T(8,128)(2,1)}, bf16[128,2048]{1,0:T(8,128)(2,1)}, u32[]{:S(2)}, u32[]{:S(2)}) %collective-permute-start.30) | collective-permute-done | bytes 524320 | tf_op jit(solution)/shard_map/ppermute | solution.py:40
  342.0 18.0 %collective-permute-done.5 = bf16[128,2048]{1,0:T(8,128)(2,1)S(1)} collective-permute-done((bf16[128,2048]{1,0:T(8,128)(2,1)S(1)}, bf16[128,2048]{1,0:T(8,128)(2,1)S(1)}, u32[]{:S(2)}, u32[]{:S(2)}) %collective-permute-start.5) | collective-permute-done | bytes 524320 | tf_op jit(solution)/shard_map/ppermute | solution.py:40
  361.8 12.5 %collective-permute-done.6 = bf16[128,2048]{1,0:T(8,128)(2,1)S(1)} collective-permute-done((bf16[128,2048]{1,0:T(8,128)(2,1)S(1)}, bf16[128,2048]{1,0:T(8,128)(2,1)S(1)}, u32[]{:S(2)}, u32[]{:S(2)}) %collective-permute-start.6) | collective-permute-done | bytes 524320 | tf_op jit(solution)/shard_map/ppermute | solution.py:40
  442.6 36.2 %collective-permute-done.15 = bf16[16,256,256]{2,1,0:T(8,128)(2,1)} collective-permute-done((bf16[16,256,256]{2,1,0:T(8,128)(2,1)}, bf16[16,256,256]{2,1,0:T(8,128)(2,1)}, u32[]{:S(2)}, u32[]{:S(2)}) %collective-permute-start.15) | collective-permute-done | bytes 2097184 | tf_op jit(solution)/shard_map/ppermute | solution.py:40
  515.8 13.3 %fusion.110 = f32[2048,1024]{0,1:T(8,128)} fusion(bf16[2048,2048]{1,0:T(8,128)(2,1)} %constant_dynamic-update-slice_fusion.8, bf16[2048,1024]{0,1:T(8,128)(2,1)S(1)} %bitcast.381), kind=kOutput, calls=%fused_computation.282 | convolution fusion | flops 8589934592 | bytes 20971520 | tf_op jit(solution)/shard_map/dot_general | solution.py:252
  529.2 13.6 %fusion.109 = f32[2048,1024]{0,1:T(8,128)} fusion(bf16[2048,2048]{1,0:T(8,128)(2,1)} %constant_dynamic-update-slice_fusion.8, bf16[2048,1024]{0,1:T(8,128)(2,1)S(1)} %bitcast.384), kind=kOutput, calls=%fused_computation.281 | convolution fusion | flops 8589934592 | bytes 20971520 | tf_op jit(solution)/shard_map/dot_general | solution.py:251
  542.8 19.7 %multiply_convert_fusion.1 = (bf16[2048,1024]{0,1:T(8,128)(2,1)}, f32[2048]{0:T(1024)S(1)}, bf16[2048,1024]{0,1:T(8,128)(2,1)}) fusion(f32[2048,1024]{0,1:T(8,128)} %fusion.109, f32[2048,1024]{0,1:T(8,128)} %fusion.110, f32[2048]{0:T(1024)S(1)} %bitcast.421, bf16[2048,2048]{1,0:T(8,128)(2,1)} %constant_dynamic-update-slice_fusion.25, ...), kind=kOutput, calls=%fused_computation.5 | convolution fusion | flops 8627681280 | bytes 37765120 | tf_op jit(solution)/shard_map/dot_general | solution.py:256
  562.5 15.3 %fusion.111 = f32[2048,2048]{1,0:T(8,128)} fusion(bf16[2048,1024]{0,1:T(8,128)(2,1)} %get-tuple-element.79, bf16[2048,1024]{0,1:T(8,128)(2,1)} %bitcast.383), kind=kOutput, calls=%fused_computation.283 | convolution fusion | flops 8589934592 | bytes 25165824 | tf_op jit(solution)/shard_map/dot_general | solution.py:35
  577.8 16.3 %convolution_add_fusion = f32[2048,2048]{1,0:T(8,128)} fusion(f32[2048,2048]{1,0:T(8,128)} %fusion.111, bf16[2048,1024]{0,1:T(8,128)(2,1)S(1)} %copy-done.82, bf16[2048,1024]{0,1:T(8,128)(2,1)S(1)} %bitcast.382), kind=kOutput, calls=%fused_computation.11 | convolution fusion | flops 8594128896 | bytes 41943040 | tf_op jit(solution)/shard_map/dot_general | solution.py:35
  635.1 11.2 collective-permute-done.36
  646.3 11.2 collective-permute-done.38
  668.3 15.5 %collective-permute-done.35 = bf16[128,2048]{1,0:T(8,128)(2,1)S(1)} collective-permute-done((bf16[128,2048]{1,0:T(8,128)(2,1)}, bf16[128,2048]{1,0:T(8,128)(2,1)S(1)}, u32[]{:S(2)}, u32[]{:S(2)}) %collective-permute-start.35) | collective-permute-done | bytes 524320 | tf_op jit(solution)/shard_map/ppermute | solution.py:40
  683.8 17.2 %collective-permute-done.37 = bf16[128,2048]{1,0:T(8,128)(2,1)S(1)} collective-permute-done((bf16[128,2048]{1,0:T(8,128)(2,1)}, bf16[128,2048]{1,0:T(8,128)(2,1)S(1)}, u32[]{:S(2)}, u32[]{:S(2)}) %collective-permute-start.37) | collective-permute-done | bytes 524320 | tf_op jit(solution)/shard_map/ppermute | solution.py:40
  747.1 16.9 %fusion.26 = f32[2048,1024]{0,1:T(8,128)} fusion(bf16[2048,2048]{1,0:T(8,128)(2,1)} %constant_dynamic-update-slice_fusion.25, f32[2048]{0:T(1024)S(1)} %bitcast.422, f32[2048,1024]{0,1:T(8,128)S(1)} %bitcast.430, f32[2048,1024]{0,1:T(8,128)} %fusion.109), kind=kOutput, calls=%fused_computation.70 | convolution fusion | flops 8604614656 | bytes 33562624 | tf_op jit(solution)/shard_map/dot_general | solution.py:35
  774.5 14.0 %fusion.115 = f32[2048,1024]{0,1:T(8,128)} fusion(bf16[2048,1024]{0,1:T(8,128)(2,1)S(1)} %copy-done.83, bf16[2048,2048]{1,0:T(8,128)(2,1)} %constant_dynamic-update-slice_fusion.8), kind=kOutput, calls=%fused_computation.287 | convolution fusion | flops 8589934592 | bytes 20971520 | tf_op jit(solution)/shard_map/dot_general | solution.py:35
  788.5 33.4 %collective-permute-done.47 = bf16[2048,512]{0,1:T(8,128)(2,1)S(1)} collective-permute-done((bf16[2048,512]{0,1:T(8,128)(2,1)S(1)}, bf16[2048,512]{0,1:T(8,128)(2,1)S(1)}, u32[]{:S(2)}, u32[]{:S(2)}) %collective-permute-start.47) | collective-permute-done | bytes 2097184 | tf_op jit(solution)/shard_map/ppermute | solution.py:40
  828.9 15.2 %all-to-all-start.10 = ((bf16[16,256,256]{2,1,0:T(8,128)(2,1)}), bf16[16,256,256]{2,1,0:T(8,128)(2,1)}, u32[]{:S(2)}, u32[]{:S(2)}) async-start(bf16[16,256,256]{2,1,0:T(8,128)(2,1)} %bitcast.363), calls=%async_computation.12 | async-start | bytes 4194304 | tf_op jit(solution)/shard_map/all_to_all | solution.py:139
  856.0 17.5 %fusion.27 = f32[2048,2048]{1,0:T(8,128)} fusion(bf16[2048,1024]{0,1:T(8,128)(2,1)} %bitcast.379, f32[2048]{0:T(1024)S(1)} %bitcast.423, f32[2048,1024]{0,1:T(8,128)} %fusion.110, f32[2048,1024]{0,1:T(8,128)} %fusion.109), kind=kOutput, calls=%fused_computation.71 | convolution fusion | flops 8604614656 | bytes 37756928 | tf_op jit(solution)/shard_map/dot_general | solution.py:35
  879.6 17.7 %collective-permute-done.46 = bf16[2048,512]{0,1:T(8,128)(2,1)} collective-permute-done((bf16[2048,512]{0,1:T(8,128)(2,1)}, bf16[2048,512]{0,1:T(8,128)(2,1)}, u32[]{:S(2)}, u32[]{:S(2)}) %collective-permute-start.46) | collective-permute-done | bytes 2097184 | tf_op jit(solution)/shard_map/ppermute | solution.py:40
  913.2 12.5 %fusion.114 = f32[2048,1024]{0,1:T(8,128)S(1)} fusion(bf16[2048,1024]{0,1:T(8,128)(2,1)} %get-tuple-element.79, bf16[2048,2048]{1,0:T(8,128)(2,1)} %constant_dynamic-update-slice_fusion.8), kind=kOutput, calls=%fused_computation.286 | convolution fusion | flops 8589934592 | bytes 20971520 | tf_op jit(solution)/shard_map/dot_general | solution.py:35
  926.7 47.4 %collective-permute-done.45 = bf16[2048,512]{0,1:T(8,128)(2,1)S(1)} collective-permute-done((bf16[2048,512]{0,1:T(8,128)(2,1)S(1)}, bf16[2048,512]{0,1:T(8,128)(2,1)S(1)}, u32[]{:S(2)}, u32[]{:S(2)}) %collective-permute-start.45) | collective-permute-done | bytes 2097184 | tf_op jit(solution)/shard_map/ppermute | solution.py:40
  994.8 10.2 fusion.103
  1010.2 18.1 %collective-permute-done.18 = bf16[128,2048]{1,0:T(8,128)(2,1)S(1)} collective-permute-done((bf16[128,2048]{1,0:T(8,128)(2,1)S(1)}, bf16[128,2048]{1,0:T(8,128)(2,1)S(1)}, u32[]{:S(2)}, u32[]{:S(2)}) %collective-permute-start.18) | collective-permute-done | bytes 524320 | tf_op jit(solution)/shard_map/ppermute | solution.py:40
  1028.3 20.5 %collective-permute-done.20 = bf16[128,2048]{1,0:T(8,128)(2,1)S(1)} collective-permute-done((bf16[128,2048]{1,0:T(8,128)(2,1)S(1)}, bf16[128,2048]{1,0:T(8,128)(2,1)S(1)}, u32[]{:S(2)}, u32[]{:S(2)}) %collective-permute-start.20) | collective-permute-done | bytes 524320 | tf_op jit(solution)/shard_map/ppermute | solution.py:40
  1048.7 13.9 %collective-permute-done.22 = bf16[128,2048]{1,0:T(8,128)(2,1)S(1)} collective-permute-done((bf16[128,2048]{1,0:T(8,128)(2,1)S(1)}, bf16[128,2048]{1,0:T(8,128)(2,1)S(1)}, u32[]{:S(2)}, u32[]{:S(2)}) %collective-permute-start.22) | collective-permute-done | bytes 524320 | tf_op jit(solution)/shard_map/ppermute | solution.py:40
  1080.4 36.3 %collective-permute-done.19 = bf16[128,2048]{1,0:T(8,128)(2,1)} collective-permute-done((bf16[128,2048]{1,0:T(8,128)(2,1)}, bf16[128,2048]{1,0:T(8,128)(2,1)}, u32[]{:S(2)}, u32[]{:S(2)}) %collective-permute-start.19) | collective-permute-done | bytes 524320 | tf_op jit(solution)/shard_map/ppermute | solution.py:40
  1118.6 10.6 collective-permute-done.23
  1172.7 15.1 %reduce-scatter.3.cloned.1.call-done = bf16[256,1536]{1,0:T(8,128)(2,1)} async-done(((bf16[2048,1536]{1,0:T(8,128)(2,1)}), bf16[256,1536]{1,0:T(8,128)(2,1)}) %reduce-scatter.3.cloned.1.call-update) | async-done | bytes 786448 | tf_op jit(solution)/shard_map/reduce_scatter | solution.py:337
  (457 shorter events, 470.2 us)
Async XLA Ops:
  7.2 171.9 %all-gather.3.cloned.1.call-start = ((), (), s32[]{:S(2)}) async-start(), calls=%async_computation.13 | async-start | bytes 7077888 | tf_op jit(solution)/shard_map/all_gather | solution.py:174
  13.7 246.9 %all-gather.5.cloned.1.call-start = ((), (), s32[]{:S(2)}) async-start(), calls=%async_computation.14 | async-start | bytes 2359296 | tf_op jit(solution)/shard_map/all_gather | solution.py:180
  13.7 43.5 %collective-permute-start = (bf16[512,512]{1,0:T(8,128)(2,1)}, bf16[512,512]{1,0:T(8,128)(2,1)}, u32[]{:S(2)}, u32[]{:S(2)}) collective-permute-start(bf16[512,512]{1,0:T(8,128)(2,1)} %param.16), channel_id=1, source_target_pairs={{0,1},{1,0},{2,3},{3,2},{4,5},{5,4},{6,7},{7,6},{8,9},{9,8},{10,11... | collective-permute-start | bytes 1572872 | tf_op jit(solution)/shard_map/ppermute | solution.py:40
  34.8 164.4 %all-to-all-start.2 = ((bf16[16,256,256]{2,1,0:T(8,128)(2,1)}), bf16[16,256,256]{2,1,0:T(8,128)(2,1)}, u32[]{:S(2)}, u32[]{:S(2)}) async-start(bf16[16,256,256]{2,1,0:T(8,128)(2,1)} %bitcast.344), calls=%async_computation.2 | async-start | bytes 4194304 | tf_op jit(solution)/shard_map/all_to_all | solution.py:120
  52.8 213.5 %collective-permute-start.24 = (bf16[128,2048]{1,0:T(8,128)(2,1)}, bf16[128,2048]{1,0:T(8,128)(2,1)}, u32[]{:S(2)}, u32[]{:S(2)}) collective-permute-start(bf16[128,2048]{1,0:T(8,128)(2,1)} %bitcast.117), channel_id=1, source_target_pairs={{0,8},{8,0},{16,24},{24,16},{1,9},{9,1},{17,25},{25,17},{2,10},{10... | collective-permute-start | bytes 1572872 | tf_op jit(solution)/shard_map/ppermute | solution.py:40
  54.5 213.9 %collective-permute-start.25 = (bf16[128,2048]{1,0:T(8,128)(2,1)}, bf16[128,2048]{1,0:T(8,128)(2,1)}, u32[]{:S(2)}, u32[]{:S(2)}) collective-permute-start(bf16[128,2048]{1,0:T(8,128)(2,1)} %bitcast.117), channel_id=1, source_target_pairs={{0,16},{8,24},{16,0},{24,8},{1,17},{9,25},{17,1},{25,9},{2,18},{10... | collective-permute-start | bytes 1572872 | tf_op jit(solution)/shard_map/ppermute | solution.py:40
  56.9 211.6 %collective-permute-start.26 = (bf16[128,2048]{1,0:T(8,128)(2,1)}, bf16[128,2048]{1,0:T(8,128)(2,1)}, u32[]{:S(2)}, u32[]{:S(2)}) collective-permute-start(bf16[128,2048]{1,0:T(8,128)(2,1)} %bitcast.117), channel_id=1, source_target_pairs={{0,24},{8,16},{16,8},{24,0},{1,25},{9,17},{17,9},{25,1},{2,26},{10... | collective-permute-start | bytes 1572872 | tf_op jit(solution)/shard_map/ppermute | solution.py:40
  199.2 83.1 %all-to-all-start.1 = ((bf16[16,256,256]{2,1,0:T(8,128)(2,1)}), bf16[16,256,256]{2,1,0:T(8,128)(2,1)}, u32[]{:S(2)}, u32[]{:S(2)}) async-start(bf16[16,256,256]{2,1,0:T(8,128)(2,1)} %bitcast.361), calls=%async_computation.1 | async-start | bytes 4194304 | tf_op jit(solution)/shard_map/all_to_all | solution.py:120
  268.4 45.8 %collective-permute-start.29 = (bf16[128,2048]{1,0:T(8,128)(2,1)}, bf16[128,2048]{1,0:T(8,128)(2,1)}, u32[]{:S(2)}, u32[]{:S(2)}) collective-permute-start(bf16[128,2048]{1,0:T(8,128)(2,1)} %collective-permute-done.25), channel_id=1, source_target_pairs={{0,4},{4,0},{1,5},{5,1},{2,6},{6,2},{3,7},{7,3},{8,12},{12,8},{9,1... | collective-permute-start | bytes 1572872 | tf_op jit(solution)/shard_map/ppermute | solution.py:40
  268.4 63.5 %collective-permute-start.30 = (bf16[128,2048]{1,0:T(8,128)(2,1)}, bf16[128,2048]{1,0:T(8,128)(2,1)}, u32[]{:S(2)}, u32[]{:S(2)}) collective-permute-start(bf16[128,2048]{1,0:T(8,128)(2,1)} %collective-permute-done.26), channel_id=1, source_target_pairs={{0,4},{4,0},{1,5},{5,1},{2,6},{6,2},{3,7},{7,3},{8,12},{12,8},{9,1... | collective-permute-start | bytes 1572872 | tf_op jit(solution)/shard_map/ppermute | solution.py:40
  282.4 109.7 %all-to-all-start.3 = ((bf16[16,256,256]{2,1,0:T(8,128)(2,1)}), bf16[16,256,256]{2,1,0:T(8,128)(2,1)}, u32[]{:S(2)}, u32[]{:S(2)}) async-start(bf16[16,256,256]{2,1,0:T(8,128)(2,1)} %bitcast.360), calls=%async_computation.3 | async-start | bytes 4194304 | tf_op jit(solution)/shard_map/all_to_all | solution.py:120
  291.8 42.3 %collective-permute-start.4 = (bf16[128,2048]{1,0:T(8,128)(2,1)S(1)}, bf16[128,2048]{1,0:T(8,128)(2,1)S(1)}, u32[]{:S(2)}, u32[]{:S(2)}) collective-permute-start(bf16[128,2048]{1,0:T(8,128)(2,1)S(1)} %fusion.83), channel_id=1, source_target_pairs={{0,2},{2,0},{1,3},{3,1},{4,6},{6,4},{5,7},{7,5},{8,10},{10,8},{9,1... | collective-permute-start | bytes 1572872 | tf_op jit(solution)/shard_map/ppermute | solution.py:40
  334.1 90.2 %collective-permute-start.31 = (bf16[1024,2048]{1,0:T(8,128)(2,1)}, bf16[1024,2048]{1,0:T(8,128)(2,1)}, u32[]{:S(2)}, u32[]{:S(2)}) collective-permute-start(bf16[1024,2048]{1,0:T(8,128)(2,1)} %get-tuple-element.110), channel_id=1, source_target_pairs={{0,1},{1,0},{2,3},{3,2},{4,5},{5,4},{6,7},{7,6},{8,9},{9,8},{10,11... | collective-permute-start | bytes 12582920 | tf_op jit(solution)/shard_map/ppermute | solution.py:40
  337.6 91.5 %collective-permute-start.14 = (bf16[16,256,256]{2,1,0:T(8,128)(2,1)}, bf16[16,256,256]{2,1,0:T(8,128)(2,1)}, u32[]{:S(2)}, u32[]{:S(2)}) collective-permute-start(bf16[16,256,256]{2,1,0:T(8,128)(2,1)} %all-to-all-done.2), channel_id=1, source_target_pairs={{0,2},{2,0},{1,3},{3,1},{4,6},{6,4},{5,7},{7,5},{8,10},{10,8},{9,1... | collective-permute-start | bytes 6291464 | tf_op jit(solution)/shard_map/ppermute | solution.py:40
  389.2 48.9 %collective-permute-start.13 = (bf16[16,256,256]{2,1,0:T(8,128)(2,1)}, bf16[16,256,256]{2,1,0:T(8,128)(2,1)}, u32[]{:S(2)}, u32[]{:S(2)}) collective-permute-start(bf16[16,256,256]{2,1,0:T(8,128)(2,1)} %all-to-all-done.1), channel_id=1, source_target_pairs={{0,2},{2,0},{1,3},{3,1},{4,6},{6,4},{5,7},{7,5},{8,10},{10,8},{9,1... | collective-permute-start | bytes 6291464 | tf_op jit(solution)/shard_map/ppermute | solution.py:40
  400.4 78.4 %collective-permute-start.15 = (bf16[16,256,256]{2,1,0:T(8,128)(2,1)}, bf16[16,256,256]{2,1,0:T(8,128)(2,1)}, u32[]{:S(2)}, u32[]{:S(2)}) collective-permute-start(bf16[16,256,256]{2,1,0:T(8,128)(2,1)} %all-to-all-done.3), channel_id=1, source_target_pairs={{0,2},{2,0},{1,3},{3,1},{4,6},{6,4},{5,7},{7,5},{8,10},{10,8},{9,1... | collective-permute-start | bytes 6291464 | tf_op jit(solution)/shard_map/ppermute | solution.py:40
  411.1 99.8 %collective-permute-start.12 = (bf16[1024,2048]{1,0:T(8,128)(2,1)}, bf16[1024,2048]{1,0:T(8,128)(2,1)}, u32[]{:S(2)}, u32[]{:S(2)}) collective-permute-start(bf16[1024,2048]{1,0:T(8,128)(2,1)} %get-tuple-element.126), channel_id=1, source_target_pairs={{0,1},{1,0},{2,3},{3,2},{4,5},{5,4},{6,7},{7,6},{8,9},{9,8},{10,11... | collective-permute-start | bytes 12582920 | tf_op jit(solution)/shard_map/ppermute | solution.py:40
  629.1 533.9 %all-reduce.8.cloned.1.call-start = ((), (), s32[]{:S(2)}) async-start(), calls=%async_computation.15 | async-start | bytes 393216 | tf_op jit(solution)/shard_map/psum | solution.py:356
  766.5 404.4 %reduce-scatter.5.cloned.1.call-start = ((), (), s32[]{:S(2)}) async-start(), calls=%async_computation.17 | async-start | bytes 2359296 | tf_op jit(solution)/shard_map/reduce_scatter | solution.py:295
  773.8 48.2 %collective-permute-start.47 = (bf16[2048,512]{0,1:T(8,128)(2,1)S(1)}, bf16[2048,512]{0,1:T(8,128)(2,1)S(1)}, u32[]{:S(2)}, u32[]{:S(2)}) collective-permute-start(bf16[2048,512]{0,1:T(8,128)(2,1)S(1)} %fusion.15), channel_id=1, source_target_pairs={{0,2},{2,0},{1,3},{3,1},{4,6},{6,4},{5,7},{7,5},{8,10},{10,8},{9,1... | collective-permute-start | bytes 6291464 | tf_op jit(solution)/shard_map/ppermute | solution.py:40
  828.9 78.2 %all-to-all-start.10 = ((bf16[16,256,256]{2,1,0:T(8,128)(2,1)}), bf16[16,256,256]{2,1,0:T(8,128)(2,1)}, u32[]{:S(2)}, u32[]{:S(2)}) async-start(bf16[16,256,256]{2,1,0:T(8,128)(2,1)} %bitcast.363), calls=%async_computation.12 | async-start | bytes 4194304 | tf_op jit(solution)/shard_map/all_to_all | solution.py:139
  844.1 343.6 %reduce-scatter.3.cloned.1.call-start = ((), (), s32[]{:S(2)}) async-start(), calls=%async_computation.16 | async-start | bytes 7077888 | tf_op jit(solution)/shard_map/reduce_scatter | solution.py:337
  848.5 48.7 %collective-permute-start.46 = (bf16[2048,512]{0,1:T(8,128)(2,1)}, bf16[2048,512]{0,1:T(8,128)(2,1)}, u32[]{:S(2)}, u32[]{:S(2)}) collective-permute-start(bf16[2048,512]{0,1:T(8,128)(2,1)} %fusion.14), channel_id=1, source_target_pairs={{0,2},{2,0},{1,3},{3,1},{4,6},{6,4},{5,7},{7,5},{8,10},{10,8},{9,1... | collective-permute-start | bytes 6291464 | tf_op jit(solution)/shard_map/ppermute | solution.py:40
  879.5 115.3 %collective-permute-start.16 = (bf16[2,4,128,2048]{3,2,1,0:T(8,128)(2,1)}, bf16[2,4,128,2048]{3,2,1,0:T(8,128)(2,1)}, u32[]{:S(2)}, u32[]{:S(2)}) collective-permute-start(bf16[2,4,128,2048]{3,2,1,0:T(8,128)(2,1)} %bitcast.32), channel_id=1, source_target_pairs={{0,1},{1,0},{2,3},{3,2},{4,5},{5,4},{6,7},{7,6},{8,9},{9,8},{10,11... | collective-permute-start | bytes 12582920 | tf_op jit(solution)/shard_map/ppermute | solution.py:40
  907.1 74.0 %all-to-all-start.9 = ((bf16[16,256,256]{2,1,0:T(8,128)(2,1)}), bf16[16,256,256]{2,1,0:T(8,128)(2,1)}, u32[]{:S(2)}, u32[]{:S(2)}) async-start(bf16[16,256,256]{2,1,0:T(8,128)(2,1)} %bitcast.364), calls=%async_computation.11 | async-start | bytes 4194304 | tf_op jit(solution)/shard_map/all_to_all | solution.py:139
  926.0 48.1 %collective-permute-start.45 = (bf16[2048,512]{0,1:T(8,128)(2,1)S(1)}, bf16[2048,512]{0,1:T(8,128)(2,1)S(1)}, u32[]{:S(2)}, u32[]{:S(2)}) collective-permute-start(bf16[2048,512]{0,1:T(8,128)(2,1)S(1)} %fusion.13), channel_id=1, source_target_pairs={{0,2},{2,0},{1,3},{3,1},{4,6},{6,4},{5,7},{7,5},{8,10},{10,8},{9,1... | collective-permute-start | bytes 6291464 | tf_op jit(solution)/shard_map/ppermute | solution.py:40
  981.1 154.0 %all-to-all-start.8 = ((bf16[16,256,256]{2,1,0:T(8,128)(2,1)}), bf16[16,256,256]{2,1,0:T(8,128)(2,1)}, u32[]{:S(2)}, u32[]{:S(2)}) async-start(bf16[16,256,256]{2,1,0:T(8,128)(2,1)} %bitcast.362), calls=%async_computation.10 | async-start | bytes 4194304 | tf_op jit(solution)/shard_map/all_to_all | solution.py:139
  1008.1 54.5 %collective-permute-start.22 = (bf16[128,2048]{1,0:T(8,128)(2,1)S(1)}, bf16[128,2048]{1,0:T(8,128)(2,1)S(1)}, u32[]{:S(2)}, u32[]{:S(2)}) collective-permute-start(bf16[128,2048]{1,0:T(8,128)(2,1)S(1)} %get-tuple-element.93), channel_id=1, source_target_pairs={{0,4},{4,0},{1,5},{5,1},{2,6},{6,2},{3,7},{7,3},{8,12},{12,8},{9,1... | collective-permute-start | bytes 1572872 | tf_op jit(solution)/shard_map/ppermute | solution.py:40
  1010.0 70.4 %collective-permute-start.17 = (bf16[128,2048]{1,0:T(8,128)(2,1)}, bf16[128,2048]{1,0:T(8,128)(2,1)}, u32[]{:S(2)}, u32[]{:S(2)}) collective-permute-start(bf16[128,2048]{1,0:T(8,128)(2,1)} %get-tuple-element.92), channel_id=1, source_target_pairs={{0,4},{4,0},{1,5},{5,1},{2,6},{6,2},{3,7},{7,3},{8,12},{12,8},{9,1... | collective-permute-start | bytes 1572872 | tf_op jit(solution)/shard_map/ppermute | solution.py:40
  1065.9 50.8 %collective-permute-start.19 = (bf16[128,2048]{1,0:T(8,128)(2,1)}, bf16[128,2048]{1,0:T(8,128)(2,1)}, u32[]{:S(2)}, u32[]{:S(2)}) collective-permute-start(bf16[128,2048]{1,0:T(8,128)(2,1)} %get-tuple-element.85), channel_id=1, source_target_pairs={{0,8},{8,0},{16,24},{24,16},{1,9},{9,1},{17,25},{25,17},{2,10},{10... | collective-permute-start | bytes 1572872 | tf_op jit(solution)/shard_map/ppermute | solution.py:40
  1071.4 47.2 %collective-permute-start.21 = (bf16[128,2048]{1,0:T(8,128)(2,1)}, bf16[128,2048]{1,0:T(8,128)(2,1)}, u32[]{:S(2)}, u32[]{:S(2)}) collective-permute-start(bf16[128,2048]{1,0:T(8,128)(2,1)} %get-tuple-element.86), channel_id=1, source_target_pairs={{0,16},{8,24},{16,0},{24,8},{1,17},{9,25},{17,1},{25,9},{2,18},{10... | collective-permute-start | bytes 1572872 | tf_op jit(solution)/shard_map/ppermute | solution.py:40
  1071.4 57.9 %collective-permute-start.23 = (bf16[128,2048]{1,0:T(8,128)(2,1)}, bf16[128,2048]{1,0:T(8,128)(2,1)}, u32[]{:S(2)}, u32[]{:S(2)}) collective-permute-start(bf16[128,2048]{1,0:T(8,128)(2,1)} %get-tuple-element.87), channel_id=1, source_target_pairs={{0,24},{8,16},{16,8},{24,0},{1,25},{9,17},{17,9},{25,1},{2,26},{10... | collective-permute-start | bytes 1572872 | tf_op jit(solution)/shard_map/ppermute | solution.py:40
  (120 other events, 4119.6 us)
Sparse Core Ops, SparseCore 0:
  10.8 168.2 all-gather.2
  181.2 79.3 all-gather.4
  766.6 144.6 all-reduce.7
  914.7 109.4 reduce-scatter.4
  1027.6 160.1 reduce-scatter.2

commit v2 on v1

v2 whole, which is shorter than its diff:
```python
import functools

import jax
import jax.numpy as jnp
from jax import lax
from jax.experimental import pallas as pl
from jax.experimental.pallas import tpu as pltpu
from jax.sharding import Mesh
from jax.sharding import PartitionSpec as P

HD = 128
EPS = 1e-05
WIDE = ("t", "g", "p")
NARROW = ("y", "c")
GROUP = ("g", "p", "c")
ALL = ("t", "g", "p", "y", "c")
BF = jnp.bfloat16
F32 = jnp.float32
ROWS = 512
COLS = 256
COST = pl.CostEstimate(flops=1000, transcendentals=0, bytes_accessed=1000)


def rms_scale(values, scales):
    return values * lax.rsqrt(jnp.mean(values * values, axis=-1, keepdims=True) + EPS) * scales


def rope_tables(length, head_dim):
    exponent = jnp.arange(0, head_dim, 2, dtype=F32) / head_dim
    angles = jnp.arange(length, dtype=F32)[:, None] * (10000.0 ** (-exponent))[None, :]
    cosines, sines = jnp.cos(angles), jnp.sin(angles)
    return (
        jnp.concatenate([cosines, cosines], axis=-1),
        jnp.concatenate([-sines, sines], axis=-1),
    )


def dot(a, b, contract):
    return lax.dot_general(a, b, (contract, ((), ())), preferred_element_type=F32)


def call(body, outs, scratch, args, flops, vmem, moved):
    return pl.pallas_call(
        body,
        out_shape=outs,
        in_specs=[pl.BlockSpec(memory_space=pl.ANY)] * len(args),
        out_specs=jax.tree.map(lambda _: pl.BlockSpec(memory_space=pl.ANY), outs),
        scratch_shapes=scratch,
        compiler_params=pltpu.CompilerParams(vmem_limit_bytes=vmem << 20),
        cost_estimate=COST,
    )(*args)


def start_all(copies):
    for one in copies:
        one.start()
    return copies


def wait_all(copies):
    for one in copies:
        one.wait()


def weight_copies(pieces, whole, sems):
    units = whole.shape[2] // 4
    copies = []
    for half, piece in enumerate(pieces):
        for c in range(2):
            k = half * 2 + c
            copies.append(
                pltpu.make_async_copy(
                    piece.at[:, c], whole.at[:, :, pl.ds(k * units, units)], sems.at[k]
                )
            )
    return copies


def block_copies(blocks, whole, sems):
    rows = blocks[0].shape[0]
    return [
        pltpu.make_async_copy(b, whole.at[pl.ds(i * rows, rows)], sems.at[i])
        for i, b in enumerate(blocks)
    ]


def arrived(view, sem):
    pltpu.make_async_copy(view, view, sem).wait()


def await_weight(whole, sems, k, now):
    units = whole.shape[2] // 4

    @pl.when(now)
    def _():
        arrived(whole.at[:, :, pl.ds(pl.multiple_of(k * units, units), units)], sems.at[k])


def await_rows(whole, sems, count, r):
    rows = whole.shape[0] // count
    each = max(1, ROWS // rows)
    if rows <= ROWS:
        for i in range(each):
            b = r * each + i
            arrived(whole.at[pl.ds(pl.multiple_of(b * rows, rows), rows)], sems.at[b])
    else:

        @pl.when(r % (rows // ROWS) == 0)
        def _():
            b = r // (rows // ROWS)
            arrived(whole.at[pl.ds(pl.multiple_of(b * rows, rows), rows)], sems.at[b])


def to_column(line):
    return jnp.transpose(jnp.broadcast_to(line, (128, 128)))


def to_line(column):
    return jnp.transpose(jnp.broadcast_to(column, (128, 128)))[:1]


def take(ref, k):
    part = ref[:, :, pl.ds(pl.multiple_of(k * COLS, COLS), COLS)]
    return part.reshape(-1, COLS)


def take_rows(ref, n):
    each = COLS // ref.shape[1]
    return ref[pl.ds(n * each, each)].reshape(COLS, ref.shape[2])


def project_body(count, *refs):
    blocks, pieces, out = refs[:count], refs[count : count + 2], refs[count + 2]
    rows_v, weight_v, out_v, sem_b, sem_w, sem_o = refs[count + 3 :]
    cw = weight_copies(pieces, weight_v, sem_w)
    cb = block_copies(blocks, rows_v, sem_b)
    ahead = max(1, count * ROWS // rows_v.shape[0])
    start_all(cb[:ahead] + cw + cb[ahead:])
    steps = rows_v.shape[0] // ROWS

    def row_step(r, carry):
        here = pl.ds(pl.multiple_of(r * ROWS, ROWS), ROWS)
        await_rows(rows_v, sem_b, count, r)

        def col_step(k, carry):
            await_weight(weight_v, sem_w, k, r == 0)
            cols = pl.ds(pl.multiple_of(k * COLS, COLS), COLS)
            out_v[here, cols] = dot(rows_v[here, :], take(weight_v, k), ((1,), (0,))).astype(BF)
            return carry

        lax.fori_loop(0, out_v.shape[1] // COLS, col_step, 0)
        pltpu.make_async_copy(out_v.at[here], out.at[here], sem_o.at[r]).start()
        return carry

    lax.fori_loop(0, steps, row_step, 0)
    for r in range(steps):
        here = pl.ds(r * ROWS, ROWS)
        pltpu.make_async_copy(out_v.at[here], out.at[here], sem_o.at[r]).wait()


def project(blocks, got, other):
    rows = blocks[0].shape[0] * len(blocks)
    model = blocks[0].shape[1]
    w, _, depth, units = got.shape
    hidden = 4 * units
    return call(
        functools.partial(project_body, len(blocks)),
        jax.ShapeDtypeStruct((rows, hidden), BF),
        [
            pltpu.VMEM((rows, model), BF),
            pltpu.VMEM((w, depth, hidden), BF),
            pltpu.VMEM((rows, hidden), BF),
            pltpu.SemaphoreType.DMA((len(blocks),)),
            pltpu.SemaphoreType.DMA((4,)),
            pltpu.SemaphoreType.DMA((rows // ROWS,)),
        ],
        (*blocks, got, other),
        2 * rows * model * hidden,
        40,
        2 * (rows * model + model * hidden + rows * hidden),
    )


def expert_body(count, *refs):
    blocks = refs[:count]
    gate_p, up_p = refs[count : count + 2], refs[count + 2 : count + 4]
    down_grad, own_gate = refs[count + 4 : count + 6]
    gg, ug, hs, dots = refs[count + 6 : count + 10]
    (rows_v, gate_v, up_v, grad_v, own_v, gg_v, ug_v, hs_v, dots_v, sem_b, sem_w, sem_i, sem_o) = (
        refs[count + 10 :]
    )
    ci = start_all(
        [
            pltpu.make_async_copy(down_grad, grad_v, sem_i.at[0]),
            pltpu.make_async_copy(own_gate, own_v, sem_i.at[1]),
        ]
    )
    cg = weight_copies(gate_p, gate_v, sem_w.at[0])
    cu = weight_copies(up_p, up_v, sem_w.at[1])
    cb = block_copies(blocks, rows_v, sem_b)
    ahead = max(1, count * ROWS // rows_v.shape[0])
    start_all(cb[:ahead] + [c for two in zip(cg, cu) for c in two] + cb[ahead:])
    wait_all(ci)
    steps = rows_v.shape[0] // ROWS
    lines = ROWS // 128
    outs = ((gg_v, gg, 0), (ug_v, ug, 1), (hs_v, hs, 2))

    def row_step(r, carry):
        here = pl.ds(pl.multiple_of(r * ROWS, ROWS), ROWS)
        await_rows(rows_v, sem_b, count, r)
        mine = own_v[pl.ds(pl.multiple_of(r * lines, lines), lines), :]
        own = jnp.concatenate([to_column(mine[i : i + 1])[:, :1] for i in range(lines)], axis=0)

        def col_step(k, total):
            await_weight(gate_v, sem_w.at[0], k, r == 0)
            await_weight(up_v, sem_w.at[1], k, r == 0)
            cols = pl.ds(pl.multiple_of(k * COLS, COLS), COLS)
            x = rows_v[here, :]
            gate = dot(x, take(gate_v, k), ((1,), (0,)))
            up = dot(x, take(up_v, k), ((1,), (0,)))
            grad = grad_v[here, cols].astype(F32)
            sig = 1.0 / (1.0 + jnp.exp(-gate))
            act = gate * sig
            hidden = act * up
            total = total + jnp.sum(hidden * grad, axis=1, keepdims=True)
            hs_v[here, cols] = (own * hidden).astype(BF)
            grad = own * grad
            gg_v[here, cols] = (grad * up * (sig + act * (1.0 - sig))).astype(BF)
            ug_v[here, cols] = (grad * act).astype(BF)
            return total

        total = lax.fori_loop(
            0, gg_v.shape[1] // COLS, col_step, jnp.zeros((ROWS, 1), F32)
        )
        dots_v[pl.ds(pl.multiple_of(r * lines, lines), lines), :] = jnp.concatenate(
            [to_line(total[i * 128 : (i + 1) * 128]) for i in range(lines)], axis=0
        )
        for src, dst, i in outs:
            pltpu.make_async_copy(src.at[here], dst.at[here], sem_o.at[i, r]).start()
        return carry

    lax.fori_loop(0, steps, row_step, 0)
    last = pltpu.make_async_copy(dots_v, dots, sem_i.at[2])
    last.start()
    for r in range(steps):
        here = pl.ds(r * ROWS, ROWS)
        for src, dst, i in outs:
            pltpu.make_async_copy(src.at[here], dst.at[here], sem_o.at[i, r]).wait()
    last.wait()


def expert(blocks, gate_p, up_p, down_grad, own_gate):
    rows = blocks[0].shape[0] * len(blocks)
    model = blocks[0].shape[1]
    w, _, depth, units = gate_p[0].shape
    hidden = 4 * units
    steps = rows // ROWS
    out = jax.ShapeDtypeStruct((rows, hidden), BF)
    wide = jax.ShapeDtypeStruct(own_gate.shape, F32)
    return call(
        functools.partial(expert_body, len(blocks)),
        (out, out, out, wide),
        [
            pltpu.VMEM((rows, model), BF),
            pltpu.VMEM((w, depth, hidden), BF),
            pltpu.VMEM((w, depth, hidden), BF),
            pltpu.VMEM((rows, hidden), BF),
            pltpu.VMEM(own_gate.shape, F32),
            pltpu.VMEM((rows, hidden), BF),
            pltpu.VMEM((rows, hidden), BF),
            pltpu.VMEM((rows, hidden), BF),
            pltpu.VMEM(own_gate.shape, F32),
            pltpu.SemaphoreType.DMA((len(blocks),)),
            pltpu.SemaphoreType.DMA((2, 4)),
            pltpu.SemaphoreType.DMA((3,)),
            pltpu.SemaphoreType.DMA((3, steps)),
        ],
        (*blocks, *gate_p, *up_p, down_grad, own_gate),
        4 * rows * model * hidden,
        56,
        2 * (rows * model + 2 * model * hidden + 4 * rows * hidden),
    )


def back_body(first, pairs, tail, *refs):
    refs = list(refs)
    ins = [refs[3 * i : 3 * i + 3] for i in range(pairs)]
    at = 3 * pairs
    if tail:
        dots, place = refs[at : at + 2]
        at += 2
    out = refs[at]
    scratch = refs[at + 1 :]
    if tail:
        dots_v, place_v, sem_t = scratch[-3:]
        scratch = scratch[:-3]
        side = start_all(
            [
                pltpu.make_async_copy(dots, dots_v, sem_t.at[0]),
                pltpu.make_async_copy(place, place_v, sem_t.at[1]),
            ]
        )
    grads, weights = scratch[:pairs], scratch[pairs : 2 * pairs]
    out_v, sem_g, sem_w, sem_o = scratch[2 * pairs :]
    rows = out_v.shape[0]
    steps = rows // ROWS
    each = COLS // weights[0].shape[1]
    parts = weights[0].shape[0] // each
    for i, (grad, got, other) in enumerate(ins):
        pltpu.make_async_copy(grad.at[pl.ds(first, ROWS)], grads[i].at[pl.ds(0, ROWS)], sem_g.at[i, 0]).start()
    for n in range(parts):
        place = pl.ds(n * each, each)
        for i, (grad, got, other) in enumerate(ins):
            start_all(weight_copies((got.at[place], other.at[place]), weights[i].at[place], sem_w.at[i, n]))
    for r in range(1, steps):
        for i, (grad, got, other) in enumerate(ins):
            here = pl.ds(r * ROWS, ROWS)
            pltpu.make_async_copy(grad.at[pl.ds(first + r * ROWS, ROWS)], grads[i].at[here], sem_g.at[i, r]).start()

    def row_step(r, carry):
        here = pl.ds(pl.multiple_of(r * ROWS, ROWS), ROWS)
        for i in range(pairs):
            arrived(grads[i].at[here], sem_g.at[i, r])

        def col_step(n, carry):
            for i in range(pairs):
                place = weights[i].at[pl.ds(n * each, each)]
                for k in range(4):
                    await_weight(place, sem_w.at[i, n], k, r == 0)
            cols = pl.ds(pl.multiple_of(n * COLS, COLS), COLS)
            total = dot(grads[0][here, :], take_rows(weights[0], n), ((1,), (1,)))
            for i in range(1, pairs):
                total += dot(grads[i][here, :], take_rows(weights[i], n), ((1,), (1,)))
            out_v[here, cols] = total.astype(BF)
            return carry

        lax.fori_loop(0, parts, col_step, 0)
        pltpu.make_async_copy(out_v.at[here], out.at[here], sem_o.at[r]).start()
        return carry

    if tail:
        wait_all(side)
        for i in range(rows // 128):
            line = dots_v[first // 128 + i : first // 128 + i + 1, :]
            out_v[i * 128 : (i + 1) * 128, parts * COLS :] = (to_column(line) * place_v[...]).astype(BF)
    lax.fori_loop(0, steps, row_step, 0)
    for r in range(steps):
        here = pl.ds(r * ROWS, ROWS)
        pltpu.make_async_copy(out_v.at[here], out.at[here], sem_o.at[r]).wait()


def back(triples, first, rows, tail=()):
    w, _, depth, units = triples[0][1].shape
    model, hidden = w * depth, 4 * units
    n = len(triples)
    full = model + 128 if tail else model
    return call(
        functools.partial(back_body, first, n, bool(tail)),
        jax.ShapeDtypeStruct((rows, full), BF),
        [pltpu.VMEM((rows, hidden), BF)] * n
        + [pltpu.VMEM((w, depth, hidden), BF)] * n
        + [
            pltpu.VMEM((rows, full), BF),
            pltpu.SemaphoreType.DMA((n, rows // ROWS)),
            pltpu.SemaphoreType.DMA((n, model // COLS, 4)),
            pltpu.SemaphoreType.DMA((rows // ROWS,)),
        ]
        + [pltpu.VMEM(t.shape, F32) for t in tail]
        + [pltpu.SemaphoreType.DMA((2,))] * bool(tail),
        [a for t in triples for a in t] + list(tail),
        2 * n * rows * model * hidden,
        40,
        2 * (n * rows * hidden + n * model * hidden + rows * model),
    )


def weight_body(count, depth, *refs):
    blocks, grad, mine, theirs = refs[:count], refs[count], refs[count + 1], refs[count + 2]
    rows_v, grad_v, out_v, sem_b, sem_g, sem_o = refs[count + 3 :]
    cg = pltpu.make_async_copy(grad, grad_v, sem_g.at[0])
    wait_all(start_all(block_copies(blocks, rows_v, sem_b) + [cg]))
    units = COLS
    each = COLS // depth
    steps = rows_v.shape[1] // COLS

    def step(n, carry):
        cols = pl.ds(pl.multiple_of(n * COLS, COLS), COLS)
        got = dot(rows_v[:, cols], grad_v[...], ((0,), (0,))).astype(BF)
        for k in range(4):
            part = got[:, k * units : (k + 1) * units].reshape(each, depth, units)
            out_v[k // 2, pl.ds(n * each, each), k % 2] = part
        place = pl.ds(n * each, each)
        pltpu.make_async_copy(out_v.at[0, place], mine.at[place], sem_o.at[0, n]).start()
        pltpu.make_async_copy(out_v.at[1, place], theirs.at[place], sem_o.at[1, n]).start()
        return carry

    lax.fori_loop(0, steps, step, 0)
    for n in range(steps):
        place = pl.ds(n * each, each)
        pltpu.make_async_copy(out_v.at[0, place], mine.at[place], sem_o.at[0, n]).wait()
        pltpu.make_async_copy(out_v.at[1, place], theirs.at[place], sem_o.at[1, n]).wait()


def weight_grad(blocks, grad, depth):
    rows = blocks[0].shape[0] * len(blocks)
    model = blocks[0].shape[1]
    hidden = grad.shape[1]
    w = model // depth
    piece = jax.ShapeDtypeStruct((w, 2, depth, hidden // 4), BF)
    steps = model // COLS
    return call(
        functools.partial(weight_body, len(blocks), depth),
        (piece, piece),
        [
            pltpu.VMEM((rows, model), BF),
            pltpu.VMEM((rows, hidden), BF),
            pltpu.VMEM((2, w, 2, depth, hidden // 4), BF),
            pltpu.SemaphoreType.DMA((len(blocks),)),
            pltpu.SemaphoreType.DMA((1,)),
            pltpu.SemaphoreType.DMA((2, steps)),
        ],
        (*blocks, grad),
        2 * rows * model * hidden,
        40,
        2 * (rows * model + model * hidden + rows * hidden),
    )


def terms_body(pairs, *refs):
    ins, me, outs = refs[: 2 * pairs], refs[2 * pairs], refs[2 * pairs + 1 : 2 * pairs + 3]
    scratch = refs[2 * pairs + 3 :]
    held, out_v, sems, out_sem = scratch[: 2 * pairs], scratch[-3], scratch[-2], scratch[-1]
    wait_all(
        start_all(
            [pltpu.make_async_copy(ins[i], held[i], sems.at[i]) for i in range(2 * pairs)]
        )
    )
    _, count, _, depth, _ = out_v.shape
    mine = me[0]

    each = COLS // depth

    def step(n, carry):
        rows = pl.ds(pl.multiple_of(n * COLS, COLS), COLS)
        at = 0
        for i in range(pairs):
            wide = held[2 * i + 1].shape[1]
            got = dot(held[2 * i][:, rows], held[2 * i + 1][...], ((0,), (0,))).astype(BF)
            for j in range(each):
                b = n * each + j
                distance = jnp.bitwise_xor(b % 8, mine)
                half = distance % 2
                far = distance // 2
                place = (far % 2) * 2 + far // 2
                out_v[half, b // 8, place, :, at : at + wide] = got[j * depth : (j + 1) * depth]
            at += wide
        return carry

    lax.fori_loop(0, count * 8 // each, step, 0)
    wait_all(
        start_all([pltpu.make_async_copy(out_v.at[i], outs[i], out_sem.at[i]) for i in range(2)])
    )


def block_terms(pairs, me, depth):
    length, model = pairs[0][0].shape
    count = model // (8 * depth)
    n = sum(c.shape[1] for _, c in pairs)
    piece = jax.ShapeDtypeStruct((count, 4, depth, n), BF)
    flat = [x for two in pairs for x in two]
    return pl.pallas_call(
        functools.partial(terms_body, len(pairs)),
        out_shape=(piece, piece),
        in_specs=[pl.BlockSpec(memory_space=pl.ANY)] * len(flat)
        + [pl.BlockSpec(memory_space=pltpu.SMEM)],
        out_specs=(pl.BlockSpec(memory_space=pl.ANY),) * 2,
        scratch_shapes=[pltpu.VMEM(x.shape, BF) for x in flat]
        + [
            pltpu.VMEM((2,) + piece.shape, BF),
            pltpu.SemaphoreType.DMA((len(flat),)),
            pltpu.SemaphoreType.DMA((2,)),
        ],
        compiler_params=pltpu.CompilerParams(vmem_limit_bytes=24 << 20),
        cost_estimate=COST,
    )(*flat, me)


def to_columns(line):
    return jnp.concatenate(
        [to_column(line[:, i : i + 128])[:, :1] for i in range(0, line.shape[1], 128)], axis=0
    )


def to_lines(column):
    return jnp.concatenate(
        [to_line(column[i : i + 128]) for i in range(0, column.shape[0], 128)], axis=1
    )


def bring(ins, held, sems):
    wait_all(
        start_all([pltpu.make_async_copy(a, b, sems.at[i]) for i, (a, b) in enumerate(zip(ins, held))])
    )


def send_out(held, outs, sems):
    wait_all(
        start_all([pltpu.make_async_copy(a, b, sems.at[i]) for i, (a, b) in enumerate(zip(held, outs))])
    )


def raw_body(normed, weights, query, key, value, squares, *scratch):
    normed_v, weights_v, query_v, key_v, value_v, squares_v, sem_i, sem_o = scratch
    wide = query_v.shape[1]
    bring((normed, weights.at[:, pl.ds(0, 3 * wide)]), (normed_v, weights_v), sem_i)
    length = query_v.shape[0]
    for place, ref in ((0, query_v), (1, key_v)):

        def step(j, total):
            cols = pl.ds(pl.multiple_of(j * COLS, COLS), COLS)
            w = weights_v[:, pl.ds(pl.multiple_of(place * wide + j * COLS, COLS), COLS)]
            got = dot(normed_v[...], w, ((1,), (0,)))
            ref[:, cols] = got
            return total + jnp.sum(got * got, axis=1, keepdims=True)

        total = lax.fori_loop(0, wide // COLS, step, jnp.zeros((length, 1), F32))
        squares_v[place : place + 1, :] = to_lines(total)

    def step(j, carry):
        cols = pl.ds(pl.multiple_of(j * COLS, COLS), COLS)
        w = weights_v[:, pl.ds(pl.multiple_of(2 * wide + j * COLS, COLS), COLS)]
        value_v[:, cols] = dot(normed_v[...], w, ((1,), (0,))).astype(BF)
        return carry

    lax.fori_loop(0, wide // COLS, step, 0)
    send_out((query_v, key_v, value_v, squares_v), (query, key, value, squares), sem_o)


def raw_heads(normed, weights, wide):
    length, model = normed.shape
    shapes = [((length, wide), F32), ((length, wide), F32), ((length, wide), BF), ((2, length), F32)]
    return call(
        raw_body,
        tuple(jax.ShapeDtypeStruct(*one) for one in shapes),
        [pltpu.VMEM((length, model), BF), pltpu.VMEM((model, 3 * wide), BF)]
        + [pltpu.VMEM(*one) for one in shapes]
        + [pltpu.SemaphoreType.DMA((2,)), pltpu.SemaphoreType.DMA((4,))],
        (normed, weights),
        0,
        32,
        0,
    )


def half_turn(values):
    return pltpu.roll(values, HD // 2, 1)


def attend_body(*refs):
    ins, outs, scratch = refs[:10], refs[10:15], refs[15:]
    held, made, sem_i, sem_o = scratch[:10], scratch[10:15], scratch[15], scratch[16]
    query, key, value, scales, gains, cosines, sines, ids, weights = ins[:9]
    wide = query.shape[1]
    views = list(ins[:9])
    views[8] = weights.at[:, pl.ds(3 * wide, wide)]
    bring(views, held[:9], sem_i)
    query_v, key_v, value_v, scales_v, gains_v, cos_v, sin_v, ids_v, weights_v = held[:9]
    query_o, key_o, attended_o, log_o, out_o = made
    line = ids_v[...]
    allowed = line <= to_columns(line)
    scale_q, scale_k = to_columns(scales_v[0:1, :]), to_columns(scales_v[1:2, :])

    def step(h, carry):
        cols = pl.ds(pl.multiple_of(h * HD, HD), HD)
        cosines, sines = cos_v[...], sin_v[...]
        q = query_v[:, cols] * scale_q * gains_v[0:1, cols]
        k = key_v[:, cols] * scale_k * gains_v[1:2, cols]
        q = (q * cosines + half_turn(q) * sines).astype(BF)
        k = (k * cosines + half_turn(k) * sines).astype(BF)
        query_o[:, cols] = q
        key_o[:, cols] = k
        scores = jnp.where(allowed, dot(q, k, ((1,), (1,))) * HD**-0.5, -1e30)
        highest = jnp.max(scores, axis=1, keepdims=True)
        shifted = jnp.exp(scores - highest)
        totals = jnp.sum(shifted, axis=1, keepdims=True)
        probs = (shifted / totals).astype(BF)
        attended_o[:, cols] = dot(probs, value_v[:, cols], ((1,), (0,))).astype(BF)
        log_o[pl.ds(h, 1), :] = to_lines(highest + jnp.log(totals))
        return carry

    lax.fori_loop(0, wide // HD, step, 0)

    def out_step(j, carry):
        cols = pl.ds(pl.multiple_of(j * COLS, COLS), COLS)
        out_o[:, cols] = dot(attended_o[...], weights_v[cols, :], ((1,), (1,))).astype(BF)
        return carry

    lax.fori_loop(0, out_o.shape[1] // COLS, out_step, 0)
    send_out(made, outs, sem_o)


def attend(query, key, value, scales, gains, tables, ids, weights):
    length, wide = query.shape
    model = weights.shape[0]
    args = (query, key, value, scales, gains, *tables, ids, weights, ids)
    held = [pltpu.VMEM(x.shape, x.dtype) for x in args[:8]]
    held += [pltpu.VMEM((model, wide), BF), pltpu.VMEM(ids.shape, ids.dtype)]
    shapes = [
        ((length, wide), BF),
        ((length, wide), BF),
        ((length, wide), BF),
        ((wide // HD, length), F32),
        ((length, model), BF),
    ]
    return call(
        attend_body,
        tuple(jax.ShapeDtypeStruct(*one) for one in shapes),
        held
        + [pltpu.VMEM(*one) for one in shapes]
        + [pltpu.SemaphoreType.DMA((9,)), pltpu.SemaphoreType.DMA((5,))],
        args,
        0,
        32,
        0,
    )


def unattend_body(*refs):
    ins, outs, scratch = refs[:12], refs[12:16], refs[16:]
    held, grad_v, made, sem_i, sem_o = (
        scratch[:12], scratch[12], scratch[13:17], scratch[17], scratch[18],
    )
    wide = ins[2].shape[1]
    views = list(ins)
    views[1] = ins[1].at[:, pl.ds(3 * wide, wide)]
    bring(views, held, sem_i)
    cot_v, weights_v, query_v, key_v, value_v, log_v, ids_v, cos_v, sin_v, gains_v, raw_q, raw_k = held
    query_o, key_o, value_o, dots_o = made
    grad_v[...] = dot(cot_v[...], weights_v[...], ((1,), (0,))).astype(BF)
    line = ids_v[...]
    allowed = line <= to_columns(line)
    length = cot_v.shape[0]
    zero = jnp.zeros((length, 1), F32)

    def step(h, carry):
        dot_q, dot_k = carry
        cols = pl.ds(pl.multiple_of(h * HD, HD), HD)
        cosines, sines = cos_v[...], sin_v[...]
        q, k, v, grad = query_v[:, cols], key_v[:, cols], value_v[:, cols], grad_v[:, cols]
        scores = jnp.where(allowed, dot(q, k, ((1,), (1,))) * HD**-0.5, -1e30)
        probs = jnp.exp(scores - to_columns(log_v[pl.ds(h, 1), :]))
        prob_grad = dot(grad, v, ((1,), (1,)))
        centre = jnp.sum(probs * prob_grad, axis=1, keepdims=True)
        score_grad = (probs * (prob_grad - centre)).astype(BF)
        value_o[:, cols] = dot(probs.astype(BF), grad, ((0,), (0,))).astype(BF)
        back_q = dot(score_grad, k, ((1,), (0,))) * HD**-0.5
        back_k = dot(score_grad, q, ((0,), (0,))) * HD**-0.5
        back_q = back_q * cosines + half_turn(back_q * sines)
        back_k = back_k * cosines + half_turn(back_k * sines)
        query_o[:, cols] = back_q
        key_o[:, cols] = back_k
        dot_q += jnp.sum(gains_v[0:1, cols] * back_q * raw_q[:, cols], axis=1, keepdims=True)
        dot_k += jnp.sum(gains_v[1:2, cols] * back_k * raw_k[:, cols], axis=1, keepdims=True)
        return dot_q, dot_k

    dot_q, dot_k = lax.fori_loop(0, wide // HD, step, (zero, zero))
    dots_o[0:1, :] = to_lines(dot_q)
    dots_o[1:2, :] = to_lines(dot_k)
    send_out(made, outs, sem_o)


def unattend(out_cot, weights, query, key, value, logs, ids, tables, gains, raw_q, raw_k):
    length, wide = query.shape
    args = (out_cot, weights, query, key, value, logs, ids, *tables, gains, raw_q, raw_k)
    held = [pltpu.VMEM(x.shape, x.dtype) for x in args]
    held[1] = pltpu.VMEM((weights.shape[0], wide), BF)
    shapes = [((length, wide), F32), ((length, wide), F32), ((length, wide), BF), ((2, length), F32)]
    return call(
        unattend_body,
        tuple(jax.ShapeDtypeStruct(*one) for one in shapes),
        held
        + [pltpu.VMEM((length, wide), BF)]
        + [pltpu.VMEM(*one) for one in shapes]
        + [pltpu.SemaphoreType.DMA((12,)), pltpu.SemaphoreType.DMA((4,))],
        args,
        0,
        40,
        0,
    )


def unnorm_body(*refs):
    ins, outs, scratch = refs[:7], refs[7:9], refs[9:]
    held, made, sem_i, sem_o = scratch[:7], scratch[7:9], scratch[9], scratch[10]
    bring(ins, held, sem_i)
    back_q, back_k, raw_q, raw_k, scales_v, dots_v, gains_v = held
    grads_o, gains_o = made
    wide = raw_q.shape[1]
    for i, (back, raw) in enumerate(((back_q, raw_q), (back_k, raw_k))):
        scale = to_columns(scales_v[i : i + 1, :])
        push = to_columns(dots_v[i : i + 1, :]) * scale * scale * scale
        grad = scale * gains_v[i : i + 1, :] * back[...] - raw[...] * push
        grads_o[:, i * wide : (i + 1) * wide] = grad.astype(BF)
        gains_o[i : i + 1, :] = jnp.sum(back[...] * raw[...] * scale, axis=0, keepdims=True)
    send_out(made, outs, sem_o)


def unnorm(back_q, back_k, raw_q, raw_k, scales, dots, gains):
    length, wide = raw_q.shape
    args = (back_q, back_k, raw_q, raw_k, scales, dots, gains)
    shapes = [((length, 2 * wide), BF), ((2, wide), F32)]
    return call(
        unnorm_body,
        tuple(jax.ShapeDtypeStruct(*one) for one in shapes),
        [pltpu.VMEM(x.shape, x.dtype) for x in args]
        + [pltpu.VMEM(*one) for one in shapes]
        + [pltpu.SemaphoreType.DMA((7,)), pltpu.SemaphoreType.DMA((2,))],
        args,
        0,
        24,
        0,
    )


def after(values, *earlier):
    return lax.optimization_barrier((values, earlier))[0]


def stage(*values):
    return lax.optimization_barrier(values)


def swap(values, axis, step=1):
    count = lax.axis_size(axis)
    return lax.ppermute(values, axis, [(i, i ^ step) for i in range(count)])


def gather_four(block, axis):
    count = lax.axis_size("y") * lax.axis_size("c")
    size = block.shape[axis]
    here = lax.axis_index("y") * lax.axis_size("c") + lax.axis_index("c")
    other = swap(block, "y")
    near = swap(block, "c")
    far = swap(other, "c")
    shape = list(block.shape)
    shape[axis] = size * count
    whole = jnp.zeros(shape, block.dtype)
    for piece, place in ((block, 0), (near, 1), (other, 2), (far, 3)):
        whole = lax.dynamic_update_slice_in_dim(whole, piece, (here ^ place) * size, axis)
    return whole


def sum_near(partial):
    length, width = partial.shape
    y, c = lax.axis_index("y"), lax.axis_index("c")
    parts = partial.reshape(2, 2, length // 4, width)
    mine = lax.dynamic_index_in_dim(parts, c, 1, False)
    theirs = lax.dynamic_index_in_dim(parts, 1 - c, 1, False)
    mine = mine.astype(F32) + swap(theirs.astype(BF), "c").astype(F32)
    keep = lax.dynamic_index_in_dim(mine, y, 0, False)
    send = lax.dynamic_index_in_dim(mine, 1 - y, 0, False)
    return keep, send.astype(BF)


def add(*pieces):
    total = pieces[0].astype(F32)
    for piece in pieces[1:]:
        total = total + piece.astype(F32)
    return total


def to_experts(columns):
    sent = lax.all_to_all(columns.T, GROUP, 0, 0, tiled=True)
    v = sent.reshape((-1, 2) + sent.shape[1:])
    c = lax.axis_index("c")
    own = lax.dynamic_index_in_dim(v, c, 1, False)
    other = lax.dynamic_index_in_dim(v, 1 - c, 1, False)
    return jnp.concatenate([own, other]).reshape(sent.shape[0], -1)


def to_group(weight):
    got = lax.all_to_all(weight, GROUP, 0, 0, tiled=True)
    return got.reshape((got.shape[0] // 2, 2) + got.shape[1:])


def over_sequences(*terms):
    if lax.axis_size("t") > 1:
        terms = [lax.psum_scatter(x, "t", scatter_dimension=0, tiled=True) for x in terms]
    return [x[0] for x in terms]


def over_groups(piece):
    if lax.axis_size("t") > 1:
        piece = lax.all_gather(piece, "t", axis=0, tiled=True)
    return piece


def sum_over(values, axis):
    step = 1
    while step < lax.axis_size(axis):
        values = values + swap(values, axis, step)
        step *= 2
    return values


def to_slices(mine, theirs):
    total = (mine.astype(F32) + theirs.astype(F32)).astype(BF)
    if lax.axis_size("t") > 1:
        total = lax.psum_scatter(total, "t", scatter_dimension=0, tiled=True)
    sent = total.reshape((-1,) + total.shape[2:])
    return lax.all_to_all(sent, GROUP, 0, 0, tiled=True)


def as_output(got):
    return jnp.transpose(got, (1, 0, 2)).astype(F32)


def per_device(
    tokens,
    cotangent,
    block_ids,
    routes,
    norm_attn,
    w_query,
    w_key,
    w_value,
    norm_query,
    norm_key,
    w_out,
    norm_ffn,
    w_router,
    w_gate,
    w_up,
    w_down,
):
    experts = w_router.shape[1]
    lane_index = lax.axis_index("y") * lax.axis_size("c") + lax.axis_index("c")
    lanes = lax.axis_size("y") * lax.axis_size("c")
    length, head_cols = tokens.shape
    model_width = head_cols * lanes
    rows = length // lanes

    all_full = lax.all_gather(
        jnp.concatenate([w_query, w_key, w_value, w_out], axis=1), WIDE, axis=0, tiled=True
    )

    rows_full = gather_four(tokens, 1)
    gains = lax.all_gather(jnp.stack([norm_attn, norm_ffn]), NARROW, axis=1, tiled=True)
    down_got = to_group(jnp.transpose(w_down, (1, 0, 2)))
    gate_sent = jnp.transpose(w_gate, (1, 0, 2))
    up_sent = jnp.transpose(w_up, (1, 0, 2))
    cot_rows = lax.all_to_all(cotangent.reshape(lanes, rows, head_cols), NARROW, 0, 0, tiled=True)
    cot_rows = jnp.transpose(cot_rows, (1, 0, 2)).reshape(rows, model_width)
    rows_full, cot_rows, gate_sent, up_sent, gains = stage(
        rows_full, cot_rows, gate_sent, up_sent, gains
    )
    attn_gain = gains[0].astype(F32)
    ffn_gain = gains[1].astype(F32)
    rows_float = rows_full.astype(F32)
    normed = rms_scale(rows_float, attn_gain).astype(BF)
    down_got, gate_sent, normed, cot_sent = stage(down_got, gate_sent, normed, cot_rows)

    down_other = swap(down_got, "y")
    all_full, normed, cot_sent, gate_sent, down_other = stage(
        all_full, normed, cot_sent, gate_sent, down_other
    )

    gate_got = to_group(gate_sent)
    cot_mine = lax.all_gather(cot_sent, ("g", "p"), axis=0, tiled=True)
    qkv_full = all_full[:, : 3 * head_cols]
    raw_query, raw_key, value_bf, squares = raw_heads(normed, all_full, head_cols)
    scales = lax.rsqrt(lax.psum(squares, NARROW) / model_width + EPS)
    scales, gate_got, up_sent = stage(scales, gate_got, up_sent)
    up_got = to_group(up_sent)
    cut = gate_got.shape[0] // 2
    gate_first = swap(gate_got[:cut], "y")
    gains_here = jnp.stack([norm_query, norm_key]).astype(F32)
    tables = rope_tables(length, HD)
    ids = block_ids.astype(F32)
    query_bf, key_bf, attended, log_totals, out_partial = attend(
        raw_query, raw_key, value_bf, scales, gains_here, tables, ids, all_full
    )

    first_row = lane_index * rows
    x_rows = lax.dynamic_slice_in_dim(rows_full, first_row, rows, 0).astype(F32)
    keep, send = sum_near(out_partial)
    keep, send, gate_first = stage(keep, send, gate_first)
    residual = x_rows + keep + swap(send, "y").astype(F32)
    ffn_in = rms_scale(residual, ffn_gain).astype(BF)
    ffn_in, up_got, gate_got, cot_mine = stage(ffn_in, up_got, gate_got, cot_mine)

    up_other = swap(up_got, "y")
    gate_last = swap(gate_got[cut:], "y")
    x_mine = lax.all_gather(ffn_in, ("g", "p"), axis=0, tiled=True)
    cot_all = [cot_mine, swap(cot_mine, "c")]
    down_own = (over_groups(down_got), over_groups(down_other))
    down_grad = project(cot_all, *down_own)
    logits = jnp.dot(ffn_in, w_router, preferred_element_type=F32)
    gate_probs = jax.nn.softmax(logits, axis=-1)
    routes_rows = lax.dynamic_slice_in_dim(routes, first_row, rows, 0)
    chosen = jnp.any(
        routes_rows[:, :, None] == jnp.arange(experts, dtype=jnp.int32)[None, None, :], axis=1
    )
    own_gate = to_experts(jnp.where(chosen, gate_probs, 0.0))
    x_mine, down_grad, own_gate, up_other, gate_last = stage(
        x_mine, down_grad, own_gate, up_other, gate_last
    )
    gate_other = jnp.concatenate([gate_first, gate_last])
    x_all = [x_mine, swap(x_mine, "c")]
    gate_own = (over_groups(gate_got), over_groups(gate_other))
    up_own = (over_groups(up_got), over_groups(up_other))

    gate_grad, up_grad, hidden_gated, own_dots = expert(
        x_all, gate_own, up_own, down_grad, own_gate
    )
    half = gate_grad.shape[0] // 2
    own_index = lax.axis_index("g") * 4 + lax.axis_index("p") * 2 + lax.axis_index("c")
    depth = down_own[0].shape[2]
    own_place = (jnp.arange(128) == own_index).astype(F32)[None]
    depth = down_own[0].shape[2]
    pairs = ((gate_grad, *gate_own), (up_grad, *up_own))
    theirs = back(pairs, half, half, (own_dots, own_place))
    gate_grad, up_grad, own_dots, theirs = stage(gate_grad, up_grad, own_dots, theirs)
    pairs = ((gate_grad, *gate_own), (up_grad, *up_own))
    mine = back(pairs, 0, half, (own_dots, own_place))
    sent = add(mine, swap(theirs, "c")).astype(BF)
    sent, hidden_gated, gate_grad, up_grad = stage(sent, hidden_gated, gate_grad, up_grad)

    input_sum = lax.psum_scatter(sent, ("g", "p"), scatter_dimension=0, tiled=True)
    down_mine, down_theirs = weight_grad(cot_all, hidden_gated, depth)
    down_theirs, gate_grad, hidden_gated, up_grad = stage(
        down_theirs, gate_grad, hidden_gated, up_grad
    )
    down_theirs = swap(down_theirs, "y")
    gate_mine, gate_theirs = weight_grad(x_all, gate_grad, depth)
    up_mine, up_theirs = weight_grad(x_all, up_grad, depth)
    moe_pair = ((hidden_gated, *down_own),)
    moe_theirs = back(moe_pair, half, half)
    moe_mine = back(moe_pair, 0, half)
    down_theirs, gate_theirs, up_theirs, moe_theirs, moe_mine = stage(
        down_theirs, gate_theirs, up_theirs, moe_theirs, moe_mine
    )
    gate_theirs = swap(gate_theirs, "y")
    down_got = to_slices(down_mine, down_theirs)
    moe_sent = add(moe_mine, swap(moe_theirs, "c")).astype(BF)
    input_sum, moe_sent, gate_theirs = stage(input_sum, moe_sent, gate_theirs)
    moe_sum = lax.psum_scatter(moe_sent, ("g", "p"), scatter_dimension=0, tiled=True)
    gate_got = to_slices(gate_mine, gate_theirs)
    input_sum = input_sum.astype(F32)
    pair_dots = jnp.where(chosen, input_sum[:, model_width : model_width + experts], 0.0)
    input_sum = input_sum[:, :model_width]

    logit_grad = (
        gate_probs * (pair_dots - jnp.sum(gate_probs * pair_dots, axis=1, keepdims=True))
    ).astype(BF)
    ffn_grad = input_sum + dot(logit_grad, w_router, ((1,), (1,)))
    router_grad = dot(logit_grad, ffn_in, ((0,), (0,)))
    _, ffn_norm_pull = jax.vjp(rms_scale, residual, ffn_gain)
    residual_norm_grad, ffn_gain_grad = ffn_norm_pull(ffn_grad)
    residual_grad = cot_rows.astype(F32) + residual_norm_grad
    out_cot = gather_four(residual_grad.astype(BF), 0)
    out_cot, up_theirs, down_got = stage(out_cot, up_theirs, down_got)

    back_query, back_key, value_grad, dots = unattend(
        out_cot, all_full, query_bf, key_bf, value_bf, log_totals, ids, tables, gains_here,
        raw_query, raw_key,
    )
    group_index = (lax.axis_index("g") * 2 + lax.axis_index("p")).astype(jnp.int32)[None]
    two_keep, two_near = over_sequences(
        *block_terms(((out_cot, attended), (normed, value_grad)), group_index, depth)
    )
    dots, two_near, two_keep = stage(dots, two_near, two_keep)
    two_near = swap(two_near, "p")
    dots = lax.psum(dots, NARROW) / model_width
    dots, up_theirs = stage(dots, up_theirs)

    up_theirs = swap(up_theirs, "y")
    pair_pre, pair_gains = unnorm(
        back_query, back_key, raw_query, raw_key, scales, dots, gains_here
    )
    qkv_grad = jnp.concatenate([pair_pre, value_grad], axis=1)
    pair_keep, pair_near = over_sequences(*block_terms(((normed, pair_pre),), group_index, depth))
    qkv_grad, pair_keep, pair_near = stage(qkv_grad, pair_keep, pair_near)
    pair_near = swap(pair_near, "p")
    keep, send = sum_near(dot(qkv_grad, qkv_full, ((1,), (1,))))
    keep, send, two_near, two_keep, up_theirs, gate_got = stage(
        keep, send, two_near, two_keep, up_theirs, gate_got
    )
    up_got = to_slices(up_mine, up_theirs)
    send = swap(send, "y")
    normed_grad = add(keep, send)
    two_parts = add(two_keep, two_near)
    two_far = swap(two_parts[2:].astype(BF), "g", 1)
    _, attn_norm_pull = jax.vjp(rms_scale, x_rows, attn_gain)
    rows_norm_grad, attn_gain_grad = attn_norm_pull(normed_grad)
    grad_rows = (residual_grad + rows_norm_grad).astype(BF)
    place = (jnp.arange(lanes) == lane_index).astype(F32)[:, None]
    small = jnp.concatenate(
        [
            router_grad,
            attn_gain_grad[None],
            ffn_gain_grad[None],
            (place * pair_gains[:1]).reshape(1, model_width),
            (place * pair_gains[1:]).reshape(1, model_width),
        ],
        axis=0,
    )
    small = sum_over(small, "c")
    small = sum_over(small, "y")
    grad_rows, two_far, two_parts, pair_near, pair_keep, small, moe_sum = stage(
        grad_rows, two_far, two_parts, pair_near, pair_keep, small, moe_sum
    )

    pair_parts = add(pair_keep, pair_near)
    pair_far = swap(pair_parts[2:].astype(BF), "g", 1)
    two_parts = add(two_parts[:2], two_far)
    two_far = swap(two_parts[1].astype(BF), "g", 2)
    small = sum_over(small, "p")
    pair_far, pair_parts, two_far, two_parts, small, up_got, grad_rows, moe_sum = stage(
        pair_far, pair_parts, two_far, two_parts, small, up_got, grad_rows, moe_sum
    )

    pair_parts = add(pair_parts[:2], pair_far)
    pair_far = swap(pair_parts[1].astype(BF), "g", 2)
    small = sum_over(sum_over(small, "g"), "t")
    grad_two = add(two_parts[0], two_far)
    both_rows = jnp.stack([(residual + moe_sum.astype(F32)).astype(BF), grad_rows])
    both_rows = jnp.transpose(both_rows.reshape(2, rows, lanes, head_cols), (2, 0, 1, 3))
    both_rows = lax.all_to_all(both_rows, NARROW, 0, 0, tiled=True)
    block_out = both_rows[:, 0].reshape(length, head_cols)
    grad_tokens = both_rows[:, 1].reshape(length, head_cols).astype(F32)
    grad_gate = as_output(gate_got)
    grad_down = as_output(down_got)
    grad_up = as_output(up_got)
    grad_pair = add(pair_parts[0], pair_far)
    grad_out, grad_value = grad_two[:, :head_cols], grad_two[:, head_cols:]
    grad_query, grad_key = grad_pair[:, :head_cols], grad_pair[:, head_cols:]
    grad_router = small[:experts].T
    four = lax.dynamic_slice_in_dim(small[experts:], lane_index * head_cols, head_cols, 1)
    return (
        block_out,
        grad_tokens,
        four[0],
        grad_query.astype(F32),
        grad_key.astype(F32),
        grad_value.astype(F32),
        four[2],
        four[3],
        grad_out.astype(F32),
        four[1],
        grad_router,
        grad_gate,
        grad_up,
        grad_down,
    )


def solution(mesh):
    wide, narrow = mesh.shape["wide"], mesh.shape["narrow"]
    near = 2
    middle = min(wide // near, 4)
    inner = Mesh(mesh.devices.reshape(wide // (near * middle), middle, near, narrow // 2, 2), ALL)
    both = P(WIDE, NARROW)
    cube = P(WIDE, None, NARROW)
    lane = P(NARROW)
    row = P(WIDE, None)
    return jax.shard_map(
        per_device,
        mesh=inner,
        in_specs=(
            both, both, row, row, lane, both, both, both, lane, lane, both, lane, P(),
            cube, cube, cube,
        ),
        out_specs=(
            both, both, lane, both, both, both, lane, lane, both, lane, P(), cube, cube, cube,
        ),
        check_vma=False,
    )
```

time: 1210 us -> 910 us (0.75)
  waiting for transfers between devices: 598 us -> 387 us
  Pallas kernels: 0 us -> 191 us
  matrix products: 180 us -> 9.19 us
  local copies, waits for them, and re-layouts: 168 us -> 102 us
  starting transfers between devices: 124 us -> 86.1 us
    pallas_call x0 -> x15, Pallas kernels: none -> 191 us  [the longest x13 179 us: call(): pl.pallas_call(body, out_shape=outs, in_specs=[pl.BlockSpec(memory_space=...]
    ppermute x48 -> x32, waiting for transfers between devices: 415 us -> 277 us  [swap(): return lax.ppermute(values, axis, [(i, i ^ step) for i in range(count)])]
    all_gather x2 -> x3, waiting for transfers between devices: 163 us -> 38.2 us  [the longest x1 28.9 us: per_device(): lax.all_gather(jnp.concatenate([w_query, w_key, w_value, w_out], axis=1),...]
    dot_general x12 -> x3, matrix products: 112 us -> 8.94 us  [dot(): lax.dot_general(a, b, (contract, ((), ())), preferred_element_type=F32)]
    dot_general x13 -> x0, matrix products: 67 us -> none  [the longest x1 19.7 us: per_device(): down_grad = jnp.dot(cot_all, down_own, preferred_element_type=F32)]
    all_to_all x10 -> x7, waiting for transfers between devices: 4.87 us -> 64.2 us  [the longest x3 64.2 us: to_group(): got = lax.all_to_all(weight, GROUP, 0, 0, tiled=True)]
    another operation x5 -> x0, other arithmetic: 29.7 us -> none
    another operation x8, local copies, waits for them, and re-layouts: 26.5 us -> 4.59 us  [the longest x4 2.78 us: per_device(): jnp.stack([(residual + moe_sum.astype(F32)).astype(BF), grad_rows])]
  transfers between devices with their start and end apart: 64 -> 45, of which waited for: 34 -> 25; matrix products, arithmetic and copies ran while one was open for 25% -> 14% of each run, Pallas kernels for 0% -> 16%
where the time goes in v2:
time: 910 us; the launch traced here: 901 us
  waiting for transfers between devices  387 us (43%)
  Pallas kernels  191 us (21%)
  local copies, waits for them, and re-layouts  102 us (11%)
  starting transfers between devices  86.1 us (9%)
  other arithmetic  74 us (8%)
  blocking collectives  37.1 us (4%)
  between operations  15.5 us (2%)
  matrix products  9.19 us (1%)
    ppermute x32, waiting for transfers between devices, swap(): return lax.ppermute(values, axis, [(i, i ^ step) for i in range(count)])  277 us
    pallas_call x13, Pallas kernels, call(): pl.pallas_call(body, out_shape=outs, in_specs=[pl.BlockSpec(memory_space=...  179 us
    unnamed x179, local copies, waits for them, and re-layouts  64.5 us
    all_to_all x3, waiting for transfers between devices, to_group(): got = lax.all_to_all(weight, GROUP, 0, 0, tiled=True)  64.2 us
    ppermute x32, starting transfers between devices, swap(): return lax.ppermute(values, axis, [(i, i ^ step) for i in range(count)])  32.2 us
    all_gather x1, waiting for transfers between devices, per_device(): lax.all_gather(jnp.concatenate([w_query, w_key, w_value, w_out], axis=1),...  28.9 us
    all_to_all x3, starting transfers between devices, to_group(): got = lax.all_to_all(weight, GROUP, 0, 0, tiled=True)  28 us
  transfers between devices with their start and end apart: 45, of which 25 were waited for; matrix products, arithmetic and copies ran while one was open for 14% of the time, Pallas kernels for 16%

profile of v2, /device:TPU:0, one launch (start us, length us, event | category | flops | bytes accessed | tf_op | source)
XLA Modules:
  0.0 901.2 jit_solution(3912229255144529268)
XLA Ops:
  30.1 13.9 %collective-permute-done.1 = bf16[512,512]{1,0:T(8,128)(2,1)} collective-permute-done((bf16[512,512]{1,0:T(8,128)(2,1)S(1)}, bf16[512,512]{1,0:T(8,128)(2,1)}, u32[]{:S(2)}, u32[]{:S(2)}) %collective-permute-start.1) | collective-permute-done | bytes 524320 | tf_op jit(solution)/shard_map/ppermute | solution.py:735
  69.6 27.9 %all-to-all-done.1 = bf16[16,256,256]{2,1,0:T(8,128)(2,1)S(1)} async-done(((bf16[16,256,256]{2,1,0:T(8,128)(2,1)}), bf16[16,256,256]{2,1,0:T(8,128)(2,1)S(1)}, u32[]{:S(2)}, u32[]{:S(2)}) %all-to-all-start.1) | async-done | bytes 2097184 | tf_op jit(solution)/shard_map/all_to_all | solution.py:782
  100.2 44.9 %collective-permute-done.3.refs_3_.refs_2_ = bf16[8,2,256,256]{3,2,1,0:T(8,128)(2,1)S(1)} collective-permute-done((bf16[8,2,256,256]{3,2,1,0:T(8,128)(2,1)S(1)}, bf16[8,2,256,256]{3,2,1,0:T(8,128)(2,1)S(1)}, u32[]{:S(2)}, u32[]{:S(2)}) %collective-permute-start.3) | collective-permute-done | bytes 2097184 | tf_op jit(solution)/shard_map/ppermute | solution.py:735
  146.5 28.9 %all-gather.4.cloned.1.call-done.weights.refs_8_.refs_1_ = bf16[2048,2048]{1,0:T(8,128)(2,1)} async-done(((bf16[256,2048]{1,0:T(8,128)(2,1)}), bf16[2048,2048]{1,0:T(8,128)(2,1)}) %all-gather.4.cloned.1.call-update) | async-done | bytes 8388624 | tf_op jit(solution)/shard_map/all_gather | solution.py:843
  200.7 36.3 %all-to-all-done.2 = bf16[16,256,256]{2,1,0:T(8,128)(2,1)S(1)} async-done(((bf16[16,256,256]{2,1,0:T(8,128)(2,1)}), bf16[16,256,256]{2,1,0:T(8,128)(2,1)S(1)}, u32[]{:S(2)}, u32[]{:S(2)}) %all-to-all-start.2) | async-done | bytes 2097184 | tf_op jit(solution)/shard_map/all_to_all | solution.py:782
  237.0 17.6 %all-to-all-start.3 = ((bf16[16,256,256]{2,1,0:T(8,128)(2,1)}), bf16[16,256,256]{2,1,0:T(8,128)(2,1)}, u32[]{:S(2)}, u32[]{:S(2)}) async-start(bf16[16,256,256]{2,1,0:T(8,128)(2,1)} %get-tuple-element.145), calls=%async_computation.3 | async-start | bytes 4194304 | tf_op jit(solution)/shard_map/all_to_all | solution.py:782
  261.6 9.1 %shard_map.264 = (bf16[512,512]{1,0:T(8,128)(2,1)S(1)}, bf16[512,512]{1,0:T(8,128)(2,1)S(1)}, bf16[512,512]{1,0:T(8,128)(2,1)S(1)}, f32[4,512]{1,0:T(4,128)S(1)}, bf16[512,2048]{1,0:T(8,128)(2,1)S(1)}) custom-call(f32[512,512]{1,0:T(8,128)S(1)} %get-tuple-element.134.refs_0_.refs_10_.refs_2_, f32[512,512]{1,0:T(8,128)S(1)} %copy-done.27, ...), custom_call_target="tpu_custom_call" | custom-call | flops 1000 | bytes 1000 | tf_op jit(solution)/shard_map/pallas_call | solution.py:43
  278.7 20.3 %collective-permute-done.5 = bf16[4,2,256,256]{3,2,1,0:T(8,128)(2,1)} collective-permute-done((bf16[4,2,256,256]{3,2,1,0:T(8,128)(2,1)}, bf16[4,2,256,256]{3,2,1,0:T(8,128)(2,1)}, u32[]{:S(2)}, u32[]{:S(2)}) %collective-permute-start.5) | collective-permute-done | bytes 1048608 | tf_op jit(solution)/shard_map/ppermute | solution.py:735
  300.3 12.3 %collective-permute-done.6 = bf16[128,2048]{1,0:T(8,128)(2,1)} collective-permute-done((bf16[128,2048]{1,0:T(8,128)(2,1)}, bf16[128,2048]{1,0:T(8,128)(2,1)}, u32[]{:S(2)}, u32[]{:S(2)}) %collective-permute-start.6) | collective-permute-done | bytes 524320 | tf_op jit(solution)/shard_map/ppermute | solution.py:735
  321.2 17.6 %all_to_all.49 = f32[16,1,128]{2,1,0:T(1,128)S(1)} all-to-all(f32[16,1,128]{2,1,0:T(1,128)S(1)} %copy.78), channel_id=1, replica_groups=mesh['t'=1,'g'=4,'p'=2,'y'=2,'c'=2] {'g','p','c'}, dimensions={0} | all-to-all | bytes 16384 | tf_op jit(solution)/shard_map/all_to_all | solution.py:773
  344.9 13.2 %shard_map.265.refs_6_ = bf16[2048,1024]{1,0:T(8,128)(2,1)S(1)} custom-call(bf16[1024,2048]{1,0:T(8,128)(2,1)S(1)} %copy-done.23, bf16[1024,2048]{1,0:T(8,128)(2,1)} %collective-permute-done.7.refs_1_, bf16[8,2,256,256]{3,2,1,0:T(8,128)(2,1)S(1)} %bitcast.107, bf16[8,2,256,256]{3,2,1,0:T(8,128)(2,1)S(1)} %copy-done.19), custom_call_target="tpu_custom_call" | custom-call | flops 1000 | bytes 1000 | tf_op jit(solution)/shard_map/pallas_call | solution.py:43
  360.1 27.2 %collective-permute-done.9 = bf16[4,2,256,256]{3,2,1,0:T(8,128)(2,1)S(1)} collective-permute-done((bf16[4,2,256,256]{3,2,1,0:T(8,128)(2,1)}, bf16[4,2,256,256]{3,2,1,0:T(8,128)(2,1)S(1)}, u32[]{:S(2)}, u32[]{:S(2)}) %collective-permute-start.9) | collective-permute-done | bytes 1048608 | tf_op jit(solution)/shard_map/ppermute | solution.py:735
  387.2 9.3 %all-gather.8.cloned.1.call-done.refs_0_ = bf16[1024,2048]{1,0:T(8,128)(2,1)} async-done(((bf16[128,2048]{1,0:T(8,128)(2,1)}), bf16[1024,2048]{1,0:T(8,128)(2,1)}) %all-gather.8.cloned.1.call-update) | async-done | bytes 4194320 | tf_op jit(solution)/shard_map/all_gather | solution.py:894
  404.0 31.7 %shard_map.266 = (bf16[2048,1024]{1,0:T(8,128)(2,1)}, bf16[2048,1024]{1,0:T(8,128)(2,1)}, bf16[2048,1024]{1,0:T(8,128)(2,1)}, f32[16,128]{1,0:T(8,128)}) custom-call(bf16[1024,2048]{1,0:T(8,128)(2,1)} %all-gather.8.cloned.1.call-done.refs_0_, bf16[1024,2048]{1,0:T(8,128)(2,1)} %collective-permute-done.10.refs_1_, bf16[8,2,256,256]{3,2,1,0:T(8,128)(2,1)} %bitcast.103, ...), custom_call_target="tpu_custom_call" | custom-call | flops 1000 | bytes 1000 | tf_op jit(solution)/shard_map/pallas_call | solution.py:43
  440.2 15.5 %shard_map.267 = bf16[1024,2176]{1,0:T(8,128)(2,1)} custom-call(bf16[2048,1024]{1,0:T(8,128)(2,1)S(1)} %copy-done.8, bf16[8,2,256,256]{3,2,1,0:T(8,128)(2,1)S(1)} %bitcast.104, bf16[8,2,256,256]{3,2,1,0:T(8,128)(2,1)S(1)} %copy-done.15, bf16[2048,1024]{1,0:T(8,128)(2,1)} %get-tuple-element.174.refs_3_.refs_2_, bf16[8,2,256,256]{3,2,1,0:T(8,128)(2,1)} %bitcast.14.refs_4_, ...), custom_call_target="tpu_custom_call" | custom-call | flops 1000 | bytes 1000 | tf_op jit(solution)/shard_map/pallas_call | solution.py:43
  455.9 15.5 %shard_map.268 = bf16[1024,2176]{1,0:T(8,128)(2,1)} custom-call(bf16[2048,1024]{1,0:T(8,128)(2,1)S(1)} %copy-done.8, bf16[8,2,256,256]{3,2,1,0:T(8,128)(2,1)S(1)} %bitcast.105, bf16[8,2,256,256]{3,2,1,0:T(8,128)(2,1)S(1)} %copy-done.15, bf16[2048,1024]{1,0:T(8,128)(2,1)} %get-tuple-element.174.refs_3_.refs_2_, bf16[8,2,256,256]{3,2,1,0:T(8,128)(2,1)} %bitcast.14.refs_4_, ...), custom_call_target="tpu_custom_call" | custom-call | flops 1000 | bytes 1000 | tf_op jit(solution)/shard_map/pallas_call | solution.py:43
  479.0 15.2 %shard_map.269 = (bf16[8,2,256,256]{3,2,1,0:T(8,128)(2,1)S(1)}, bf16[8,2,256,256]{3,2,1,0:T(8,128)(2,1)S(1)}) custom-call(bf16[1024,2048]{1,0:T(8,128)(2,1)S(1)} %copy-done.24, bf16[1024,2048]{1,0:T(8,128)(2,1)} %collective-permute-done.7.refs_1_, bf16[2048,1024]{1,0:T(8,128)(2,1)} %get-tuple-element.176.refs_2_.refs_0_), custom_call_target="tpu_custom_call" | custom-call | flops 1000 | bytes 1000 | tf_op jit(solution)/shard_map/pallas_call | solution.py:43
  495.5 9.0 %shard_map.273 = bf16[1024,2048]{1,0:T(8,128)(2,1)S(1)} custom-call(bf16[2048,1024]{1,0:T(8,128)(2,1)S(1)} %copy-done.7, bf16[8,2,256,256]{3,2,1,0:T(8,128)(2,1)S(1)} %bitcast.108, bf16[8,2,256,256]{3,2,1,0:T(8,128)(2,1)S(1)} %copy-done.20), custom_call_target="tpu_custom_call" | custom-call | flops 1000 | bytes 1000 | tf_op jit(solution)/shard_map/pallas_call | solution.py:43
  506.5 10.0 %shard_map.272 = bf16[1024,2048]{1,0:T(8,128)(2,1)} custom-call(bf16[2048,1024]{1,0:T(8,128)(2,1)S(1)} %copy-done.7, bf16[8,2,256,256]{3,2,1,0:T(8,128)(2,1)S(1)} %bitcast.109, bf16[8,2,256,256]{3,2,1,0:T(8,128)(2,1)S(1)} %copy-done.21), custom_call_target="tpu_custom_call" | custom-call | flops 1000 | bytes 1000 | tf_op jit(solution)/shard_map/pallas_call | solution.py:43
  516.5 15.4 %shard_map.271 = (bf16[8,2,256,256]{3,2,1,0:T(8,128)(2,1)S(1)}, bf16[8,2,256,256]{3,2,1,0:T(8,128)(2,1)}) custom-call(bf16[1024,2048]{1,0:T(8,128)(2,1)S(1)} %copy-done.6, bf16[1024,2048]{1,0:T(8,128)(2,1)} %collective-permute-done.10.refs_1_, bf16[2048,1024]{1,0:T(8,128)(2,1)} %get-tuple-element.174.refs_3_.refs_2_), custom_call_target="tpu_custom_call" | custom-call | flops 1000 | bytes 1000 | tf_op jit(solution)/shard_map/pallas_call | solution.py:43
  533.3 24.3 %shard_map.270 = (bf16[8,2,256,256]{3,2,1,0:T(8,128)(2,1)S(1)}, bf16[8,2,256,256]{3,2,1,0:T(8,128)(2,1)S(1)}) custom-call(bf16[1024,2048]{1,0:T(8,128)(2,1)S(1)} %copy-done.6, bf16[1024,2048]{1,0:T(8,128)(2,1)} %collective-permute-done.10.refs_1_, bf16[2048,1024]{1,0:T(8,128)(2,1)} %get-tuple-element.172.refs_0_.refs_2_), custom_call_target="tpu_custom_call" | custom-call | flops 1000 | bytes 1000 | tf_op jit(solution)/shard_map/pallas_call | solution.py:43
  566.8 7.8 add_convert_fusion.1
  574.6 31.2 %collective-permute-done.14 = bf16[8,2,256,256]{3,2,1,0:T(8,128)(2,1)} collective-permute-done((bf16[8,2,256,256]{3,2,1,0:T(8,128)(2,1)S(1)}, bf16[8,2,256,256]{3,2,1,0:T(8,128)(2,1)}, u32[]{:S(2)}, u32[]{:S(2)}) %collective-permute-start.14) | collective-permute-done | bytes 2097184 | tf_op jit(solution)/shard_map/ppermute | solution.py:735
  614.5 12.7 %collective-permute-done.16 = bf16[128,2048]{1,0:T(8,128)(2,1)} collective-permute-done((bf16[128,2048]{1,0:T(8,128)(2,1)}, bf16[128,2048]{1,0:T(8,128)(2,1)}, u32[]{:S(2)}, u32[]{:S(2)}) %collective-permute-start.16) | collective-permute-done | bytes 524320 | tf_op jit(solution)/shard_map/ppermute | solution.py:735
  644.5 13.0 %shard_map.274 = (f32[512,512]{1,0:T(8,128)S(1)}, f32[512,512]{1,0:T(8,128)S(1)}, bf16[512,512]{1,0:T(8,128)(2,1)S(1)}, f32[2,512]{1,0:T(2,128)S(1)}) custom-call(bf16[512,2048]{1,0:T(8,128)(2,1)S(1)} %copy-done.17, bf16[2048,2048]{1,0:T(8,128)(2,1)} %all-gather.4.cloned.1.call-done.weights.refs_8_.refs_1_, bf16[512,512]{1,0:T(8,128)(2,1)S(1)} %copy-done.50, ...), custom_call_target="tpu_custom_call" | custom-call | flops 1000 | bytes 1000 | tf_op jit(solution)/shard_map/pallas_call | solution.py:43
  699.5 31.0 %collective-permute-done.20 = bf16[8,2,256,256]{3,2,1,0:T(8,128)(2,1)} collective-permute-done((bf16[8,2,256,256]{3,2,1,0:T(8,128)(2,1)}, bf16[8,2,256,256]{3,2,1,0:T(8,128)(2,1)}, u32[]{:S(2)}, u32[]{:S(2)}) %collective-permute-start.20) | collective-permute-done | bytes 2097184 | tf_op jit(solution)/shard_map/ppermute | solution.py:735
  730.5 8.8 collective-permute-done.19
  742.9 8.7 all-to-all-start.7
  759.8 7.8 collective-permute-done.21
  777.9 23.3 %collective-permute-done.23 = bf16[4,256,1024]{2,1,0:T(8,128)(2,1)} collective-permute-done((bf16[4,256,1024]{2,1,0:T(8,128)(2,1)}, bf16[4,256,1024]{2,1,0:T(8,128)(2,1)}, u32[]{:S(2)}, u32[]{:S(2)}) %collective-permute-start.23) | collective-permute-done | bytes 2097184 | tf_op jit(solution)/shard_map/ppermute | solution.py:735
  801.1 9.7 %collective-permute-done.22 = bf16[2,256,1024]{2,1,0:T(8,128)(2,1)} collective-permute-done((bf16[2,256,1024]{2,1,0:T(8,128)(2,1)}, bf16[2,256,1024]{2,1,0:T(8,128)(2,1)}, u32[]{:S(2)}, u32[]{:S(2)}) %collective-permute-start.22) | collective-permute-done | bytes 1048608 | tf_op jit(solution)/shard_map/ppermute | solution.py:735
  835.0 14.5 %collective-permute-done.27 = bf16[256,1024]{1,0:T(8,128)(2,1)} collective-permute-done((bf16[256,1024]{1,0:T(8,128)(2,1)}, bf16[256,1024]{1,0:T(8,128)(2,1)}, u32[]{:S(2)}, u32[]{:S(2)}) %collective-permute-start.27) | collective-permute-done | bytes 524320 | tf_op jit(solution)/shard_map/ppermute | solution.py:735
  (366 shorter events, 302.4 us)
Async XLA Ops:
  7.2 168.2 %all-gather.4.cloned.1.call-start = ((), (), s32[]{:S(2)}) async-start(), calls=%async_computation.11 | async-start | bytes 9437184 | tf_op jit(solution)/shard_map/all_gather | solution.py:843
  22.8 74.7 %all-to-all-start.1 = ((bf16[16,256,256]{2,1,0:T(8,128)(2,1)}), bf16[16,256,256]{2,1,0:T(8,128)(2,1)S(1)}, u32[]{:S(2)}, u32[]{:S(2)}) async-start(bf16[16,256,256]{2,1,0:T(8,128)(2,1)} %bitcast.117), calls=%async_computation.1 | async-start | bytes 4194304 | tf_op jit(solution)/shard_map/all_to_all | solution.py:782
  29.5 14.4 %collective-permute-start.1 = (bf16[512,512]{1,0:T(8,128)(2,1)S(1)}, bf16[512,512]{1,0:T(8,128)(2,1)}, u32[]{:S(2)}, u32[]{:S(2)}) collective-permute-start(bf16[512,512]{1,0:T(8,128)(2,1)S(1)} %copy-done.77), channel_id=1, source_target_pairs={{0,2},{2,0},{1,3},{3,1},{4,6},{6,4},{5,7},{7,5},{8,10},{10,8},{9,1... | collective-permute-start | bytes 1572872 | tf_op jit(solution)/shard_map/ppermute | solution.py:735
  30.0 28.2 %collective-permute-start = (bf16[512,512]{1,0:T(8,128)(2,1)S(1)}, bf16[512,512]{1,0:T(8,128)(2,1)}, u32[]{:S(2)}, u32[]{:S(2)}) collective-permute-start(bf16[512,512]{1,0:T(8,128)(2,1)S(1)} %copy-done.77), channel_id=1, source_target_pairs={{0,1},{1,0},{2,3},{3,2},{4,5},{5,4},{6,7},{7,6},{8,9},{9,8},{10,11... | collective-permute-start | bytes 1572872 | tf_op jit(solution)/shard_map/ppermute | solution.py:735
  44.0 18.1 %collective-permute-start.2 = (bf16[512,512]{1,0:T(8,128)(2,1)}, bf16[512,512]{1,0:T(8,128)(2,1)}, u32[]{:S(2)}, u32[]{:S(2)}) collective-permute-start(bf16[512,512]{1,0:T(8,128)(2,1)} %collective-permute-done.1), channel_id=1, source_target_pairs={{0,1},{1,0},{2,3},{3,2},{4,5},{5,4},{6,7},{7,6},{8,9},{9,8},{10,11... | collective-permute-start | bytes 1572872 | tf_op jit(solution)/shard_map/ppermute | solution.py:735
  97.5 47.6 %collective-permute-start.3 = (bf16[8,2,256,256]{3,2,1,0:T(8,128)(2,1)S(1)}, bf16[8,2,256,256]{3,2,1,0:T(8,128)(2,1)S(1)}, u32[]{:S(2)}, u32[]{:S(2)}) collective-permute-start(bf16[8,2,256,256]{3,2,1,0:T(8,128)(2,1)S(1)} %bitcast.106), channel_id=1, source_target_pairs={{0,2},{2,0},{1,3},{3,1},{4,6},{6,4},{5,7},{7,5},{8,10},{10,8},{9,1... | collective-permute-start | bytes 6291464 | tf_op jit(solution)/shard_map/ppermute | solution.py:735
  175.4 61.6 %all-to-all-start.2 = ((bf16[16,256,256]{2,1,0:T(8,128)(2,1)}), bf16[16,256,256]{2,1,0:T(8,128)(2,1)S(1)}, u32[]{:S(2)}, u32[]{:S(2)}) async-start(bf16[16,256,256]{2,1,0:T(8,128)(2,1)} %get-tuple-element.138), calls=%async_computation.2 | async-start | bytes 4194304 | tf_op jit(solution)/shard_map/all_to_all | solution.py:782
  179.1 137.2 %all-gather.6.cloned.1.call-start = ((), (), s32[]{:S(2)}) async-start(), calls=%async_computation.12 | async-start | bytes 4718592 | tf_op jit(solution)/shard_map/all_gather | solution.py:869
  237.0 79.3 %all-to-all-start.3 = ((bf16[16,256,256]{2,1,0:T(8,128)(2,1)}), bf16[16,256,256]{2,1,0:T(8,128)(2,1)}, u32[]{:S(2)}, u32[]{:S(2)}) async-start(bf16[16,256,256]{2,1,0:T(8,128)(2,1)} %get-tuple-element.145), calls=%async_computation.3 | async-start | bytes 4194304 | tf_op jit(solution)/shard_map/all_to_all | solution.py:782
  254.7 141.9 %all-gather.8.cloned.1.call-start = ((), (), s32[]{:S(2)}) async-start(), calls=%async_computation.13 | async-start | bytes 4718592 | tf_op jit(solution)/shard_map/all_gather | solution.py:894
  273.4 25.7 %collective-permute-start.5 = (bf16[4,2,256,256]{3,2,1,0:T(8,128)(2,1)}, bf16[4,2,256,256]{3,2,1,0:T(8,128)(2,1)}, u32[]{:S(2)}, u32[]{:S(2)}) collective-permute-start(bf16[4,2,256,256]{3,2,1,0:T(8,128)(2,1)} %slice.92), channel_id=1, source_target_pairs={{0,2},{2,0},{1,3},{3,1},{4,6},{6,4},{5,7},{7,5},{8,10},{10,8},{9,1... | collective-permute-start | bytes 3145736 | tf_op jit(solution)/shard_map/ppermute | solution.py:735
  316.4 289.5 %reduce-scatter.3.cloned.1.call-start = ((), (), s32[]{:S(2)}) async-start(), calls=%async_computation.14 | async-start | bytes 5013504 | tf_op jit(solution)/shard_map/reduce_scatter | solution.py:929
  316.4 23.0 %collective-permute-start.7 = (bf16[1024,2048]{1,0:T(8,128)(2,1)}, bf16[1024,2048]{1,0:T(8,128)(2,1)}, u32[]{:S(2)}, u32[]{:S(2)}) collective-permute-start(bf16[1024,2048]{1,0:T(8,128)(2,1)} %all-gather.6.cloned.1.call-done.refs_0_), channel_id=1, source_target_pairs={{0,1},{1,0},{2,3},{3,2},{4,5},{5,4},{6,7},{7,6},{8,9},{9,8},{10,11... | collective-permute-start | bytes 12582920 | tf_op jit(solution)/shard_map/ppermute | solution.py:735
  316.6 70.7 %collective-permute-start.8 = (bf16[8,2,256,256]{3,2,1,0:T(8,128)(2,1)}, bf16[8,2,256,256]{3,2,1,0:T(8,128)(2,1)}, u32[]{:S(2)}, u32[]{:S(2)}) collective-permute-start(bf16[8,2,256,256]{3,2,1,0:T(8,128)(2,1)} %bitcast.14.refs_4_), channel_id=1, source_target_pairs={{0,2},{2,0},{1,3},{3,1},{4,6},{6,4},{5,7},{7,5},{8,10},{10,8},{9,1... | collective-permute-start | bytes 6291464 | tf_op jit(solution)/shard_map/ppermute | solution.py:735
  319.1 68.1 %collective-permute-start.9 = (bf16[4,2,256,256]{3,2,1,0:T(8,128)(2,1)}, bf16[4,2,256,256]{3,2,1,0:T(8,128)(2,1)S(1)}, u32[]{:S(2)}, u32[]{:S(2)}) collective-permute-start(bf16[4,2,256,256]{3,2,1,0:T(8,128)(2,1)} %slice.94), channel_id=1, source_target_pairs={{0,2},{2,0},{1,3},{3,1},{4,6},{6,4},{5,7},{7,5},{8,10},{10,8},{9,1... | collective-permute-start | bytes 3145736 | tf_op jit(solution)/shard_map/ppermute | solution.py:735
  455.7 15.7 %collective-permute-start.11 = (bf16[1024,2176]{1,0:T(8,128)(2,1)}, bf16[1024,2176]{1,0:T(8,128)(2,1)S(1)}, u32[]{:S(2)}, u32[]{:S(2)}) collective-permute-start(bf16[1024,2176]{1,0:T(8,128)(2,1)} %shard_map.267), channel_id=1, source_target_pairs={{0,1},{1,0},{2,3},{3,2},{4,5},{5,4},{6,7},{7,6},{8,9},{9,8},{10,11... | collective-permute-start | bytes 13369352 | tf_op jit(solution)/shard_map/ppermute | solution.py:735
  494.3 63.3 %collective-permute-start.12 = (bf16[8,2,256,256]{3,2,1,0:T(8,128)(2,1)S(1)}, bf16[8,2,256,256]{3,2,1,0:T(8,128)(2,1)}, u32[]{:S(2)}, u32[]{:S(2)}) collective-permute-start(bf16[8,2,256,256]{3,2,1,0:T(8,128)(2,1)S(1)} %get-tuple-element.171), channel_id=1, source_target_pairs={{0,2},{2,0},{1,3},{3,1},{4,6},{6,4},{5,7},{7,5},{8,10},{10,8},{9,1... | collective-permute-start | bytes 6291464 | tf_op jit(solution)/shard_map/ppermute | solution.py:735
  557.9 47.9 %collective-permute-start.14 = (bf16[8,2,256,256]{3,2,1,0:T(8,128)(2,1)S(1)}, bf16[8,2,256,256]{3,2,1,0:T(8,128)(2,1)}, u32[]{:S(2)}, u32[]{:S(2)}) collective-permute-start(bf16[8,2,256,256]{3,2,1,0:T(8,128)(2,1)S(1)} %get-tuple-element.179), channel_id=1, source_target_pairs={{0,2},{2,0},{1,3},{3,1},{4,6},{6,4},{5,7},{7,5},{8,10},{10,8},{9,1... | collective-permute-start | bytes 6291464 | tf_op jit(solution)/shard_map/ppermute | solution.py:735
  562.3 70.3 %all-to-all-start.5 = ((bf16[16,256,256]{2,1,0:T(8,128)(2,1)}), bf16[16,256,256]{2,1,0:T(8,128)(2,1)}, u32[]{:S(2)}, u32[]{:S(2)}) async-start(bf16[16,256,256]{2,1,0:T(8,128)(2,1)} %bitcast.116), calls=%async_computation.6 | async-start | bytes 4194304 | tf_op jit(solution)/shard_map/all_to_all | solution.py:811
  566.8 244.1 %reduce-scatter.5.cloned.1.call-start = ((), (), s32[]{:S(2)}) async-start(), calls=%async_computation.15 | async-start | bytes 4718592 | tf_op jit(solution)/shard_map/reduce_scatter | solution.py:947
  614.5 17.0 %collective-permute-start.15 = (bf16[128,2048]{1,0:T(8,128)(2,1)}, bf16[128,2048]{1,0:T(8,128)(2,1)}, u32[]{:S(2)}, u32[]{:S(2)}) collective-permute-start(bf16[128,2048]{1,0:T(8,128)(2,1)} %get-tuple-element.267), channel_id=1, source_target_pairs={{0,1},{1,0},{2,3},{3,2},{4,5},{5,4},{6,7},{7,6},{8,9},{9,8},{10,11... | collective-permute-start | bytes 1572872 | tf_op jit(solution)/shard_map/ppermute | solution.py:735
  632.6 106.7 %all-to-all-start.6 = ((bf16[16,256,256]{2,1,0:T(8,128)(2,1)}), bf16[16,256,256]{2,1,0:T(8,128)(2,1)}, u32[]{:S(2)}, u32[]{:S(2)}) async-start(bf16[16,256,256]{2,1,0:T(8,128)(2,1)} %bitcast.115), calls=%async_computation.7 | async-start | bytes 4194304 | tf_op jit(solution)/shard_map/all_to_all | solution.py:811
  683.7 46.8 %collective-permute-start.20 = (bf16[8,2,256,256]{3,2,1,0:T(8,128)(2,1)}, bf16[8,2,256,256]{3,2,1,0:T(8,128)(2,1)}, u32[]{:S(2)}, u32[]{:S(2)}) collective-permute-start(bf16[8,2,256,256]{3,2,1,0:T(8,128)(2,1)} %get-tuple-element.204), channel_id=1, source_target_pairs={{0,2},{2,0},{1,3},{3,1},{4,6},{6,4},{5,7},{7,5},{8,10},{10,8},{9,1... | collective-permute-start | bytes 6291464 | tf_op jit(solution)/shard_map/ppermute | solution.py:735
  684.8 54.5 %collective-permute-start.19 = (bf16[4,256,1024]{2,1,0:T(8,128)(2,1)}, bf16[4,256,1024]{2,1,0:T(8,128)(2,1)}, u32[]{:S(2)}, u32[]{:S(2)}) collective-permute-start(bf16[4,256,1024]{2,1,0:T(8,128)(2,1)} %bitcast.22), channel_id=1, source_target_pairs={{0,4},{4,0},{1,5},{5,1},{2,6},{6,2},{3,7},{7,3},{8,12},{12,8},{9,1... | collective-permute-start | bytes 6291464 | tf_op jit(solution)/shard_map/ppermute | solution.py:735
  694.1 107.0 %collective-permute-start.23 = (bf16[4,256,1024]{2,1,0:T(8,128)(2,1)}, bf16[4,256,1024]{2,1,0:T(8,128)(2,1)}, u32[]{:S(2)}, u32[]{:S(2)}) collective-permute-start(bf16[4,256,1024]{2,1,0:T(8,128)(2,1)} %bitcast.25), channel_id=1, source_target_pairs={{0,4},{4,0},{1,5},{5,1},{2,6},{6,2},{3,7},{7,3},{8,12},{12,8},{9,1... | collective-permute-start | bytes 6291464 | tf_op jit(solution)/shard_map/ppermute | solution.py:735
  742.9 92.1 %all-to-all-start.7 = ((bf16[16,256,256]{2,1,0:T(8,128)(2,1)}), bf16[16,256,256]{2,1,0:T(8,128)(2,1)}, u32[]{:S(2)}, u32[]{:S(2)}) async-start(bf16[16,256,256]{2,1,0:T(8,128)(2,1)} %bitcast.114), calls=%async_computation.9 | async-start | bytes 4194304 | tf_op jit(solution)/shard_map/all_to_all | solution.py:811
  753.1 14.4 %collective-permute-start.21 = (bf16[128,2048]{1,0:T(8,128)(2,1)}, bf16[128,2048]{1,0:T(8,128)(2,1)S(1)}, u32[]{:S(2)}, u32[]{:S(2)}) collective-permute-start(bf16[128,2048]{1,0:T(8,128)(2,1)} %fusion.16), channel_id=1, source_target_pairs={{0,2},{2,0},{1,3},{3,1},{4,6},{6,4},{5,7},{7,5},{8,10},{10,8},{9,1... | collective-permute-start | bytes 1572872 | tf_op jit(solution)/shard_map/ppermute | solution.py:735
  757.8 53.0 %collective-permute-start.22 = (bf16[2,256,1024]{2,1,0:T(8,128)(2,1)}, bf16[2,256,1024]{2,1,0:T(8,128)(2,1)}, u32[]{:S(2)}, u32[]{:S(2)}) collective-permute-start(bf16[2,256,1024]{2,1,0:T(8,128)(2,1)} %slice.167), channel_id=1, source_target_pairs={{0,8},{8,0},{16,24},{24,16},{1,9},{9,1},{17,25},{25,17},{2,10},{10... | collective-permute-start | bytes 3145736 | tf_op jit(solution)/shard_map/ppermute | solution.py:735
  814.8 36.1 %collective-permute-start.26 = (bf16[2,256,1024]{2,1,0:T(8,128)(2,1)}, bf16[2,256,1024]{2,1,0:T(8,128)(2,1)S(1)}, u32[]{:S(2)}, u32[]{:S(2)}) collective-permute-start(bf16[2,256,1024]{2,1,0:T(8,128)(2,1)} %slice.166), channel_id=1, source_target_pairs={{0,8},{8,0},{16,24},{24,16},{1,9},{9,1},{17,25},{25,17},{2,10},{10... | collective-permute-start | bytes 3145736 | tf_op jit(solution)/shard_map/ppermute | solution.py:735
  818.0 31.5 %collective-permute-start.27 = (bf16[256,1024]{1,0:T(8,128)(2,1)}, bf16[256,1024]{1,0:T(8,128)(2,1)}, u32[]{:S(2)}, u32[]{:S(2)}) collective-permute-start(bf16[256,1024]{1,0:T(8,128)(2,1)} %fusion.17), channel_id=1, source_target_pairs={{0,16},{8,24},{16,0},{24,8},{1,17},{9,25},{17,1},{25,9},{2,18},{10... | collective-permute-start | bytes 1572872 | tf_op jit(solution)/shard_map/ppermute | solution.py:735
  854.3 35.6 %collective-permute-start.31 = (bf16[256,1024]{1,0:T(8,128)(2,1)}, bf16[256,1024]{1,0:T(8,128)(2,1)}, u32[]{:S(2)}, u32[]{:S(2)}) collective-permute-start(bf16[256,1024]{1,0:T(8,128)(2,1)} %fusion.18), channel_id=1, source_target_pairs={{0,16},{8,24},{16,0},{24,8},{1,17},{9,25},{17,1},{25,9},{2,18},{10... | collective-permute-start | bytes 1572872 | tf_op jit(solution)/shard_map/ppermute | solution.py:735
  870.0 22.2 %all-to-all-start.8 = ((bf16[4,2,128,512]{3,2,1,0:T(8,128)(2,1)}), bf16[4,2,128,512]{3,2,1,0:T(8,128)(2,1)S(1)}, u32[]{:S(2)}, u32[]{:S(2)}) async-start(bf16[4,2,128,512]{3,2,1,0:T(8,128)(2,1)} %maximum_bitcast_fusion), calls=%async_computation.10 | async-start | bytes 2097152 | tf_op jit(solution)/shard_map/all_to_all | solution.py:1029
  (99 other events, 1319.8 us)
Sparse Core Ops, SparseCore 0:
  10.7 164.6 all-gather.3
  182.7 129.5 all-gather.5
  316.5 79.9 all-gather.7
  477.0 90.1 reduce-scatter.2
  608.1 109.9 reduce-scatter.4

commit v3 on v2

--- a/solution.py
+++ b/solution.py
@@ -16,8 +16,9 @@
 ALL = ("t", "g", "p", "y", "c")
 BF = jnp.bfloat16
 F32 = jnp.float32
-ROWS = 512
+ROWS = 1024
 COLS = 256
+WIDE_COLS = 512
 COST = pl.CostEstimate(flops=1000, transcendentals=0, bytes_accessed=1000)
 
 
@@ -39,11 +40,16 @@
     return lax.dot_general(a, b, (contract, ((), ())), preferred_element_type=F32)
 
 
+def place_of(array):
+    large = array.size * array.dtype.itemsize > 1 << 20
+    return pl.BlockSpec(memory_space=pltpu.HBM if large else pl.ANY)
+
+
 def call(body, outs, scratch, args, flops, vmem, moved):
     return pl.pallas_call(
         body,
         out_shape=outs,
-        in_specs=[pl.BlockSpec(memory_space=pl.ANY)] * len(args),
+        in_specs=[place_of(a) for a in args],
         out_specs=jax.tree.map(lambda _: pl.BlockSpec(memory_space=pl.ANY), outs),
         scratch_shapes=scratch,
         compiler_params=pltpu.CompilerParams(vmem_limit_bytes=vmem << 20),
@@ -62,16 +68,15 @@
         one.wait()
 
 
-def weight_copies(pieces, whole, sems):
-    units = whole.shape[2] // 4
+def weight_copies(pieces, whole, sems, stride=1, at=0):
+    units = pieces[0].shape[3]
     copies = []
     for half, piece in enumerate(pieces):
         for c in range(2):
             k = half * 2 + c
+            there = pl.ds((k * stride + at) * units, units)
             copies.append(
-                pltpu.make_async_copy(
-                    piece.at[:, c], whole.at[:, :, pl.ds(k * units, units)], sems.at[k]
-                )
+                pltpu.make_async_copy(piece.at[:, c], whole.at[:, :, there], sems.at[k])
             )
     return copies
 
@@ -119,14 +124,14 @@
     return jnp.transpose(jnp.broadcast_to(column, (128, 128)))[:1]
 
 
-def take(ref, k):
-    part = ref[:, :, pl.ds(pl.multiple_of(k * COLS, COLS), COLS)]
-    return part.reshape(-1, COLS)
-
-
-def take_rows(ref, n):
-    each = COLS // ref.shape[1]
-    return ref[pl.ds(n * each, each)].reshape(COLS, ref.shape[2])
+def take(ref, k, size=COLS):
+    part = ref[:, :, pl.ds(pl.multiple_of(k * size, size), size)]
+    return part.reshape(-1, size)
+
+
+def take_rows(ref, n, size=COLS):
+    each = size // ref.shape[1]
+    return ref[pl.ds(n * each, each)].reshape(size, ref.shape[2])
 
 
 def project_body(count, *refs):
@@ -143,12 +148,14 @@
         await_rows(rows_v, sem_b, count, r)
 
         def col_step(k, carry):
-            await_weight(weight_v, sem_w, k, r == 0)
-            cols = pl.ds(pl.multiple_of(k * COLS, COLS), COLS)
-            out_v[here, cols] = dot(rows_v[here, :], take(weight_v, k), ((1,), (0,))).astype(BF)
+            for n in range(WIDE_COLS // COLS):
+                await_weight(weight_v, sem_w, k * (WIDE_COLS // COLS) + n, r == 0)
+            cols = pl.ds(pl.multiple_of(k * WIDE_COLS, WIDE_COLS), WIDE_COLS)
+            got = dot(rows_v[here, :], take(weight_v, k, WIDE_COLS), ((1,), (0,)))
+            out_v[here, cols] = got.astype(BF)
             return carry
 
-        lax.fori_loop(0, out_v.shape[1] // COLS, col_step, 0)
+        lax.fori_loop(0, out_v.shape[1] // WIDE_COLS, col_step, 0)
         pltpu.make_async_copy(out_v.at[here], out.at[here], sem_o.at[r]).start()
         return carry
 
@@ -186,17 +193,16 @@
     gate_p, up_p = refs[count : count + 2], refs[count + 2 : count + 4]
     down_grad, own_gate = refs[count + 4 : count + 6]
     gg, ug, hs, dots = refs[count + 6 : count + 10]
-    (rows_v, gate_v, up_v, grad_v, own_v, gg_v, ug_v, hs_v, dots_v, sem_b, sem_w, sem_i, sem_o) = (
-        refs[count + 10 :]
-    )
+    rows_v, pair_v, grad_v, own_v, gg_v, ug_v, hs_v, dots_v = refs[count + 10 : count + 18]
+    own_c, pair_a, pair_b, sem_b, sem_w, sem_i, sem_o = refs[count + 18 :]
     ci = start_all(
         [
             pltpu.make_async_copy(down_grad, grad_v, sem_i.at[0]),
             pltpu.make_async_copy(own_gate, own_v, sem_i.at[1]),
         ]
     )
-    cg = weight_copies(gate_p, gate_v, sem_w.at[0])
-    cu = weight_copies(up_p, up_v, sem_w.at[1])
+    cg = weight_copies(gate_p, pair_v, sem_w.at[0], 2, 0)
+    cu = weight_copies(up_p, pair_v, sem_w.at[1], 2, 1)
     cb = block_copies(blocks, rows_v, sem_b)
     ahead = max(1, count * ROWS // rows_v.shape[0])
     start_all(cb[:ahead] + [c for two in zip(cg, cu) for c in two] + cb[ahead:])
@@ -204,42 +210,78 @@
     steps = rows_v.shape[0] // ROWS
     lines = ROWS // 128
     outs = ((gg_v, gg, 0), (ug_v, ug, 1), (hs_v, hs, 2))
-
-    def row_step(r, carry):
-        here = pl.ds(pl.multiple_of(r * ROWS, ROWS), ROWS)
-        await_rows(rows_v, sem_b, count, r)
-        mine = own_v[pl.ds(pl.multiple_of(r * lines, lines), lines), :]
-        own = jnp.concatenate([to_column(mine[i : i + 1])[:, :1] for i in range(lines)], axis=0)
-
-        def col_step(k, total):
-            await_weight(gate_v, sem_w.at[0], k, r == 0)
-            await_weight(up_v, sem_w.at[1], k, r == 0)
-            cols = pl.ds(pl.multiple_of(k * COLS, COLS), COLS)
-            x = rows_v[here, :]
-            gate = dot(x, take(gate_v, k), ((1,), (0,)))
-            up = dot(x, take(up_v, k), ((1,), (0,)))
-            grad = grad_v[here, cols].astype(F32)
-            sig = 1.0 / (1.0 + jnp.exp(-gate))
-            act = gate * sig
-            hidden = act * up
-            total = total + jnp.sum(hidden * grad, axis=1, keepdims=True)
-            hs_v[here, cols] = (own * hidden).astype(BF)
-            grad = own * grad
-            gg_v[here, cols] = (grad * up * (sig + act * (1.0 - sig))).astype(BF)
-            ug_v[here, cols] = (grad * act).astype(BF)
-            return total
-
-        total = lax.fori_loop(
-            0, gg_v.shape[1] // COLS, col_step, jnp.zeros((ROWS, 1), F32)
+    chunks = gg_v.shape[1] // COLS
+    for i in range(own_v.shape[0]):
+        own_c[i * 128 : (i + 1) * 128, :] = to_column(own_v[i : i + 1, :])
+
+    def ready(i):
+        k = i % chunks
+
+        @pl.when(k == 0)
+        def _():
+            await_rows(rows_v, sem_b, count, i // chunks)
+
+        @pl.when(i < chunks)
+        def _():
+            for n in range(2):
+                there = pl.ds(pl.multiple_of((2 * k + n) * COLS, COLS), COLS)
+                arrived(pair_v.at[:, :, there], sem_w.at[n, k])
+
+    def rows_at(i):
+        return pl.ds(pl.multiple_of((i // chunks) * ROWS, ROWS), ROWS)
+
+    def products(i, pair_s):
+        pair_s[...] = dot(
+            rows_v[rows_at(i), :], take(pair_v, i % chunks, 2 * COLS), ((1,), (0,))
         )
-        dots_v[pl.ds(pl.multiple_of(r * lines, lines), lines), :] = jnp.concatenate(
-            [to_line(total[i * 128 : (i + 1) * 128]) for i in range(lines)], axis=0
-        )
-        for src, dst, i in outs:
-            pltpu.make_async_copy(src.at[here], dst.at[here], sem_o.at[i, r]).start()
-        return carry
-
-    lax.fori_loop(0, steps, row_step, 0)
+
+    def activate(i, pair_s, total):
+        here, k = rows_at(i), i % chunks
+        cols = pl.ds(pl.multiple_of(k * COLS, COLS), COLS)
+        own = own_c[here, :1]
+        gate, up = pair_s[:, :COLS], pair_s[:, COLS:]
+        grad = grad_v[here, cols].astype(F32)
+        sig = 1.0 / (1.0 + jnp.exp(-gate))
+        act = gate * sig
+        hidden = act * up
+        hs_v[here, cols] = (own * hidden).astype(BF)
+        part = jnp.sum(hidden * grad, axis=1, keepdims=True)
+        grad = own * grad
+        gg_v[here, cols] = (grad * up * (sig + act * (1.0 - sig))).astype(BF)
+        ug_v[here, cols] = (grad * act).astype(BF)
+        return jnp.where(k == 0, 0.0, total) + part
+
+    ready(0)
+    products(0, pair_a)
+    most = steps * chunks - 1
+
+    def step(j, total):
+        i = 2 * j
+        ready(i + 1)
+        after_next = jnp.minimum(i + 2, most)
+
+        @pl.when(i + 2 <= most)
+        def _():
+            ready(i + 2)
+
+        products(i + 1, pair_b)
+        total = activate(i, pair_a, total)
+        products(after_next, pair_a)
+        total = activate(i + 1, pair_b, total)
+
+        @pl.when((i + 1) % chunks == chunks - 1)
+        def _():
+            r = i // chunks
+            dots_v[pl.ds(pl.multiple_of(r * lines, lines), lines), :] = jnp.concatenate(
+                [to_line(total[n * 128 : (n + 1) * 128]) for n in range(lines)], axis=0
+            )
+            for src, dst, n in outs:
+                here = rows_at(i)
+                pltpu.make_async_copy(src.at[here], dst.at[here], sem_o.at[n, r]).start()
+
+        return total
+
+    lax.fori_loop(0, steps * chunks // 2, step, jnp.zeros((ROWS, 1), F32))
     last = pltpu.make_async_copy(dots_v, dots, sem_i.at[2])
     last.start()
     for r in range(steps):
@@ -262,14 +304,17 @@
         (out, out, out, wide),
         [
             pltpu.VMEM((rows, model), BF),
-            pltpu.VMEM((w, depth, hidden), BF),
-            pltpu.VMEM((w, depth, hidden), BF),
+            pltpu.VMEM((w, depth, 2 * hidden), BF),
             pltpu.VMEM((rows, hidden), BF),
             pltpu.VMEM(own_gate.shape, F32),
             pltpu.VMEM((rows, hidden), BF),
             pltpu.VMEM((rows, hidden), BF),
             pltpu.VMEM((rows, hidden), BF),
             pltpu.VMEM(own_gate.shape, F32),
+            pltpu.VMEM((rows, 128), F32),
+        ]
+        + [pltpu.VMEM((ROWS, 2 * COLS), F32)] * 2
+        + [
             pltpu.SemaphoreType.DMA((len(blocks),)),
             pltpu.SemaphoreType.DMA((2, 4)),
             pltpu.SemaphoreType.DMA((3,)),
@@ -303,50 +348,46 @@
     grads, weights = scratch[:pairs], scratch[pairs : 2 * pairs]
     out_v, sem_g, sem_w, sem_o = scratch[2 * pairs :]
     rows = out_v.shape[0]
-    steps = rows // ROWS
-    each = COLS // weights[0].shape[1]
+    each = WIDE_COLS // weights[0].shape[1]
     parts = weights[0].shape[0] // each
     for i, (grad, got, other) in enumerate(ins):
-        pltpu.make_async_copy(grad.at[pl.ds(first, ROWS)], grads[i].at[pl.ds(0, ROWS)], sem_g.at[i, 0]).start()
+        pltpu.make_async_copy(grad.at[pl.ds(first, rows)], grads[i], sem_g.at[i]).start()
     for n in range(parts):
         place = pl.ds(n * each, each)
         for i, (grad, got, other) in enumerate(ins):
-            start_all(weight_copies((got.at[place], other.at[place]), weights[i].at[place], sem_w.at[i, n]))
-    for r in range(1, steps):
-        for i, (grad, got, other) in enumerate(ins):
-            here = pl.ds(r * ROWS, ROWS)
-            pltpu.make_async_copy(grad.at[pl.ds(first + r * ROWS, ROWS)], grads[i].at[here], sem_g.at[i, r]).start()
-
-    def row_step(r, carry):
-        here = pl.ds(pl.multiple_of(r * ROWS, ROWS), ROWS)
+            pieces = (got.at[place], other.at[place])
+            start_all(weight_copies(pieces, weights[i].at[place], sem_w.at[i, n]))
+    for i in range(pairs):
+        arrived(grads[i], sem_g.at[i])
+
+    def col_step(n, carry):
         for i in range(pairs):
-            arrived(grads[i].at[here], sem_g.at[i, r])
-
-        def col_step(n, carry):
-            for i in range(pairs):
-                place = weights[i].at[pl.ds(n * each, each)]
-                for k in range(4):
-                    await_weight(place, sem_w.at[i, n], k, r == 0)
-            cols = pl.ds(pl.multiple_of(n * COLS, COLS), COLS)
-            total = dot(grads[0][here, :], take_rows(weights[0], n), ((1,), (1,)))
-            for i in range(1, pairs):
-                total += dot(grads[i][here, :], take_rows(weights[i], n), ((1,), (1,)))
-            out_v[here, cols] = total.astype(BF)
-            return carry
-
-        lax.fori_loop(0, parts, col_step, 0)
-        pltpu.make_async_copy(out_v.at[here], out.at[here], sem_o.at[r]).start()
+            block = weights[i].at[pl.ds(n * each, each)]
+            for k in range(4):
+                await_weight(block, sem_w.at[i, n], k, n >= 0)
+        cols = pl.ds(pl.multiple_of(n * WIDE_COLS, WIDE_COLS), WIDE_COLS)
+        total = dot(grads[0][...], take_rows(weights[0], n, WIDE_COLS), ((1,), (1,)))
+        for i in range(1, pairs):
+            total += dot(grads[i][...], take_rows(weights[i], n, WIDE_COLS), ((1,), (1,)))
+        out_v[:, cols] = total.astype(BF)
+        pltpu.make_async_copy(out_v.at[:, cols], out.at[:, cols], sem_o.at[n]).start()
         return carry
 
     if tail:
         wait_all(side)
+        cols = pl.ds(parts * WIDE_COLS, 128)
         for i in range(rows // 128):
             line = dots_v[first // 128 + i : first // 128 + i + 1, :]
-            out_v[i * 128 : (i + 1) * 128, parts * COLS :] = (to_column(line) * place_v[...]).astype(BF)
-    lax.fori_loop(0, steps, row_step, 0)
-    for r in range(steps):
-        here = pl.ds(r * ROWS, ROWS)
-        pltpu.make_async_copy(out_v.at[here], out.at[here], sem_o.at[r]).wait()
+            value = (to_column(line) * place_v[...]).astype(BF)
+            out_v[i * 128 : (i + 1) * 128, parts * WIDE_COLS :] = value
+        last = pltpu.make_async_copy(out_v.at[:, cols], out.at[:, cols], sem_o.at[parts])
+        last.start()
+    lax.fori_loop(0, parts, col_step, 0)
+    for n in range(parts):
+        cols = pl.ds(n * WIDE_COLS, WIDE_COLS)
+        pltpu.make_async_copy(out_v.at[:, cols], out.at[:, cols], sem_o.at[n]).wait()
+    if tail:
+        last.wait()
 
 
 def back(triples, first, rows, tail=()):
@@ -361,9 +402,9 @@
         + [pltpu.VMEM((w, depth, hidden), BF)] * n
         + [
             pltpu.VMEM((rows, full), BF),
-            pltpu.SemaphoreType.DMA((n, rows // ROWS)),
-            pltpu.SemaphoreType.DMA((n, model // COLS, 4)),
-            pltpu.SemaphoreType.DMA((rows // ROWS,)),
+            pltpu.SemaphoreType.DMA((n,)),
+            pltpu.SemaphoreType.DMA((n, model // WIDE_COLS, 4)),
+            pltpu.SemaphoreType.DMA((model // WIDE_COLS + 1,)),
         ]
         + [pltpu.VMEM(t.shape, F32) for t in tail]
         + [pltpu.SemaphoreType.DMA((2,))] * bool(tail),
@@ -471,7 +512,7 @@
     return pl.pallas_call(
         functools.partial(terms_body, len(pairs)),
         out_shape=(piece, piece),
-        in_specs=[pl.BlockSpec(memory_space=pl.ANY)] * len(flat)
+        in_specs=[place_of(a) for a in flat]
         + [pl.BlockSpec(memory_space=pltpu.SMEM)],
         out_specs=(pl.BlockSpec(memory_space=pl.ANY),) * 2,
         scratch_shapes=[pltpu.VMEM(x.shape, BF) for x in flat]
@@ -940,12 +981,12 @@
     down_theirs, gate_theirs, up_theirs, moe_theirs, moe_mine = stage(
         down_theirs, gate_theirs, up_theirs, moe_theirs, moe_mine
     )
-    gate_theirs = swap(gate_theirs, "y")
+    cut = gate_theirs.shape[0] // 2
+    gate_first = swap(gate_theirs[:cut], "y")
     down_got = to_slices(down_mine, down_theirs)
     moe_sent = add(moe_mine, swap(moe_theirs, "c")).astype(BF)
-    input_sum, moe_sent, gate_theirs = stage(input_sum, moe_sent, gate_theirs)
+    input_sum, moe_sent, gate_first = stage(input_sum, moe_sent, gate_first)
     moe_sum = lax.psum_scatter(moe_sent, ("g", "p"), scatter_dimension=0, tiled=True)
-    gate_got = to_slices(gate_mine, gate_theirs)
     input_sum = input_sum.astype(F32)
     pair_dots = jnp.where(chosen, input_sum[:, model_width : model_width + experts], 0.0)
     input_sum = input_sum[:, :model_width]
@@ -959,8 +1000,9 @@
     residual_norm_grad, ffn_gain_grad = ffn_norm_pull(ffn_grad)
     residual_grad = cot_rows.astype(F32) + residual_norm_grad
     out_cot = gather_four(residual_grad.astype(BF), 0)
-    out_cot, up_theirs, down_got = stage(out_cot, up_theirs, down_got)
-
+    out_cot, up_theirs, down_got, gate_theirs = stage(out_cot, up_theirs, down_got, gate_theirs)
+
+    gate_last = swap(gate_theirs[cut:], "y")
     back_query, back_key, value_grad, dots = unattend(
         out_cot, all_full, query_bf, key_bf, value_bf, log_totals, ids, tables, gains_here,
         raw_query, raw_key,
@@ -969,7 +1011,8 @@
     two_keep, two_near = over_sequences(
         *block_terms(((out_cot, attended), (normed, value_grad)), group_index, depth)
     )
-    dots, two_near, two_keep = stage(dots, two_near, two_keep)
+    dots, two_near, two_keep, gate_last = stage(dots, two_near, two_keep, gate_last)
+    gate_got = to_slices(gate_mine, jnp.concatenate([gate_first, gate_last]))
     two_near = swap(two_near, "p")
     dots = lax.psum(dots, NARROW) / model_width
     dots, up_theirs = stage(dots, up_theirs)

time: 910 us -> 893 us (0.981)
  Pallas kernels: 191 us -> 167 us
    pallas_call x13, Pallas kernels: 179 us -> 156 us  [call(): pl.pallas_call(body, out_shape=outs, in_specs=[place_of(a) for a in args]...]
    ppermute x32 -> x33, waiting for transfers between devices: 277 us -> 272 us  [swap(): return lax.ppermute(values, axis, [(i, i ^ step) for i in range(count)])]
    ppermute x32 -> x33, starting transfers between devices: 32.2 us -> 35 us  [swap(): return lax.ppermute(values, axis, [(i, i ^ step) for i in range(count)])]
    unnamed x179 -> x183, local copies, waits for them, and re-layouts: 64.5 us -> 66.2 us
  transfers between devices with their start and end apart: 45 -> 46, of which waited for: 25 -> 26; matrix products, arithmetic and copies ran while one was open for 14% -> 14% of each run, Pallas kernels for 16% -> 14%
where the time goes in v3:
time: 893 us; the launch traced here: 884 us
  waiting for transfers between devices  386 us (43%)
  Pallas kernels  167 us (19%)
  local copies, waits for them, and re-layouts  106 us (12%)
  starting transfers between devices  91.7 us (10%)
  other arithmetic  73.3 us (8%)
  blocking collectives  36.6 us (4%)
  between operations  15.5 us (2%)
    ppermute x33, waiting for transfers between devices, swap(): return lax.ppermute(values, axis, [(i, i ^ step) for i in range(count)])  272 us
    pallas_call x13, Pallas kernels, call(): pl.pallas_call(body, out_shape=outs, in_specs=[place_of(a) for a in args]...  156 us
    unnamed x183, local copies, waits for them, and re-layouts  66.2 us
    all_to_all x3, waiting for transfers between devices, to_group(): got = lax.all_to_all(weight, GROUP, 0, 0, tiled=True)  64.3 us
    ppermute x33, starting transfers between devices, swap(): return lax.ppermute(values, axis, [(i, i ^ step) for i in range(count)])  35 us
    all_gather x1, waiting for transfers between devices, per_device(): lax.all_gather(jnp.concatenate([w_query, w_key, w_value, w_out], axis=1),...  28.9 us
    all_to_all x3, starting transfers between devices, to_group(): got = lax.all_to_all(weight, GROUP, 0, 0, tiled=True)  28 us
    all_to_all x3, starting transfers between devices, to_slices(): return lax.all_to_all(sent, GROUP, 0, 0, tiled=True)  20.4 us
  transfers between devices with their start and end apart: 46, of which 26 were waited for; matrix products, arithmetic and copies ran while one was open for 14% of the time, Pallas kernels for 14%

profile of v3, /device:TPU:0, one launch (start us, length us, event | category | flops | bytes accessed | tf_op | source)
XLA Modules:
  0.0 883.7 jit_solution(3545766250245837361)
XLA Ops:
  30.1 13.9 %collective-permute-done.1 = bf16[512,512]{1,0:T(8,128)(2,1)} collective-permute-done((bf16[512,512]{1,0:T(8,128)(2,1)S(1)}, bf16[512,512]{1,0:T(8,128)(2,1)}, u32[]{:S(2)}, u32[]{:S(2)}) %collective-permute-start.1) | collective-permute-done | bytes 524320 | tf_op jit(solution)/shard_map/ppermute | solution.py:776
  69.6 27.9 %all-to-all-done.1 = bf16[16,256,256]{2,1,0:T(8,128)(2,1)S(1)} async-done(((bf16[16,256,256]{2,1,0:T(8,128)(2,1)}), bf16[16,256,256]{2,1,0:T(8,128)(2,1)S(1)}, u32[]{:S(2)}, u32[]{:S(2)}) %all-to-all-start.1) | async-done | bytes 2097184 | tf_op jit(solution)/shard_map/all_to_all | solution.py:823
  100.2 44.9 %collective-permute-done.3.refs_3_.refs_2_ = bf16[8,2,256,256]{3,2,1,0:T(8,128)(2,1)S(1)} collective-permute-done((bf16[8,2,256,256]{3,2,1,0:T(8,128)(2,1)S(1)}, bf16[8,2,256,256]{3,2,1,0:T(8,128)(2,1)S(1)}, u32[]{:S(2)}, u32[]{:S(2)}) %collective-permute-start.3) | collective-permute-done | bytes 2097184 | tf_op jit(solution)/shard_map/ppermute | solution.py:776
  146.5 28.9 %all-gather.4.cloned.1.call-done.weights.refs_8_.refs_1_ = bf16[2048,2048]{1,0:T(8,128)(2,1)} async-done(((bf16[256,2048]{1,0:T(8,128)(2,1)}), bf16[2048,2048]{1,0:T(8,128)(2,1)}) %all-gather.4.cloned.1.call-update) | async-done | bytes 8388624 | tf_op jit(solution)/shard_map/all_gather | solution.py:884
  193.3 7.4 psum.14
  200.7 36.3 %all-to-all-done.2 = bf16[16,256,256]{2,1,0:T(8,128)(2,1)S(1)} async-done(((bf16[16,256,256]{2,1,0:T(8,128)(2,1)}), bf16[16,256,256]{2,1,0:T(8,128)(2,1)S(1)}, u32[]{:S(2)}, u32[]{:S(2)}) %all-to-all-start.2) | async-done | bytes 2097184 | tf_op jit(solution)/shard_map/all_to_all | solution.py:823
  237.0 17.6 %all-to-all-start.3 = ((bf16[16,256,256]{2,1,0:T(8,128)(2,1)}), bf16[16,256,256]{2,1,0:T(8,128)(2,1)}, u32[]{:S(2)}, u32[]{:S(2)}) async-start(bf16[16,256,256]{2,1,0:T(8,128)(2,1)} %get-tuple-element.147), calls=%async_computation.3 | async-start | bytes 4194304 | tf_op jit(solution)/shard_map/all_to_all | solution.py:823
  261.6 9.1 %shard_map.264 = (bf16[512,512]{1,0:T(8,128)(2,1)S(1)}, bf16[512,512]{1,0:T(8,128)(2,1)S(1)}, bf16[512,512]{1,0:T(8,128)(2,1)S(1)}, f32[4,512]{1,0:T(4,128)S(1)}, bf16[512,2048]{1,0:T(8,128)(2,1)S(1)}) custom-call(f32[512,512]{1,0:T(8,128)S(1)} %get-tuple-element.136.refs_0_.refs_10_.refs_2_, f32[512,512]{1,0:T(8,128)S(1)} %copy-done.27, ...), custom_call_target="tpu_custom_call" | custom-call | flops 1000 | bytes 1000 | tf_op jit(solution)/shard_map/pallas_call | solution.py:49
  278.7 20.3 %collective-permute-done.5 = bf16[4,2,256,256]{3,2,1,0:T(8,128)(2,1)} collective-permute-done((bf16[4,2,256,256]{3,2,1,0:T(8,128)(2,1)}, bf16[4,2,256,256]{3,2,1,0:T(8,128)(2,1)}, u32[]{:S(2)}, u32[]{:S(2)}) %collective-permute-start.5) | collective-permute-done | bytes 1048608 | tf_op jit(solution)/shard_map/ppermute | solution.py:776
  300.3 12.3 %collective-permute-done.6 = bf16[128,2048]{1,0:T(8,128)(2,1)} collective-permute-done((bf16[128,2048]{1,0:T(8,128)(2,1)}, bf16[128,2048]{1,0:T(8,128)(2,1)}, u32[]{:S(2)}, u32[]{:S(2)}) %collective-permute-start.6) | collective-permute-done | bytes 524320 | tf_op jit(solution)/shard_map/ppermute | solution.py:776
  321.2 17.6 %all_to_all.49 = f32[16,1,128]{2,1,0:T(1,128)S(1)} all-to-all(f32[16,1,128]{2,1,0:T(1,128)S(1)} %copy.78), channel_id=1, replica_groups=mesh['t'=1,'g'=4,'p'=2,'y'=2,'c'=2] {'g','p','c'}, dimensions={0} | all-to-all | bytes 16384 | tf_op jit(solution)/shard_map/all_to_all | solution.py:814
  344.9 10.6 %shard_map.265.refs_6_ = bf16[2048,1024]{1,0:T(8,128)(2,1)S(1)} custom-call(bf16[1024,2048]{1,0:T(8,128)(2,1)S(1)} %copy-done.23, bf16[1024,2048]{1,0:T(8,128)(2,1)} %collective-permute-done.7.refs_1_, bf16[8,2,256,256]{3,2,1,0:T(8,128)(2,1)S(1)} %bitcast.107, bf16[8,2,256,256]{3,2,1,0:T(8,128)(2,1)S(1)} %copy-done.19), custom_call_target="tpu_custom_call" | custom-call | flops 1000 | bytes 1000 | tf_op jit(solution)/shard_map/pallas_call | solution.py:49
  357.5 29.7 %collective-permute-done.9 = bf16[4,2,256,256]{3,2,1,0:T(8,128)(2,1)S(1)} collective-permute-done((bf16[4,2,256,256]{3,2,1,0:T(8,128)(2,1)}, bf16[4,2,256,256]{3,2,1,0:T(8,128)(2,1)S(1)}, u32[]{:S(2)}, u32[]{:S(2)}) %collective-permute-start.9) | collective-permute-done | bytes 1048608 | tf_op jit(solution)/shard_map/ppermute | solution.py:776
  387.2 9.3 %all-gather.8.cloned.1.call-done.refs_0_ = bf16[1024,2048]{1,0:T(8,128)(2,1)} async-done(((bf16[128,2048]{1,0:T(8,128)(2,1)}), bf16[1024,2048]{1,0:T(8,128)(2,1)}) %all-gather.8.cloned.1.call-update) | async-done | bytes 4194320 | tf_op jit(solution)/shard_map/all_gather | solution.py:935
  404.0 29.7 %shard_map.266 = (bf16[2048,1024]{1,0:T(8,128)(2,1)}, bf16[2048,1024]{1,0:T(8,128)(2,1)}, bf16[2048,1024]{1,0:T(8,128)(2,1)}, f32[16,128]{1,0:T(8,128)}) custom-call(bf16[1024,2048]{1,0:T(8,128)(2,1)} %all-gather.8.cloned.1.call-done.refs_0_, bf16[1024,2048]{1,0:T(8,128)(2,1)} %collective-permute-done.10.refs_1_, bf16[8,2,256,256]{3,2,1,0:T(8,128)(2,1)} %bitcast.103, ...), custom_call_target="tpu_custom_call" | custom-call | flops 1000 | bytes 1000 | tf_op jit(solution)/shard_map/pallas_call | solution.py:49
  438.3 12.9 %shard_map.267 = bf16[1024,2176]{1,0:T(8,128)(2,1)} custom-call(bf16[2048,1024]{1,0:T(8,128)(2,1)S(1)} %copy-done.8, bf16[8,2,256,256]{3,2,1,0:T(8,128)(2,1)S(1)} %bitcast.104, bf16[8,2,256,256]{3,2,1,0:T(8,128)(2,1)S(1)} %copy-done.15, bf16[2048,1024]{1,0:T(8,128)(2,1)} %get-tuple-element.176.refs_3_.refs_2_, bf16[8,2,256,256]{3,2,1,0:T(8,128)(2,1)} %bitcast.14.refs_4_, ...), custom_call_target="tpu_custom_call" | custom-call | flops 1000 | bytes 1000 | tf_op jit(solution)/shard_map/pallas_call | solution.py:49
  451.3 13.3 %shard_map.268 = bf16[1024,2176]{1,0:T(8,128)(2,1)} custom-call(bf16[2048,1024]{1,0:T(8,128)(2,1)S(1)} %copy-done.8, bf16[8,2,256,256]{3,2,1,0:T(8,128)(2,1)S(1)} %bitcast.105, bf16[8,2,256,256]{3,2,1,0:T(8,128)(2,1)S(1)} %copy-done.15, bf16[2048,1024]{1,0:T(8,128)(2,1)} %get-tuple-element.176.refs_3_.refs_2_, bf16[8,2,256,256]{3,2,1,0:T(8,128)(2,1)} %bitcast.14.refs_4_, ...), custom_call_target="tpu_custom_call" | custom-call | flops 1000 | bytes 1000 | tf_op jit(solution)/shard_map/pallas_call | solution.py:49
  472.2 15.1 %shard_map.269 = (bf16[8,2,256,256]{3,2,1,0:T(8,128)(2,1)S(1)}, bf16[8,2,256,256]{3,2,1,0:T(8,128)(2,1)S(1)}) custom-call(bf16[1024,2048]{1,0:T(8,128)(2,1)S(1)} %copy-done.24, bf16[1024,2048]{1,0:T(8,128)(2,1)} %collective-permute-done.7.refs_1_, bf16[2048,1024]{1,0:T(8,128)(2,1)} %get-tuple-element.178.refs_2_.refs_0_), custom_call_target="tpu_custom_call" | custom-call | flops 1000 | bytes 1000 | tf_op jit(solution)/shard_map/pallas_call | solution.py:49
  488.6 7.1 shard_map.273
  504.9 15.3 %shard_map.271 = (bf16[8,2,256,256]{3,2,1,0:T(8,128)(2,1)S(1)}, bf16[8,2,256,256]{3,2,1,0:T(8,128)(2,1)}) custom-call(bf16[1024,2048]{1,0:T(8,128)(2,1)S(1)} %copy-done.6, bf16[1024,2048]{1,0:T(8,128)(2,1)} %collective-permute-done.10.refs_1_, bf16[2048,1024]{1,0:T(8,128)(2,1)} %get-tuple-element.176.refs_3_.refs_2_), custom_call_target="tpu_custom_call" | custom-call | flops 1000 | bytes 1000 | tf_op jit(solution)/shard_map/pallas_call | solution.py:49
  521.6 14.9 %shard_map.270 = (bf16[8,2,256,256]{3,2,1,0:T(8,128)(2,1)S(1)}, bf16[8,2,256,256]{3,2,1,0:T(8,128)(2,1)S(1)}) custom-call(bf16[1024,2048]{1,0:T(8,128)(2,1)S(1)} %copy-done.6, bf16[1024,2048]{1,0:T(8,128)(2,1)} %collective-permute-done.10.refs_1_, bf16[2048,1024]{1,0:T(8,128)(2,1)} %get-tuple-element.174.refs_0_.refs_2_), custom_call_target="tpu_custom_call" | custom-call | flops 1000 | bytes 1000 | tf_op jit(solution)/shard_map/pallas_call | solution.py:49
  548.1 7.9 add_convert_fusion.1
  555.9 17.0 %collective-permute-done.14 = bf16[4,2,256,256]{3,2,1,0:T(8,128)(2,1)} collective-permute-done((bf16[4,2,256,256]{3,2,1,0:T(8,128)(2,1)}, bf16[4,2,256,256]{3,2,1,0:T(8,128)(2,1)}, u32[]{:S(2)}, u32[]{:S(2)}) %collective-permute-start.14) | collective-permute-done | bytes 1048608 | tf_op jit(solution)/shard_map/ppermute | solution.py:776
  583.1 11.8 %collective-permute-done.16 = bf16[128,2048]{1,0:T(8,128)(2,1)} collective-permute-done((bf16[128,2048]{1,0:T(8,128)(2,1)}, bf16[128,2048]{1,0:T(8,128)(2,1)}, u32[]{:S(2)}, u32[]{:S(2)}) %collective-permute-start.16) | collective-permute-done | bytes 524320 | tf_op jit(solution)/shard_map/ppermute | solution.py:776
  609.9 13.0 %shard_map.274 = (f32[512,512]{1,0:T(8,128)S(1)}, f32[512,512]{1,0:T(8,128)S(1)}, bf16[512,512]{1,0:T(8,128)(2,1)S(1)}, f32[2,512]{1,0:T(2,128)S(1)}) custom-call(bf16[512,2048]{1,0:T(8,128)(2,1)S(1)} %copy-done.17, bf16[2048,2048]{1,0:T(8,128)(2,1)} %all-gather.4.cloned.1.call-done.weights.refs_8_.refs_1_, bf16[512,512]{1,0:T(8,128)(2,1)S(1)} %copy-done.52, ...), custom_call_target="tpu_custom_call" | custom-call | flops 1000 | bytes 1000 | tf_op jit(solution)/shard_map/pallas_call | solution.py:49
  633.8 9.3 %all-to-all-start.6 = ((bf16[16,256,256]{2,1,0:T(8,128)(2,1)}), bf16[16,256,256]{2,1,0:T(8,128)(2,1)}, u32[]{:S(2)}, u32[]{:S(2)}) async-start(bf16[16,256,256]{2,1,0:T(8,128)(2,1)} %bitcast.116), calls=%async_computation.7 | async-start | bytes 4194304 | tf_op jit(solution)/shard_map/all_to_all | solution.py:852
  677.5 31.2 %collective-permute-done.21 = bf16[8,2,256,256]{3,2,1,0:T(8,128)(2,1)} collective-permute-done((bf16[8,2,256,256]{3,2,1,0:T(8,128)(2,1)}, bf16[8,2,256,256]{3,2,1,0:T(8,128)(2,1)}, u32[]{:S(2)}, u32[]{:S(2)}) %collective-permute-start.21) | collective-permute-done | bytes 2097184 | tf_op jit(solution)/shard_map/ppermute | solution.py:776
  708.7 16.6 %collective-permute-done.20 = bf16[4,256,1024]{2,1,0:T(8,128)(2,1)} collective-permute-done((bf16[4,256,1024]{2,1,0:T(8,128)(2,1)}, bf16[4,256,1024]{2,1,0:T(8,128)(2,1)}, u32[]{:S(2)}, u32[]{:S(2)}) %collective-permute-start.20) | collective-permute-done | bytes 2097184 | tf_op jit(solution)/shard_map/ppermute | solution.py:776
  743.4 8.0 collective-permute-done.22
  761.7 25.3 %collective-permute-done.24 = bf16[4,256,1024]{2,1,0:T(8,128)(2,1)} collective-permute-done((bf16[4,256,1024]{2,1,0:T(8,128)(2,1)}, bf16[4,256,1024]{2,1,0:T(8,128)(2,1)}, u32[]{:S(2)}, u32[]{:S(2)}) %collective-permute-start.24) | collective-permute-done | bytes 2097184 | tf_op jit(solution)/shard_map/ppermute | solution.py:776
  787.1 7.6 collective-permute-done.23
  817.6 14.4 %collective-permute-done.28 = bf16[256,1024]{1,0:T(8,128)(2,1)} collective-permute-done((bf16[256,1024]{1,0:T(8,128)(2,1)S(1)}, bf16[256,1024]{1,0:T(8,128)(2,1)}, u32[]{:S(2)}, u32[]{:S(2)}) %collective-permute-start.28) | collective-permute-done | bytes 524320 | tf_op jit(solution)/shard_map/ppermute | solution.py:776
  (374 shorter events, 312.1 us)
Async XLA Ops:
  7.2 168.2 %all-gather.4.cloned.1.call-start = ((), (), s32[]{:S(2)}) async-start(), calls=%async_computation.11 | async-start | bytes 9437184 | tf_op jit(solution)/shard_map/all_gather | solution.py:884
  22.8 74.7 %all-to-all-start.1 = ((bf16[16,256,256]{2,1,0:T(8,128)(2,1)}), bf16[16,256,256]{2,1,0:T(8,128)(2,1)S(1)}, u32[]{:S(2)}, u32[]{:S(2)}) async-start(bf16[16,256,256]{2,1,0:T(8,128)(2,1)} %bitcast.117), calls=%async_computation.1 | async-start | bytes 4194304 | tf_op jit(solution)/shard_map/all_to_all | solution.py:823
  29.5 14.4 %collective-permute-start.1 = (bf16[512,512]{1,0:T(8,128)(2,1)S(1)}, bf16[512,512]{1,0:T(8,128)(2,1)}, u32[]{:S(2)}, u32[]{:S(2)}) collective-permute-start(bf16[512,512]{1,0:T(8,128)(2,1)S(1)} %copy-done.79), channel_id=1, source_target_pairs={{0,2},{2,0},{1,3},{3,1},{4,6},{6,4},{5,7},{7,5},{8,10},{10,8},{9,1... | collective-permute-start | bytes 1572872 | tf_op jit(solution)/shard_map/ppermute | solution.py:776
  30.0 28.3 %collective-permute-start = (bf16[512,512]{1,0:T(8,128)(2,1)S(1)}, bf16[512,512]{1,0:T(8,128)(2,1)}, u32[]{:S(2)}, u32[]{:S(2)}) collective-permute-start(bf16[512,512]{1,0:T(8,128)(2,1)S(1)} %copy-done.79), channel_id=1, source_target_pairs={{0,1},{1,0},{2,3},{3,2},{4,5},{5,4},{6,7},{7,6},{8,9},{9,8},{10,11... | collective-permute-start | bytes 1572872 | tf_op jit(solution)/shard_map/ppermute | solution.py:776
  44.0 18.1 %collective-permute-start.2 = (bf16[512,512]{1,0:T(8,128)(2,1)}, bf16[512,512]{1,0:T(8,128)(2,1)}, u32[]{:S(2)}, u32[]{:S(2)}) collective-permute-start(bf16[512,512]{1,0:T(8,128)(2,1)} %collective-permute-done.1), channel_id=1, source_target_pairs={{0,1},{1,0},{2,3},{3,2},{4,5},{5,4},{6,7},{7,6},{8,9},{9,8},{10,11... | collective-permute-start | bytes 1572872 | tf_op jit(solution)/shard_map/ppermute | solution.py:776
  97.5 47.6 %collective-permute-start.3 = (bf16[8,2,256,256]{3,2,1,0:T(8,128)(2,1)S(1)}, bf16[8,2,256,256]{3,2,1,0:T(8,128)(2,1)S(1)}, u32[]{:S(2)}, u32[]{:S(2)}) collective-permute-start(bf16[8,2,256,256]{3,2,1,0:T(8,128)(2,1)S(1)} %bitcast.106), channel_id=1, source_target_pairs={{0,2},{2,0},{1,3},{3,1},{4,6},{6,4},{5,7},{7,5},{8,10},{10,8},{9,1... | collective-permute-start | bytes 6291464 | tf_op jit(solution)/shard_map/ppermute | solution.py:776
  175.4 61.6 %all-to-all-start.2 = ((bf16[16,256,256]{2,1,0:T(8,128)(2,1)}), bf16[16,256,256]{2,1,0:T(8,128)(2,1)S(1)}, u32[]{:S(2)}, u32[]{:S(2)}) async-start(bf16[16,256,256]{2,1,0:T(8,128)(2,1)} %get-tuple-element.140), calls=%async_computation.2 | async-start | bytes 4194304 | tf_op jit(solution)/shard_map/all_to_all | solution.py:823
  179.1 137.2 %all-gather.6.cloned.1.call-start = ((), (), s32[]{:S(2)}) async-start(), calls=%async_computation.12 | async-start | bytes 4718592 | tf_op jit(solution)/shard_map/all_gather | solution.py:910
  237.0 79.3 %all-to-all-start.3 = ((bf16[16,256,256]{2,1,0:T(8,128)(2,1)}), bf16[16,256,256]{2,1,0:T(8,128)(2,1)}, u32[]{:S(2)}, u32[]{:S(2)}) async-start(bf16[16,256,256]{2,1,0:T(8,128)(2,1)} %get-tuple-element.147), calls=%async_computation.3 | async-start | bytes 4194304 | tf_op jit(solution)/shard_map/all_to_all | solution.py:823
  254.7 141.9 %all-gather.8.cloned.1.call-start = ((), (), s32[]{:S(2)}) async-start(), calls=%async_computation.13 | async-start | bytes 4718592 | tf_op jit(solution)/shard_map/all_gather | solution.py:935
  273.3 25.7 %collective-permute-start.5 = (bf16[4,2,256,256]{3,2,1,0:T(8,128)(2,1)}, bf16[4,2,256,256]{3,2,1,0:T(8,128)(2,1)}, u32[]{:S(2)}, u32[]{:S(2)}) collective-permute-start(bf16[4,2,256,256]{3,2,1,0:T(8,128)(2,1)} %slice.98), channel_id=1, source_target_pairs={{0,2},{2,0},{1,3},{3,1},{4,6},{6,4},{5,7},{7,5},{8,10},{10,8},{9,1... | collective-permute-start | bytes 3145736 | tf_op jit(solution)/shard_map/ppermute | solution.py:776
  316.3 260.4 %reduce-scatter.3.cloned.1.call-start = ((), (), s32[]{:S(2)}) async-start(), calls=%async_computation.14 | async-start | bytes 5013504 | tf_op jit(solution)/shard_map/reduce_scatter | solution.py:970
  316.4 23.1 %collective-permute-start.7 = (bf16[1024,2048]{1,0:T(8,128)(2,1)}, bf16[1024,2048]{1,0:T(8,128)(2,1)}, u32[]{:S(2)}, u32[]{:S(2)}) collective-permute-start(bf16[1024,2048]{1,0:T(8,128)(2,1)} %all-gather.6.cloned.1.call-done.refs_0_), channel_id=1, source_target_pairs={{0,1},{1,0},{2,3},{3,2},{4,5},{5,4},{6,7},{7,6},{8,9},{9,8},{10,11... | collective-permute-start | bytes 12582920 | tf_op jit(solution)/shard_map/ppermute | solution.py:776
  316.6 70.6 %collective-permute-start.8 = (bf16[8,2,256,256]{3,2,1,0:T(8,128)(2,1)}, bf16[8,2,256,256]{3,2,1,0:T(8,128)(2,1)}, u32[]{:S(2)}, u32[]{:S(2)}) collective-permute-start(bf16[8,2,256,256]{3,2,1,0:T(8,128)(2,1)} %bitcast.14.refs_4_), channel_id=1, source_target_pairs={{0,2},{2,0},{1,3},{3,1},{4,6},{6,4},{5,7},{7,5},{8,10},{10,8},{9,1... | collective-permute-start | bytes 6291464 | tf_op jit(solution)/shard_map/ppermute | solution.py:776
  319.1 68.1 %collective-permute-start.9 = (bf16[4,2,256,256]{3,2,1,0:T(8,128)(2,1)}, bf16[4,2,256,256]{3,2,1,0:T(8,128)(2,1)S(1)}, u32[]{:S(2)}, u32[]{:S(2)}) collective-permute-start(bf16[4,2,256,256]{3,2,1,0:T(8,128)(2,1)} %slice.100), channel_id=1, source_target_pairs={{0,2},{2,0},{1,3},{3,1},{4,6},{6,4},{5,7},{7,5},{8,10},{10,8},{9,1... | collective-permute-start | bytes 3145736 | tf_op jit(solution)/shard_map/ppermute | solution.py:776
  487.4 49.1 %collective-permute-start.12 = (bf16[8,2,256,256]{3,2,1,0:T(8,128)(2,1)S(1)}, bf16[8,2,256,256]{3,2,1,0:T(8,128)(2,1)}, u32[]{:S(2)}, u32[]{:S(2)}) collective-permute-start(bf16[8,2,256,256]{3,2,1,0:T(8,128)(2,1)S(1)} %get-tuple-element.173), channel_id=1, source_target_pairs={{0,2},{2,0},{1,3},{3,1},{4,6},{6,4},{5,7},{7,5},{8,10},{10,8},{9,1... | collective-permute-start | bytes 6291464 | tf_op jit(solution)/shard_map/ppermute | solution.py:776
  541.6 56.6 %all-to-all-start.5 = ((bf16[16,256,256]{2,1,0:T(8,128)(2,1)}), bf16[16,256,256]{2,1,0:T(8,128)(2,1)}, u32[]{:S(2)}, u32[]{:S(2)}) async-start(bf16[16,256,256]{2,1,0:T(8,128)(2,1)} %bitcast.115), calls=%async_computation.6 | async-start | bytes 4194304 | tf_op jit(solution)/shard_map/all_to_all | solution.py:852
  546.1 248.6 %reduce-scatter.5.cloned.1.call-start = ((), (), s32[]{:S(2)}) async-start(), calls=%async_computation.15 | async-start | bytes 4718592 | tf_op jit(solution)/shard_map/reduce_scatter | solution.py:989
  547.4 25.6 %collective-permute-start.14 = (bf16[4,2,256,256]{3,2,1,0:T(8,128)(2,1)}, bf16[4,2,256,256]{3,2,1,0:T(8,128)(2,1)}, u32[]{:S(2)}, u32[]{:S(2)}) collective-permute-start(bf16[4,2,256,256]{3,2,1,0:T(8,128)(2,1)} %slice.101), channel_id=1, source_target_pairs={{0,2},{2,0},{1,3},{3,1},{4,6},{6,4},{5,7},{7,5},{8,10},{10,8},{9,1... | collective-permute-start | bytes 3145736 | tf_op jit(solution)/shard_map/ppermute | solution.py:776
  581.1 13.8 %collective-permute-start.16 = (bf16[128,2048]{1,0:T(8,128)(2,1)}, bf16[128,2048]{1,0:T(8,128)(2,1)}, u32[]{:S(2)}, u32[]{:S(2)}) collective-permute-start(bf16[128,2048]{1,0:T(8,128)(2,1)} %get-tuple-element.271), channel_id=1, source_target_pairs={{0,2},{2,0},{1,3},{3,1},{4,6},{6,4},{5,7},{7,5},{8,10},{10,8},{9,1... | collective-permute-start | bytes 1572872 | tf_op jit(solution)/shard_map/ppermute | solution.py:776
  601.3 28.9 %collective-permute-start.18 = (bf16[4,2,256,256]{3,2,1,0:T(8,128)(2,1)}, bf16[4,2,256,256]{3,2,1,0:T(8,128)(2,1)}, u32[]{:S(2)}, u32[]{:S(2)}) collective-permute-start(bf16[4,2,256,256]{3,2,1,0:T(8,128)(2,1)} %slice.104), channel_id=1, source_target_pairs={{0,2},{2,0},{1,3},{3,1},{4,6},{6,4},{5,7},{7,5},{8,10},{10,8},{9,1... | collective-permute-start | bytes 3145736 | tf_op jit(solution)/shard_map/ppermute | solution.py:776
  633.8 91.5 %all-to-all-start.6 = ((bf16[16,256,256]{2,1,0:T(8,128)(2,1)}), bf16[16,256,256]{2,1,0:T(8,128)(2,1)}, u32[]{:S(2)}, u32[]{:S(2)}) async-start(bf16[16,256,256]{2,1,0:T(8,128)(2,1)} %bitcast.116), calls=%async_computation.7 | async-start | bytes 4194304 | tf_op jit(solution)/shard_map/all_to_all | solution.py:852
  661.4 47.3 %collective-permute-start.21 = (bf16[8,2,256,256]{3,2,1,0:T(8,128)(2,1)}, bf16[8,2,256,256]{3,2,1,0:T(8,128)(2,1)}, u32[]{:S(2)}, u32[]{:S(2)}) collective-permute-start(bf16[8,2,256,256]{3,2,1,0:T(8,128)(2,1)} %get-tuple-element.207), channel_id=1, source_target_pairs={{0,2},{2,0},{1,3},{3,1},{4,6},{6,4},{5,7},{7,5},{8,10},{10,8},{9,1... | collective-permute-start | bytes 6291464 | tf_op jit(solution)/shard_map/ppermute | solution.py:776
  663.0 62.2 %collective-permute-start.20 = (bf16[4,256,1024]{2,1,0:T(8,128)(2,1)}, bf16[4,256,1024]{2,1,0:T(8,128)(2,1)}, u32[]{:S(2)}, u32[]{:S(2)}) collective-permute-start(bf16[4,256,1024]{2,1,0:T(8,128)(2,1)} %bitcast.22), channel_id=1, source_target_pairs={{0,4},{4,0},{1,5},{5,1},{2,6},{6,2},{3,7},{7,3},{8,12},{12,8},{9,1... | collective-permute-start | bytes 6291464 | tf_op jit(solution)/shard_map/ppermute | solution.py:776
  672.1 115.0 %collective-permute-start.24 = (bf16[4,256,1024]{2,1,0:T(8,128)(2,1)}, bf16[4,256,1024]{2,1,0:T(8,128)(2,1)}, u32[]{:S(2)}, u32[]{:S(2)}) collective-permute-start(bf16[4,256,1024]{2,1,0:T(8,128)(2,1)} %bitcast.25), channel_id=1, source_target_pairs={{0,4},{4,0},{1,5},{5,1},{2,6},{6,2},{3,7},{7,3},{8,12},{12,8},{9,1... | collective-permute-start | bytes 6291464 | tf_op jit(solution)/shard_map/ppermute | solution.py:776
  728.8 104.6 %all-to-all-start.7 = ((bf16[16,256,256]{2,1,0:T(8,128)(2,1)}), bf16[16,256,256]{2,1,0:T(8,128)(2,1)}, u32[]{:S(2)}, u32[]{:S(2)}) async-start(bf16[16,256,256]{2,1,0:T(8,128)(2,1)} %bitcast.114), calls=%async_computation.9 | async-start | bytes 4194304 | tf_op jit(solution)/shard_map/all_to_all | solution.py:852
  736.9 14.4 %collective-permute-start.22 = (bf16[128,2048]{1,0:T(8,128)(2,1)}, bf16[128,2048]{1,0:T(8,128)(2,1)S(1)}, u32[]{:S(2)}, u32[]{:S(2)}) collective-permute-start(bf16[128,2048]{1,0:T(8,128)(2,1)} %fusion.16), channel_id=1, source_target_pairs={{0,2},{2,0},{1,3},{3,1},{4,6},{6,4},{5,7},{7,5},{8,10},{10,8},{9,1... | collective-permute-start | bytes 1572872 | tf_op jit(solution)/shard_map/ppermute | solution.py:776
  741.1 53.6 %collective-permute-start.23 = (bf16[2,256,1024]{2,1,0:T(8,128)(2,1)}, bf16[2,256,1024]{2,1,0:T(8,128)(2,1)}, u32[]{:S(2)}, u32[]{:S(2)}) collective-permute-start(bf16[2,256,1024]{2,1,0:T(8,128)(2,1)} %slice.175), channel_id=1, source_target_pairs={{0,8},{8,0},{16,24},{24,16},{1,9},{9,1},{17,25},{25,17},{2,10},{10... | collective-permute-start | bytes 3145736 | tf_op jit(solution)/shard_map/ppermute | solution.py:776
  797.5 35.9 %collective-permute-start.27 = (bf16[2,256,1024]{2,1,0:T(8,128)(2,1)S(1)}, bf16[2,256,1024]{2,1,0:T(8,128)(2,1)S(1)}, u32[]{:S(2)}, u32[]{:S(2)}) collective-permute-start(bf16[2,256,1024]{2,1,0:T(8,128)(2,1)S(1)} %slice.174), channel_id=1, source_target_pairs={{0,8},{8,0},{16,24},{24,16},{1,9},{9,1},{17,25},{25,17},{2,10},{10... | collective-permute-start | bytes 3145736 | tf_op jit(solution)/shard_map/ppermute | solution.py:776
  800.6 31.5 %collective-permute-start.28 = (bf16[256,1024]{1,0:T(8,128)(2,1)S(1)}, bf16[256,1024]{1,0:T(8,128)(2,1)}, u32[]{:S(2)}, u32[]{:S(2)}) collective-permute-start(bf16[256,1024]{1,0:T(8,128)(2,1)S(1)} %fusion.17), channel_id=1, source_target_pairs={{0,16},{8,24},{16,0},{24,8},{1,17},{9,25},{17,1},{25,9},{2,18},{10... | collective-permute-start | bytes 1572872 | tf_op jit(solution)/shard_map/ppermute | solution.py:776
  836.8 35.7 %collective-permute-start.32 = (bf16[256,1024]{1,0:T(8,128)(2,1)}, bf16[256,1024]{1,0:T(8,128)(2,1)}, u32[]{:S(2)}, u32[]{:S(2)}) collective-permute-start(bf16[256,1024]{1,0:T(8,128)(2,1)} %fusion.18), channel_id=1, source_target_pairs={{0,16},{8,24},{16,0},{24,8},{1,17},{9,25},{17,1},{25,9},{2,18},{10... | collective-permute-start | bytes 1572872 | tf_op jit(solution)/shard_map/ppermute | solution.py:776
  852.5 22.2 %all-to-all-start.8 = ((bf16[4,2,128,512]{3,2,1,0:T(8,128)(2,1)}), bf16[4,2,128,512]{3,2,1,0:T(8,128)(2,1)S(1)}, u32[]{:S(2)}, u32[]{:S(2)}) async-start(bf16[4,2,128,512]{3,2,1,0:T(8,128)(2,1)} %maximum_bitcast_fusion), calls=%async_computation.10 | async-start | bytes 2097152 | tf_op jit(solution)/shard_map/all_to_all | solution.py:1072
  (102 other events, 1405.5 us)
Sparse Core Ops, SparseCore 0:
  10.7 164.6 all-gather.3
  182.7 129.5 all-gather.5
  316.5 80.0 all-gather.7
  470.2 106.4 reduce-scatter.2
  595.1 112.5 reduce-scatter.4

commit v4 on v3

--- a/solution.py
+++ b/solution.py
@@ -1026,11 +1026,10 @@
     qkv_grad, pair_keep, pair_near = stage(qkv_grad, pair_keep, pair_near)
     pair_near = swap(pair_near, "p")
     keep, send = sum_near(dot(qkv_grad, qkv_full, ((1,), (1,))))
-    keep, send, two_near, two_keep, up_theirs, gate_got = stage(
-        keep, send, two_near, two_keep, up_theirs, gate_got
-    )
+    keep, send, up_theirs, gate_got = stage(keep, send, up_theirs, gate_got)
     up_got = to_slices(up_mine, up_theirs)
     send = swap(send, "y")
+    send, two_near, two_keep = stage(send, two_near, two_keep)
     normed_grad = add(keep, send)
     two_parts = add(two_keep, two_near)
     two_far = swap(two_parts[2:].astype(BF), "g", 1)
@@ -1048,8 +1047,7 @@
         ],
         axis=0,
     )
-    small = sum_over(small, "c")
-    small = sum_over(small, "y")
+    small = sum_over(small, "g")
     grad_rows, two_far, two_parts, pair_near, pair_keep, small, moe_sum = stage(
         grad_rows, two_far, two_parts, pair_near, pair_keep, small, moe_sum
     )
@@ -1058,14 +1056,14 @@
     pair_far = swap(pair_parts[2:].astype(BF), "g", 1)
     two_parts = add(two_parts[:2], two_far)
     two_far = swap(two_parts[1].astype(BF), "g", 2)
-    small = sum_over(small, "p")
+    small = sum_over(sum_over(small, "p"), "t")
     pair_far, pair_parts, two_far, two_parts, small, up_got, grad_rows, moe_sum = stage(
         pair_far, pair_parts, two_far, two_parts, small, up_got, grad_rows, moe_sum
     )
 
     pair_parts = add(pair_parts[:2], pair_far)
     pair_far = swap(pair_parts[1].astype(BF), "g", 2)
-    small = sum_over(sum_over(small, "g"), "t")
+    small = sum_over(sum_over(small, "y"), "c")
     grad_two = add(two_parts[0], two_far)
     both_rows = jnp.stack([(residual + moe_sum.astype(F32)).astype(BF), grad_rows])
     both_rows = jnp.transpose(both_rows.reshape(2, rows, lanes, head_cols), (2, 0, 1, 3))

time: 893 us -> 888 us (level)
  transfers between devices with their start and end apart: 46 -> 46, of which waited for: 26 -> 24; matrix products, arithmetic and copies ran while one was open for 14% -> 14% of each run, Pallas kernels for 14% -> 14%
where the time goes in v4:
time: 888 us; the launch traced here: 878 us
  waiting for transfers between devices  385 us (43%)
  Pallas kernels  167 us (19%)
  local copies, waits for them, and re-layouts  106 us (12%)
  starting transfers between devices  87.8 us (10%)
  other arithmetic  73.1 us (8%)
  blocking collectives  36.6 us (4%)
  between operations  15.5 us (2%)
    ppermute x33, waiting for transfers between devices, swap(): return lax.ppermute(values, axis, [(i, i ^ step) for i in range(count)])  265 us
    pallas_call x13, Pallas kernels, call(): pl.pallas_call(body, out_shape=outs, in_specs=[place_of(a) for a in args]...  156 us
    unnamed x183, local copies, waits for them, and re-layouts  66.2 us
    all_to_all x3, waiting for transfers between devices, to_group(): got = lax.all_to_all(weight, GROUP, 0, 0, tiled=True)  64.3 us
    ppermute x33, starting transfers between devices, swap(): return lax.ppermute(values, axis, [(i, i ^ step) for i in range(count)])  31.5 us
    all_gather x1, waiting for transfers between devices, per_device(): lax.all_gather(jnp.concatenate([w_query, w_key, w_value, w_out], axis=1),...  28.9 us
    all_to_all x3, starting transfers between devices, to_group(): got = lax.all_to_all(weight, GROUP, 0, 0, tiled=True)  28 us
    all_to_all x3, starting transfers between devices, to_slices(): return lax.all_to_all(sent, GROUP, 0, 0, tiled=True)  19.8 us
  transfers between devices with their start and end apart: 46, of which 24 were waited for; matrix products, arithmetic and copies ran while one was open for 14% of the time, Pallas kernels for 14%

profile of v4, /device:TPU:0, one launch (start us, length us, event | category | flops | bytes accessed | tf_op | source)
XLA Modules:
  0.0 878.2 jit_solution(976350602883485935)
XLA Ops:
  16.0 6.8 all-to-all-done
  30.1 13.9 %collective-permute-done.1 = bf16[512,512]{1,0:T(8,128)(2,1)} collective-permute-done((bf16[512,512]{1,0:T(8,128)(2,1)S(1)}, bf16[512,512]{1,0:T(8,128)(2,1)}, u32[]{:S(2)}, u32[]{:S(2)}) %collective-permute-start.1) | collective-permute-done | bytes 524320 | tf_op jit(solution)/shard_map/ppermute | solution.py:776
  69.6 27.9 %all-to-all-done.1 = bf16[16,256,256]{2,1,0:T(8,128)(2,1)S(1)} async-done(((bf16[16,256,256]{2,1,0:T(8,128)(2,1)}), bf16[16,256,256]{2,1,0:T(8,128)(2,1)S(1)}, u32[]{:S(2)}, u32[]{:S(2)}) %all-to-all-start.1) | async-done | bytes 2097184 | tf_op jit(solution)/shard_map/all_to_all | solution.py:823
  100.2 44.9 %collective-permute-done.3.refs_3_.refs_2_ = bf16[8,2,256,256]{3,2,1,0:T(8,128)(2,1)S(1)} collective-permute-done((bf16[8,2,256,256]{3,2,1,0:T(8,128)(2,1)S(1)}, bf16[8,2,256,256]{3,2,1,0:T(8,128)(2,1)S(1)}, u32[]{:S(2)}, u32[]{:S(2)}) %collective-permute-start.3) | collective-permute-done | bytes 2097184 | tf_op jit(solution)/shard_map/ppermute | solution.py:776
  146.5 28.9 %all-gather.4.cloned.1.call-done.weights.refs_8_.refs_1_ = bf16[2048,2048]{1,0:T(8,128)(2,1)} async-done(((bf16[256,2048]{1,0:T(8,128)(2,1)}), bf16[2048,2048]{1,0:T(8,128)(2,1)}) %all-gather.4.cloned.1.call-update) | async-done | bytes 8388624 | tf_op jit(solution)/shard_map/all_gather | solution.py:884
  193.3 7.4 psum.14
  200.7 36.3 %all-to-all-done.2 = bf16[16,256,256]{2,1,0:T(8,128)(2,1)S(1)} async-done(((bf16[16,256,256]{2,1,0:T(8,128)(2,1)}), bf16[16,256,256]{2,1,0:T(8,128)(2,1)S(1)}, u32[]{:S(2)}, u32[]{:S(2)}) %all-to-all-start.2) | async-done | bytes 2097184 | tf_op jit(solution)/shard_map/all_to_all | solution.py:823
  237.0 17.6 %all-to-all-start.3 = ((bf16[16,256,256]{2,1,0:T(8,128)(2,1)}), bf16[16,256,256]{2,1,0:T(8,128)(2,1)}, u32[]{:S(2)}, u32[]{:S(2)}) async-start(bf16[16,256,256]{2,1,0:T(8,128)(2,1)} %get-tuple-element.148), calls=%async_computation.3 | async-start | bytes 4194304 | tf_op jit(solution)/shard_map/all_to_all | solution.py:823
  261.6 9.1 %shard_map.264 = (bf16[512,512]{1,0:T(8,128)(2,1)S(1)}, bf16[512,512]{1,0:T(8,128)(2,1)S(1)}, bf16[512,512]{1,0:T(8,128)(2,1)S(1)}, f32[4,512]{1,0:T(4,128)S(1)}, bf16[512,2048]{1,0:T(8,128)(2,1)S(1)}) custom-call(f32[512,512]{1,0:T(8,128)S(1)} %get-tuple-element.137.refs_0_.refs_10_.refs_2_, f32[512,512]{1,0:T(8,128)S(1)} %copy-done.27, ...), custom_call_target="tpu_custom_call" | custom-call | flops 1000 | bytes 1000 | tf_op jit(solution)/shard_map/pallas_call | solution.py:49
  278.7 20.3 %collective-permute-done.5 = bf16[4,2,256,256]{3,2,1,0:T(8,128)(2,1)} collective-permute-done((bf16[4,2,256,256]{3,2,1,0:T(8,128)(2,1)}, bf16[4,2,256,256]{3,2,1,0:T(8,128)(2,1)}, u32[]{:S(2)}, u32[]{:S(2)}) %collective-permute-start.5) | collective-permute-done | bytes 1048608 | tf_op jit(solution)/shard_map/ppermute | solution.py:776
  300.3 12.3 %collective-permute-done.6 = bf16[128,2048]{1,0:T(8,128)(2,1)} collective-permute-done((bf16[128,2048]{1,0:T(8,128)(2,1)}, bf16[128,2048]{1,0:T(8,128)(2,1)}, u32[]{:S(2)}, u32[]{:S(2)}) %collective-permute-start.6) | collective-permute-done | bytes 524320 | tf_op jit(solution)/shard_map/ppermute | solution.py:776
  321.2 17.6 %all_to_all.49 = f32[16,1,128]{2,1,0:T(1,128)S(1)} all-to-all(f32[16,1,128]{2,1,0:T(1,128)S(1)} %copy.78), channel_id=1, replica_groups=mesh['t'=1,'g'=4,'p'=2,'y'=2,'c'=2] {'g','p','c'}, dimensions={0} | all-to-all | bytes 16384 | tf_op jit(solution)/shard_map/all_to_all | solution.py:814
  344.9 10.6 %shard_map.265.refs_6_ = bf16[2048,1024]{1,0:T(8,128)(2,1)S(1)} custom-call(bf16[1024,2048]{1,0:T(8,128)(2,1)S(1)} %copy-done.23, bf16[1024,2048]{1,0:T(8,128)(2,1)} %collective-permute-done.7.refs_1_, bf16[8,2,256,256]{3,2,1,0:T(8,128)(2,1)S(1)} %bitcast.107, bf16[8,2,256,256]{3,2,1,0:T(8,128)(2,1)S(1)} %copy-done.19), custom_call_target="tpu_custom_call" | custom-call | flops 1000 | bytes 1000 | tf_op jit(solution)/shard_map/pallas_call | solution.py:49
  357.5 29.7 %collective-permute-done.9 = bf16[4,2,256,256]{3,2,1,0:T(8,128)(2,1)S(1)} collective-permute-done((bf16[4,2,256,256]{3,2,1,0:T(8,128)(2,1)}, bf16[4,2,256,256]{3,2,1,0:T(8,128)(2,1)S(1)}, u32[]{:S(2)}, u32[]{:S(2)}) %collective-permute-start.9) | collective-permute-done | bytes 1048608 | tf_op jit(solution)/shard_map/ppermute | solution.py:776
  387.2 9.3 %all-gather.8.cloned.1.call-done.refs_0_ = bf16[1024,2048]{1,0:T(8,128)(2,1)} async-done(((bf16[128,2048]{1,0:T(8,128)(2,1)}), bf16[1024,2048]{1,0:T(8,128)(2,1)}) %all-gather.8.cloned.1.call-update) | async-done | bytes 4194320 | tf_op jit(solution)/shard_map/all_gather | solution.py:935
  404.0 29.7 %shard_map.266 = (bf16[2048,1024]{1,0:T(8,128)(2,1)}, bf16[2048,1024]{1,0:T(8,128)(2,1)}, bf16[2048,1024]{1,0:T(8,128)(2,1)}, f32[16,128]{1,0:T(8,128)}) custom-call(bf16[1024,2048]{1,0:T(8,128)(2,1)} %all-gather.8.cloned.1.call-done.refs_0_, bf16[1024,2048]{1,0:T(8,128)(2,1)} %collective-permute-done.10.refs_1_, bf16[8,2,256,256]{3,2,1,0:T(8,128)(2,1)} %bitcast.103, ...), custom_call_target="tpu_custom_call" | custom-call | flops 1000 | bytes 1000 | tf_op jit(solution)/shard_map/pallas_call | solution.py:49
  438.3 12.9 %shard_map.267 = bf16[1024,2176]{1,0:T(8,128)(2,1)} custom-call(bf16[2048,1024]{1,0:T(8,128)(2,1)S(1)} %copy-done.8, bf16[8,2,256,256]{3,2,1,0:T(8,128)(2,1)S(1)} %bitcast.104, bf16[8,2,256,256]{3,2,1,0:T(8,128)(2,1)S(1)} %copy-done.15, bf16[2048,1024]{1,0:T(8,128)(2,1)} %get-tuple-element.177.refs_3_.refs_2_, bf16[8,2,256,256]{3,2,1,0:T(8,128)(2,1)} %bitcast.14.refs_4_, ...), custom_call_target="tpu_custom_call" | custom-call | flops 1000 | bytes 1000 | tf_op jit(solution)/shard_map/pallas_call | solution.py:49
  451.3 13.3 %shard_map.268 = bf16[1024,2176]{1,0:T(8,128)(2,1)} custom-call(bf16[2048,1024]{1,0:T(8,128)(2,1)S(1)} %copy-done.8, bf16[8,2,256,256]{3,2,1,0:T(8,128)(2,1)S(1)} %bitcast.105, bf16[8,2,256,256]{3,2,1,0:T(8,128)(2,1)S(1)} %copy-done.15, bf16[2048,1024]{1,0:T(8,128)(2,1)} %get-tuple-element.177.refs_3_.refs_2_, bf16[8,2,256,256]{3,2,1,0:T(8,128)(2,1)} %bitcast.14.refs_4_, ...), custom_call_target="tpu_custom_call" | custom-call | flops 1000 | bytes 1000 | tf_op jit(solution)/shard_map/pallas_call | solution.py:49
  472.2 15.1 %shard_map.269 = (bf16[8,2,256,256]{3,2,1,0:T(8,128)(2,1)S(1)}, bf16[8,2,256,256]{3,2,1,0:T(8,128)(2,1)S(1)}) custom-call(bf16[1024,2048]{1,0:T(8,128)(2,1)S(1)} %copy-done.24, bf16[1024,2048]{1,0:T(8,128)(2,1)} %collective-permute-done.7.refs_1_, bf16[2048,1024]{1,0:T(8,128)(2,1)} %get-tuple-element.179.refs_2_.refs_0_), custom_call_target="tpu_custom_call" | custom-call | flops 1000 | bytes 1000 | tf_op jit(solution)/shard_map/pallas_call | solution.py:49
  488.6 7.1 shard_map.273
  497.8 7.1 shard_map.272
  504.9 15.3 %shard_map.271 = (bf16[8,2,256,256]{3,2,1,0:T(8,128)(2,1)S(1)}, bf16[8,2,256,256]{3,2,1,0:T(8,128)(2,1)}) custom-call(bf16[1024,2048]{1,0:T(8,128)(2,1)S(1)} %copy-done.6, bf16[1024,2048]{1,0:T(8,128)(2,1)} %collective-permute-done.10.refs_1_, bf16[2048,1024]{1,0:T(8,128)(2,1)} %get-tuple-element.177.refs_3_.refs_2_), custom_call_target="tpu_custom_call" | custom-call | flops 1000 | bytes 1000 | tf_op jit(solution)/shard_map/pallas_call | solution.py:49
  521.6 14.9 %shard_map.270 = (bf16[8,2,256,256]{3,2,1,0:T(8,128)(2,1)S(1)}, bf16[8,2,256,256]{3,2,1,0:T(8,128)(2,1)S(1)}) custom-call(bf16[1024,2048]{1,0:T(8,128)(2,1)S(1)} %copy-done.6, bf16[1024,2048]{1,0:T(8,128)(2,1)} %collective-permute-done.10.refs_1_, bf16[2048,1024]{1,0:T(8,128)(2,1)} %get-tuple-element.175.refs_0_.refs_2_), custom_call_target="tpu_custom_call" | custom-call | flops 1000 | bytes 1000 | tf_op jit(solution)/shard_map/pallas_call | solution.py:49
  548.1 7.9 add_convert_fusion.1
  555.9 17.0 %collective-permute-done.14 = bf16[4,2,256,256]{3,2,1,0:T(8,128)(2,1)} collective-permute-done((bf16[4,2,256,256]{3,2,1,0:T(8,128)(2,1)}, bf16[4,2,256,256]{3,2,1,0:T(8,128)(2,1)}, u32[]{:S(2)}, u32[]{:S(2)}) %collective-permute-start.14) | collective-permute-done | bytes 1048608 | tf_op jit(solution)/shard_map/ppermute | solution.py:776
  583.1 11.8 %collective-permute-done.16 = bf16[128,2048]{1,0:T(8,128)(2,1)} collective-permute-done((bf16[128,2048]{1,0:T(8,128)(2,1)}, bf16[128,2048]{1,0:T(8,128)(2,1)}, u32[]{:S(2)}, u32[]{:S(2)}) %collective-permute-start.16) | collective-permute-done | bytes 524320 | tf_op jit(solution)/shard_map/ppermute | solution.py:776
  609.9 13.0 %shard_map.274 = (f32[512,512]{1,0:T(8,128)S(1)}, f32[512,512]{1,0:T(8,128)S(1)}, bf16[512,512]{1,0:T(8,128)(2,1)S(1)}, f32[2,512]{1,0:T(2,128)S(1)}) custom-call(bf16[512,2048]{1,0:T(8,128)(2,1)S(1)} %copy-done.17, bf16[2048,2048]{1,0:T(8,128)(2,1)} %all-gather.4.cloned.1.call-done.weights.refs_8_.refs_1_, bf16[512,512]{1,0:T(8,128)(2,1)S(1)} %copy-done.52, ...), custom_call_target="tpu_custom_call" | custom-call | flops 1000 | bytes 1000 | tf_op jit(solution)/shard_map/pallas_call | solution.py:49
  633.7 9.2 %all-to-all-start.6 = ((bf16[16,256,256]{2,1,0:T(8,128)(2,1)}), bf16[16,256,256]{2,1,0:T(8,128)(2,1)}, u32[]{:S(2)}, u32[]{:S(2)}) async-start(bf16[16,256,256]{2,1,0:T(8,128)(2,1)} %bitcast.116), calls=%async_computation.7 | async-start | bytes 4194304 | tf_op jit(solution)/shard_map/all_to_all | solution.py:852
  676.2 32.4 %collective-permute-done.20 = bf16[8,2,256,256]{3,2,1,0:T(8,128)(2,1)} collective-permute-done((bf16[8,2,256,256]{3,2,1,0:T(8,128)(2,1)}, bf16[8,2,256,256]{3,2,1,0:T(8,128)(2,1)}, u32[]{:S(2)}, u32[]{:S(2)}) %collective-permute-start.20) | collective-permute-done | bytes 2097184 | tf_op jit(solution)/shard_map/ppermute | solution.py:776
  720.2 17.7 %collective-permute-done.22 = bf16[4,256,1024]{2,1,0:T(8,128)(2,1)} collective-permute-done((bf16[4,256,1024]{2,1,0:T(8,128)(2,1)}, bf16[4,256,1024]{2,1,0:T(8,128)(2,1)}, u32[]{:S(2)}, u32[]{:S(2)}) %collective-permute-start.22) | collective-permute-done | bytes 2097184 | tf_op jit(solution)/shard_map/ppermute | solution.py:776
  745.7 35.9 %collective-permute-done.25 = f32[20,2048]{1,0:T(8,128)S(1)} collective-permute-done((f32[20,2048]{1,0:T(8,128)S(1)}, f32[20,2048]{1,0:T(8,128)S(1)}, u32[]{:S(2)}, u32[]{:S(2)}) %collective-permute-start.25) | collective-permute-done | bytes 163872 | tf_op jit(solution)/shard_map/ppermute | solution.py:776
  817.2 14.3 %collective-permute-done.28 = bf16[256,1024]{1,0:T(8,128)(2,1)} collective-permute-done((bf16[256,1024]{1,0:T(8,128)(2,1)S(1)}, bf16[256,1024]{1,0:T(8,128)(2,1)}, u32[]{:S(2)}, u32[]{:S(2)}) %collective-permute-start.28) | collective-permute-done | bytes 524320 | tf_op jit(solution)/shard_map/ppermute | solution.py:776
  (374 shorter events, 295.4 us)
Async XLA Ops:
  7.2 168.2 %all-gather.4.cloned.1.call-start = ((), (), s32[]{:S(2)}) async-start(), calls=%async_computation.11 | async-start | bytes 9437184 | tf_op jit(solution)/shard_map/all_gather | solution.py:884
  22.8 74.7 %all-to-all-start.1 = ((bf16[16,256,256]{2,1,0:T(8,128)(2,1)}), bf16[16,256,256]{2,1,0:T(8,128)(2,1)S(1)}, u32[]{:S(2)}, u32[]{:S(2)}) async-start(bf16[16,256,256]{2,1,0:T(8,128)(2,1)} %bitcast.117), calls=%async_computation.1 | async-start | bytes 4194304 | tf_op jit(solution)/shard_map/all_to_all | solution.py:823
  29.5 14.4 %collective-permute-start.1 = (bf16[512,512]{1,0:T(8,128)(2,1)S(1)}, bf16[512,512]{1,0:T(8,128)(2,1)}, u32[]{:S(2)}, u32[]{:S(2)}) collective-permute-start(bf16[512,512]{1,0:T(8,128)(2,1)S(1)} %copy-done.79), channel_id=1, source_target_pairs={{0,2},{2,0},{1,3},{3,1},{4,6},{6,4},{5,7},{7,5},{8,10},{10,8},{9,1... | collective-permute-start | bytes 1572872 | tf_op jit(solution)/shard_map/ppermute | solution.py:776
  30.0 28.3 %collective-permute-start = (bf16[512,512]{1,0:T(8,128)(2,1)S(1)}, bf16[512,512]{1,0:T(8,128)(2,1)}, u32[]{:S(2)}, u32[]{:S(2)}) collective-permute-start(bf16[512,512]{1,0:T(8,128)(2,1)S(1)} %copy-done.79), channel_id=1, source_target_pairs={{0,1},{1,0},{2,3},{3,2},{4,5},{5,4},{6,7},{7,6},{8,9},{9,8},{10,11... | collective-permute-start | bytes 1572872 | tf_op jit(solution)/shard_map/ppermute | solution.py:776
  44.0 18.1 %collective-permute-start.2 = (bf16[512,512]{1,0:T(8,128)(2,1)}, bf16[512,512]{1,0:T(8,128)(2,1)}, u32[]{:S(2)}, u32[]{:S(2)}) collective-permute-start(bf16[512,512]{1,0:T(8,128)(2,1)} %collective-permute-done.1), channel_id=1, source_target_pairs={{0,1},{1,0},{2,3},{3,2},{4,5},{5,4},{6,7},{7,6},{8,9},{9,8},{10,11... | collective-permute-start | bytes 1572872 | tf_op jit(solution)/shard_map/ppermute | solution.py:776
  97.5 47.6 %collective-permute-start.3 = (bf16[8,2,256,256]{3,2,1,0:T(8,128)(2,1)S(1)}, bf16[8,2,256,256]{3,2,1,0:T(8,128)(2,1)S(1)}, u32[]{:S(2)}, u32[]{:S(2)}) collective-permute-start(bf16[8,2,256,256]{3,2,1,0:T(8,128)(2,1)S(1)} %bitcast.106), channel_id=1, source_target_pairs={{0,2},{2,0},{1,3},{3,1},{4,6},{6,4},{5,7},{7,5},{8,10},{10,8},{9,1... | collective-permute-start | bytes 6291464 | tf_op jit(solution)/shard_map/ppermute | solution.py:776
  175.4 61.6 %all-to-all-start.2 = ((bf16[16,256,256]{2,1,0:T(8,128)(2,1)}), bf16[16,256,256]{2,1,0:T(8,128)(2,1)S(1)}, u32[]{:S(2)}, u32[]{:S(2)}) async-start(bf16[16,256,256]{2,1,0:T(8,128)(2,1)} %get-tuple-element.141), calls=%async_computation.2 | async-start | bytes 4194304 | tf_op jit(solution)/shard_map/all_to_all | solution.py:823
  179.1 137.2 %all-gather.6.cloned.1.call-start = ((), (), s32[]{:S(2)}) async-start(), calls=%async_computation.12 | async-start | bytes 4718592 | tf_op jit(solution)/shard_map/all_gather | solution.py:910
  237.0 79.3 %all-to-all-start.3 = ((bf16[16,256,256]{2,1,0:T(8,128)(2,1)}), bf16[16,256,256]{2,1,0:T(8,128)(2,1)}, u32[]{:S(2)}, u32[]{:S(2)}) async-start(bf16[16,256,256]{2,1,0:T(8,128)(2,1)} %get-tuple-element.148), calls=%async_computation.3 | async-start | bytes 4194304 | tf_op jit(solution)/shard_map/all_to_all | solution.py:823
  254.7 141.9 %all-gather.8.cloned.1.call-start = ((), (), s32[]{:S(2)}) async-start(), calls=%async_computation.13 | async-start | bytes 4718592 | tf_op jit(solution)/shard_map/all_gather | solution.py:935
  273.3 25.7 %collective-permute-start.5 = (bf16[4,2,256,256]{3,2,1,0:T(8,128)(2,1)}, bf16[4,2,256,256]{3,2,1,0:T(8,128)(2,1)}, u32[]{:S(2)}, u32[]{:S(2)}) collective-permute-start(bf16[4,2,256,256]{3,2,1,0:T(8,128)(2,1)} %slice.98), channel_id=1, source_target_pairs={{0,2},{2,0},{1,3},{3,1},{4,6},{6,4},{5,7},{7,5},{8,10},{10,8},{9,1... | collective-permute-start | bytes 3145736 | tf_op jit(solution)/shard_map/ppermute | solution.py:776
  316.3 260.4 %reduce-scatter.3.cloned.1.call-start = ((), (), s32[]{:S(2)}) async-start(), calls=%async_computation.14 | async-start | bytes 5013504 | tf_op jit(solution)/shard_map/reduce_scatter | solution.py:970
  316.4 23.1 %collective-permute-start.7 = (bf16[1024,2048]{1,0:T(8,128)(2,1)}, bf16[1024,2048]{1,0:T(8,128)(2,1)}, u32[]{:S(2)}, u32[]{:S(2)}) collective-permute-start(bf16[1024,2048]{1,0:T(8,128)(2,1)} %all-gather.6.cloned.1.call-done.refs_0_), channel_id=1, source_target_pairs={{0,1},{1,0},{2,3},{3,2},{4,5},{5,4},{6,7},{7,6},{8,9},{9,8},{10,11... | collective-permute-start | bytes 12582920 | tf_op jit(solution)/shard_map/ppermute | solution.py:776
  316.6 70.6 %collective-permute-start.8 = (bf16[8,2,256,256]{3,2,1,0:T(8,128)(2,1)}, bf16[8,2,256,256]{3,2,1,0:T(8,128)(2,1)}, u32[]{:S(2)}, u32[]{:S(2)}) collective-permute-start(bf16[8,2,256,256]{3,2,1,0:T(8,128)(2,1)} %bitcast.14.refs_4_), channel_id=1, source_target_pairs={{0,2},{2,0},{1,3},{3,1},{4,6},{6,4},{5,7},{7,5},{8,10},{10,8},{9,1... | collective-permute-start | bytes 6291464 | tf_op jit(solution)/shard_map/ppermute | solution.py:776
  319.1 68.1 %collective-permute-start.9 = (bf16[4,2,256,256]{3,2,1,0:T(8,128)(2,1)}, bf16[4,2,256,256]{3,2,1,0:T(8,128)(2,1)S(1)}, u32[]{:S(2)}, u32[]{:S(2)}) collective-permute-start(bf16[4,2,256,256]{3,2,1,0:T(8,128)(2,1)} %slice.100), channel_id=1, source_target_pairs={{0,2},{2,0},{1,3},{3,1},{4,6},{6,4},{5,7},{7,5},{8,10},{10,8},{9,1... | collective-permute-start | bytes 3145736 | tf_op jit(solution)/shard_map/ppermute | solution.py:776
  487.4 49.1 %collective-permute-start.12 = (bf16[8,2,256,256]{3,2,1,0:T(8,128)(2,1)S(1)}, bf16[8,2,256,256]{3,2,1,0:T(8,128)(2,1)}, u32[]{:S(2)}, u32[]{:S(2)}) collective-permute-start(bf16[8,2,256,256]{3,2,1,0:T(8,128)(2,1)S(1)} %get-tuple-element.174), channel_id=1, source_target_pairs={{0,2},{2,0},{1,3},{3,1},{4,6},{6,4},{5,7},{7,5},{8,10},{10,8},{9,1... | collective-permute-start | bytes 6291464 | tf_op jit(solution)/shard_map/ppermute | solution.py:776
  541.6 56.6 %all-to-all-start.5 = ((bf16[16,256,256]{2,1,0:T(8,128)(2,1)}), bf16[16,256,256]{2,1,0:T(8,128)(2,1)}, u32[]{:S(2)}, u32[]{:S(2)}) async-start(bf16[16,256,256]{2,1,0:T(8,128)(2,1)} %bitcast.115), calls=%async_computation.6 | async-start | bytes 4194304 | tf_op jit(solution)/shard_map/all_to_all | solution.py:852
  546.1 247.4 %reduce-scatter.5.cloned.1.call-start = ((), (), s32[]{:S(2)}) async-start(), calls=%async_computation.15 | async-start | bytes 4718592 | tf_op jit(solution)/shard_map/reduce_scatter | solution.py:989
  547.4 25.6 %collective-permute-start.14 = (bf16[4,2,256,256]{3,2,1,0:T(8,128)(2,1)}, bf16[4,2,256,256]{3,2,1,0:T(8,128)(2,1)}, u32[]{:S(2)}, u32[]{:S(2)}) collective-permute-start(bf16[4,2,256,256]{3,2,1,0:T(8,128)(2,1)} %slice.101), channel_id=1, source_target_pairs={{0,2},{2,0},{1,3},{3,1},{4,6},{6,4},{5,7},{7,5},{8,10},{10,8},{9,1... | collective-permute-start | bytes 3145736 | tf_op jit(solution)/shard_map/ppermute | solution.py:776
  601.3 28.9 %collective-permute-start.18 = (bf16[4,2,256,256]{3,2,1,0:T(8,128)(2,1)}, bf16[4,2,256,256]{3,2,1,0:T(8,128)(2,1)}, u32[]{:S(2)}, u32[]{:S(2)}) collective-permute-start(bf16[4,2,256,256]{3,2,1,0:T(8,128)(2,1)} %slice.104), channel_id=1, source_target_pairs={{0,2},{2,0},{1,3},{3,1},{4,6},{6,4},{5,7},{7,5},{8,10},{10,8},{9,1... | collective-permute-start | bytes 3145736 | tf_op jit(solution)/shard_map/ppermute | solution.py:776
  633.7 75.0 %all-to-all-start.6 = ((bf16[16,256,256]{2,1,0:T(8,128)(2,1)}), bf16[16,256,256]{2,1,0:T(8,128)(2,1)}, u32[]{:S(2)}, u32[]{:S(2)}) async-start(bf16[16,256,256]{2,1,0:T(8,128)(2,1)} %bitcast.116), calls=%async_computation.7 | async-start | bytes 4194304 | tf_op jit(solution)/shard_map/all_to_all | solution.py:852
  661.4 47.3 %collective-permute-start.20 = (bf16[8,2,256,256]{3,2,1,0:T(8,128)(2,1)}, bf16[8,2,256,256]{3,2,1,0:T(8,128)(2,1)}, u32[]{:S(2)}, u32[]{:S(2)}) collective-permute-start(bf16[8,2,256,256]{3,2,1,0:T(8,128)(2,1)} %get-tuple-element.206), channel_id=1, source_target_pairs={{0,2},{2,0},{1,3},{3,1},{4,6},{6,4},{5,7},{7,5},{8,10},{10,8},{9,1... | collective-permute-start | bytes 6291464 | tf_op jit(solution)/shard_map/ppermute | solution.py:776
  670.8 67.1 %collective-permute-start.22 = (bf16[4,256,1024]{2,1,0:T(8,128)(2,1)}, bf16[4,256,1024]{2,1,0:T(8,128)(2,1)}, u32[]{:S(2)}, u32[]{:S(2)}) collective-permute-start(bf16[4,256,1024]{2,1,0:T(8,128)(2,1)} %bitcast.22), channel_id=1, source_target_pairs={{0,4},{4,0},{1,5},{5,1},{2,6},{6,2},{3,7},{7,3},{8,12},{12,8},{9,1... | collective-permute-start | bytes 6291464 | tf_op jit(solution)/shard_map/ppermute | solution.py:776
  672.1 121.3 %collective-permute-start.24 = (bf16[4,256,1024]{2,1,0:T(8,128)(2,1)}, bf16[4,256,1024]{2,1,0:T(8,128)(2,1)}, u32[]{:S(2)}, u32[]{:S(2)}) collective-permute-start(bf16[4,256,1024]{2,1,0:T(8,128)(2,1)} %bitcast.25), channel_id=1, source_target_pairs={{0,4},{4,0},{1,5},{5,1},{2,6},{6,2},{3,7},{7,3},{8,12},{12,8},{9,1... | collective-permute-start | bytes 6291464 | tf_op jit(solution)/shard_map/ppermute | solution.py:776
  712.2 120.1 %all-to-all-start.7 = ((bf16[16,256,256]{2,1,0:T(8,128)(2,1)}), bf16[16,256,256]{2,1,0:T(8,128)(2,1)}, u32[]{:S(2)}, u32[]{:S(2)}) async-start(bf16[16,256,256]{2,1,0:T(8,128)(2,1)} %bitcast.114), calls=%async_computation.9 | async-start | bytes 4194304 | tf_op jit(solution)/shard_map/all_to_all | solution.py:852
  718.4 19.6 %collective-permute-start.21 = (bf16[128,2048]{1,0:T(8,128)(2,1)}, bf16[128,2048]{1,0:T(8,128)(2,1)S(1)}, u32[]{:S(2)}, u32[]{:S(2)}) collective-permute-start(bf16[128,2048]{1,0:T(8,128)(2,1)} %fusion.16), channel_id=1, source_target_pairs={{0,2},{2,0},{1,3},{3,1},{4,6},{6,4},{5,7},{7,5},{8,10},{10,8},{9,1... | collective-permute-start | bytes 1572872 | tf_op jit(solution)/shard_map/ppermute | solution.py:776
  741.9 51.6 %collective-permute-start.23 = (bf16[2,256,1024]{2,1,0:T(8,128)(2,1)}, bf16[2,256,1024]{2,1,0:T(8,128)(2,1)}, u32[]{:S(2)}, u32[]{:S(2)}) collective-permute-start(bf16[2,256,1024]{2,1,0:T(8,128)(2,1)} %slice.175), channel_id=1, source_target_pairs={{0,8},{8,0},{16,24},{24,16},{1,9},{9,1},{17,25},{25,17},{2,10},{10... | collective-permute-start | bytes 3145736 | tf_op jit(solution)/shard_map/ppermute | solution.py:776
  744.0 37.7 %collective-permute-start.25 = (f32[20,2048]{1,0:T(8,128)S(1)}, f32[20,2048]{1,0:T(8,128)S(1)}, u32[]{:S(2)}, u32[]{:S(2)}) collective-permute-start(f32[20,2048]{1,0:T(8,128)S(1)} %concatenate.32), channel_id=1, source_target_pairs={{0,8},{8,0},{16,24},{24,16},{1,9},{9,1},{17,25},{25,17},{2,10},{10... | collective-permute-start | bytes 491528 | tf_op jit(solution)/shard_map/ppermute | solution.py:776
  796.4 36.0 %collective-permute-start.27 = (bf16[2,256,1024]{2,1,0:T(8,128)(2,1)S(1)}, bf16[2,256,1024]{2,1,0:T(8,128)(2,1)S(1)}, u32[]{:S(2)}, u32[]{:S(2)}) collective-permute-start(bf16[2,256,1024]{2,1,0:T(8,128)(2,1)S(1)} %slice.174), channel_id=1, source_target_pairs={{0,8},{8,0},{16,24},{24,16},{1,9},{9,1},{17,25},{25,17},{2,10},{10... | collective-permute-start | bytes 3145736 | tf_op jit(solution)/shard_map/ppermute | solution.py:776
  799.5 32.1 %collective-permute-start.28 = (bf16[256,1024]{1,0:T(8,128)(2,1)S(1)}, bf16[256,1024]{1,0:T(8,128)(2,1)}, u32[]{:S(2)}, u32[]{:S(2)}) collective-permute-start(bf16[256,1024]{1,0:T(8,128)(2,1)S(1)} %fusion.17), channel_id=1, source_target_pairs={{0,16},{8,24},{16,0},{24,8},{1,17},{9,25},{17,1},{25,9},{2,18},{10... | collective-permute-start | bytes 1572872 | tf_op jit(solution)/shard_map/ppermute | solution.py:776
  835.7 25.6 %collective-permute-start.32 = (bf16[256,1024]{1,0:T(8,128)(2,1)}, bf16[256,1024]{1,0:T(8,128)(2,1)}, u32[]{:S(2)}, u32[]{:S(2)}) collective-permute-start(bf16[256,1024]{1,0:T(8,128)(2,1)} %fusion.18), channel_id=1, source_target_pairs={{0,16},{8,24},{16,0},{24,8},{1,17},{9,25},{17,1},{25,9},{2,18},{10... | collective-permute-start | bytes 1572872 | tf_op jit(solution)/shard_map/ppermute | solution.py:776
  851.2 18.0 %all-to-all-start.8 = ((bf16[4,2,128,512]{3,2,1,0:T(8,128)(2,1)}), bf16[4,2,128,512]{3,2,1,0:T(8,128)(2,1)S(1)}, u32[]{:S(2)}, u32[]{:S(2)}) async-start(bf16[4,2,128,512]{3,2,1,0:T(8,128)(2,1)} %maximum_bitcast_fusion), calls=%async_computation.10 | async-start | bytes 2097152 | tf_op jit(solution)/shard_map/all_to_all | solution.py:1070
  (102 other events, 1336.1 us)
Sparse Core Ops, SparseCore 0:
  10.7 164.6 all-gather.3
  182.7 129.5 all-gather.5
  316.5 80.0 all-gather.7
  470.2 106.4 reduce-scatter.2
  595.1 110.6 reduce-scatter.4

commit v5 on v4

--- a/solution.py
+++ b/solution.py
@@ -588,7 +588,7 @@
         + [pltpu.SemaphoreType.DMA((2,)), pltpu.SemaphoreType.DMA((4,))],
         (normed, weights),
         0,
-        32,
+        58,
         0,
     )
 
@@ -661,7 +661,7 @@
         + [pltpu.SemaphoreType.DMA((9,)), pltpu.SemaphoreType.DMA((5,))],
         args,
         0,
-        32,
+        58,
         0,
     )
 
@@ -725,7 +725,7 @@
         + [pltpu.SemaphoreType.DMA((12,)), pltpu.SemaphoreType.DMA((4,))],
         args,
         0,
-        40,
+        58,
         0,
     )
 

time: 888 us -> 884 us (level)
  local copies, waits for them, and re-layouts: 106 us -> 83.2 us
  Pallas kernels: 167 us -> 176 us
    unnamed x183 -> x143, local copies, waits for them, and re-layouts: 66.2 us -> 47.5 us
    pallas_call x13, Pallas kernels: 156 us -> 165 us  [call(): pl.pallas_call(body, out_shape=outs, in_specs=[place_of(a) for a in args]...]
  transfers between devices with their start and end apart: 46 -> 46, of which waited for: 24 -> 26; matrix products, arithmetic and copies ran while one was open for 14% -> 14% of each run, Pallas kernels for 14% -> 15%
where the time goes in v5:
time: 884 us; the launch traced here: 875 us
  waiting for transfers between devices  389 us (44%)
  Pallas kernels  176 us (20%)
  starting transfers between devices  90.5 us (10%)
  local copies, waits for them, and re-layouts  83.2 us (9%)
  other arithmetic  74.7 us (8%)
  blocking collectives  37.8 us (4%)
  between operations  15.4 us (2%)
    ppermute x33, waiting for transfers between devices, swap(): return lax.ppermute(values, axis, [(i, i ^ step) for i in range(count)])  264 us
    pallas_call x13, Pallas kernels, call(): pl.pallas_call(body, out_shape=outs, in_specs=[place_of(a) for a in args]...  165 us
    all_to_all x3, waiting for transfers between devices, to_group(): got = lax.all_to_all(weight, GROUP, 0, 0, tiled=True)  68.1 us
    unnamed x143, local copies, waits for them, and re-layouts  47.5 us
    ppermute x33, starting transfers between devices, swap(): return lax.ppermute(values, axis, [(i, i ^ step) for i in range(count)])  32.7 us
    all_gather x1, waiting for transfers between devices, per_device(): lax.all_gather(jnp.concatenate([w_query, w_key, w_value, w_out], axis=1),...  28.9 us
    all_to_all x3, starting transfers between devices, to_group(): got = lax.all_to_all(weight, GROUP, 0, 0, tiled=True)  27.9 us
    all_to_all x3, starting transfers between devices, to_slices(): return lax.all_to_all(sent, GROUP, 0, 0, tiled=True)  21.5 us
  transfers between devices with their start and end apart: 46, of which 26 were waited for; matrix products, arithmetic and copies ran while one was open for 14% of the time, Pallas kernels for 15%

profile of v5, /device:TPU:0, one launch (start us, length us, event | category | flops | bytes accessed | tf_op | source)
XLA Modules:
  0.0 875.0 jit_solution(6860087096736654414)
XLA Ops:
  30.1 13.9 %collective-permute-done.1 = bf16[512,512]{1,0:T(8,128)(2,1)} collective-permute-done((bf16[512,512]{1,0:T(8,128)(2,1)S(1)}, bf16[512,512]{1,0:T(8,128)(2,1)}, u32[]{:S(2)}, u32[]{:S(2)}) %collective-permute-start.1) | collective-permute-done | bytes 524320 | tf_op jit(solution)/shard_map/ppermute | solution.py:776
  69.5 28.0 %all-to-all-done.1 = bf16[16,256,256]{2,1,0:T(8,128)(2,1)S(1)} async-done(((bf16[16,256,256]{2,1,0:T(8,128)(2,1)}), bf16[16,256,256]{2,1,0:T(8,128)(2,1)S(1)}, u32[]{:S(2)}, u32[]{:S(2)}) %all-to-all-start.1) | async-done | bytes 2097184 | tf_op jit(solution)/shard_map/all_to_all | solution.py:823
  100.2 44.9 %collective-permute-done.3.refs_3_.refs_2_ = bf16[8,2,256,256]{3,2,1,0:T(8,128)(2,1)S(1)} collective-permute-done((bf16[8,2,256,256]{3,2,1,0:T(8,128)(2,1)S(1)}, bf16[8,2,256,256]{3,2,1,0:T(8,128)(2,1)S(1)}, u32[]{:S(2)}, u32[]{:S(2)}) %collective-permute-start.3) | collective-permute-done | bytes 2097184 | tf_op jit(solution)/shard_map/ppermute | solution.py:776
  146.5 28.9 %all-gather.4.cloned.1.call-done.weights.refs_8_.refs_1_ = bf16[2048,2048]{1,0:T(8,128)(2,1)} async-done(((bf16[256,2048]{1,0:T(8,128)(2,1)}), bf16[2048,2048]{1,0:T(8,128)(2,1)}) %all-gather.4.cloned.1.call-update) | async-done | bytes 8388624 | tf_op jit(solution)/shard_map/all_gather | solution.py:884
  182.6 9.1 %shard_map.263 = (f32[512,512]{1,0:T(8,128)}, f32[512,512]{1,0:T(8,128)}, bf16[512,512]{1,0:T(8,128)(2,1)}, f32[2,512]{1,0:T(2,128)}) custom-call(bf16[512,2048]{1,0:T(8,128)(2,1)} %fusion.4.normed.refs_2_.refs_0_, bf16[2048,2048]{1,0:T(8,128)(2,1)} %all-gather.4.cloned.1.call-done.weights.refs_8_.refs_1_), custom_call_target="tpu_custom_call" | custom-call | flops 1000 | bytes 1000 | tf_op jit(solution)/shard_map/pallas_call | solution.py:49
  191.7 7.6 psum.14
  199.9 37.2 %all-to-all-done.2 = bf16[16,256,256]{2,1,0:T(8,128)(2,1)S(1)} async-done(((bf16[16,256,256]{2,1,0:T(8,128)(2,1)}), bf16[16,256,256]{2,1,0:T(8,128)(2,1)S(1)}, u32[]{:S(2)}, u32[]{:S(2)}) %all-to-all-start.2) | async-done | bytes 2097184 | tf_op jit(solution)/shard_map/all_to_all | solution.py:823
  237.0 17.5 %all-to-all-start.3 = ((bf16[16,256,256]{2,1,0:T(8,128)(2,1)}), bf16[16,256,256]{2,1,0:T(8,128)(2,1)}, u32[]{:S(2)}, u32[]{:S(2)}) async-start(bf16[16,256,256]{2,1,0:T(8,128)(2,1)} %get-tuple-element.148), calls=%async_computation.3 | async-start | bytes 4194304 | tf_op jit(solution)/shard_map/all_to_all | solution.py:823
  255.4 12.3 %shard_map.264 = (bf16[512,512]{1,0:T(8,128)(2,1)}, bf16[512,512]{1,0:T(8,128)(2,1)}, bf16[512,512]{1,0:T(8,128)(2,1)}, f32[4,512]{1,0:T(4,128)}, bf16[512,2048]{1,0:T(8,128)(2,1)}) custom-call(f32[512,512]{1,0:T(8,128)} %get-tuple-element.137.refs_0_.refs_10_.refs_2_, f32[512,512]{1,0:T(8,128)} %get-tuple-element.138.refs_1_.refs_11_.refs_3_, ...), custom_call_target="tpu_custom_call" | custom-call | flops 1000 | bytes 1000 | tf_op jit(solution)/shard_map/pallas_call | solution.py:49
  275.6 21.4 %collective-permute-done.5 = bf16[4,2,256,256]{3,2,1,0:T(8,128)(2,1)} collective-permute-done((bf16[4,2,256,256]{3,2,1,0:T(8,128)(2,1)}, bf16[4,2,256,256]{3,2,1,0:T(8,128)(2,1)}, u32[]{:S(2)}, u32[]{:S(2)}) %collective-permute-start.5) | collective-permute-done | bytes 1048608 | tf_op jit(solution)/shard_map/ppermute | solution.py:776
  298.4 11.9 %collective-permute-done.6 = bf16[128,2048]{1,0:T(8,128)(2,1)} collective-permute-done((bf16[128,2048]{1,0:T(8,128)(2,1)S(1)}, bf16[128,2048]{1,0:T(8,128)(2,1)}, u32[]{:S(2)}, u32[]{:S(2)}) %collective-permute-start.6) | collective-permute-done | bytes 524320 | tf_op jit(solution)/shard_map/ppermute | solution.py:776
  321.2 17.6 %all_to_all.49 = f32[16,1,128]{2,1,0:T(1,128)S(1)} all-to-all(f32[16,1,128]{2,1,0:T(1,128)S(1)} %copy.78), channel_id=1, replica_groups=mesh['t'=1,'g'=4,'p'=2,'y'=2,'c'=2] {'g','p','c'}, dimensions={0} | all-to-all | bytes 16384 | tf_op jit(solution)/shard_map/all_to_all | solution.py:814
  344.8 10.6 %shard_map.265.refs_6_ = bf16[2048,1024]{1,0:T(8,128)(2,1)S(1)} custom-call(bf16[1024,2048]{1,0:T(8,128)(2,1)S(1)} %copy-done.20, bf16[1024,2048]{1,0:T(8,128)(2,1)} %collective-permute-done.7.refs_1_, bf16[8,2,256,256]{3,2,1,0:T(8,128)(2,1)S(1)} %bitcast.107, bf16[8,2,256,256]{3,2,1,0:T(8,128)(2,1)S(1)} %copy-done.16), custom_call_target="tpu_custom_call" | custom-call | flops 1000 | bytes 1000 | tf_op jit(solution)/shard_map/pallas_call | solution.py:49
  357.5 29.7 %collective-permute-done.9 = bf16[4,2,256,256]{3,2,1,0:T(8,128)(2,1)S(1)} collective-permute-done((bf16[4,2,256,256]{3,2,1,0:T(8,128)(2,1)}, bf16[4,2,256,256]{3,2,1,0:T(8,128)(2,1)S(1)}, u32[]{:S(2)}, u32[]{:S(2)}) %collective-permute-start.9) | collective-permute-done | bytes 1048608 | tf_op jit(solution)/shard_map/ppermute | solution.py:776
  387.2 9.4 %all-gather.8.cloned.1.call-done.refs_0_ = bf16[1024,2048]{1,0:T(8,128)(2,1)} async-done(((bf16[128,2048]{1,0:T(8,128)(2,1)}), bf16[1024,2048]{1,0:T(8,128)(2,1)}) %all-gather.8.cloned.1.call-update) | async-done | bytes 4194320 | tf_op jit(solution)/shard_map/all_gather | solution.py:935
  404.0 29.7 %shard_map.266 = (bf16[2048,1024]{1,0:T(8,128)(2,1)}, bf16[2048,1024]{1,0:T(8,128)(2,1)}, bf16[2048,1024]{1,0:T(8,128)(2,1)}, f32[16,128]{1,0:T(8,128)}) custom-call(bf16[1024,2048]{1,0:T(8,128)(2,1)} %all-gather.8.cloned.1.call-done.refs_0_, bf16[1024,2048]{1,0:T(8,128)(2,1)} %collective-permute-done.10.refs_1_, bf16[8,2,256,256]{3,2,1,0:T(8,128)(2,1)} %bitcast.103, ...), custom_call_target="tpu_custom_call" | custom-call | flops 1000 | bytes 1000 | tf_op jit(solution)/shard_map/pallas_call | solution.py:49
  438.2 12.9 %shard_map.267 = bf16[1024,2176]{1,0:T(8,128)(2,1)} custom-call(bf16[2048,1024]{1,0:T(8,128)(2,1)S(1)} %copy-done.6, bf16[8,2,256,256]{3,2,1,0:T(8,128)(2,1)S(1)} %bitcast.104, bf16[8,2,256,256]{3,2,1,0:T(8,128)(2,1)S(1)} %copy-done.12, bf16[2048,1024]{1,0:T(8,128)(2,1)} %get-tuple-element.177.refs_3_.refs_2_, bf16[8,2,256,256]{3,2,1,0:T(8,128)(2,1)} %bitcast.14.refs_4_, ...), custom_call_target="tpu_custom_call" | custom-call | flops 1000 | bytes 1000 | tf_op jit(solution)/shard_map/pallas_call | solution.py:49
  451.3 13.3 %shard_map.268 = bf16[1024,2176]{1,0:T(8,128)(2,1)} custom-call(bf16[2048,1024]{1,0:T(8,128)(2,1)S(1)} %copy-done.6, bf16[8,2,256,256]{3,2,1,0:T(8,128)(2,1)S(1)} %bitcast.105, bf16[8,2,256,256]{3,2,1,0:T(8,128)(2,1)S(1)} %copy-done.12, bf16[2048,1024]{1,0:T(8,128)(2,1)} %get-tuple-element.177.refs_3_.refs_2_, bf16[8,2,256,256]{3,2,1,0:T(8,128)(2,1)} %bitcast.14.refs_4_, ...), custom_call_target="tpu_custom_call" | custom-call | flops 1000 | bytes 1000 | tf_op jit(solution)/shard_map/pallas_call | solution.py:49
  472.4 15.2 %shard_map.269 = (bf16[8,2,256,256]{3,2,1,0:T(8,128)(2,1)S(1)}, bf16[8,2,256,256]{3,2,1,0:T(8,128)(2,1)S(1)}) custom-call(bf16[1024,2048]{1,0:T(8,128)(2,1)S(1)} %copy-done.21, bf16[1024,2048]{1,0:T(8,128)(2,1)} %collective-permute-done.7.refs_1_, bf16[2048,1024]{1,0:T(8,128)(2,1)} %get-tuple-element.179.refs_2_.refs_0_), custom_call_target="tpu_custom_call" | custom-call | flops 1000 | bytes 1000 | tf_op jit(solution)/shard_map/pallas_call | solution.py:49
  488.8 7.1 shard_map.273
  505.1 15.3 %shard_map.271 = (bf16[8,2,256,256]{3,2,1,0:T(8,128)(2,1)S(1)}, bf16[8,2,256,256]{3,2,1,0:T(8,128)(2,1)}) custom-call(bf16[1024,2048]{1,0:T(8,128)(2,1)S(1)} %copy-done.4, bf16[1024,2048]{1,0:T(8,128)(2,1)} %collective-permute-done.10.refs_1_, bf16[2048,1024]{1,0:T(8,128)(2,1)} %get-tuple-element.177.refs_3_.refs_2_), custom_call_target="tpu_custom_call" | custom-call | flops 1000 | bytes 1000 | tf_op jit(solution)/shard_map/pallas_call | solution.py:49
  521.8 14.9 %shard_map.270 = (bf16[8,2,256,256]{3,2,1,0:T(8,128)(2,1)S(1)}, bf16[8,2,256,256]{3,2,1,0:T(8,128)(2,1)S(1)}) custom-call(bf16[1024,2048]{1,0:T(8,128)(2,1)S(1)} %copy-done.4, bf16[1024,2048]{1,0:T(8,128)(2,1)} %collective-permute-done.10.refs_1_, bf16[2048,1024]{1,0:T(8,128)(2,1)} %get-tuple-element.175.refs_0_.refs_2_), custom_call_target="tpu_custom_call" | custom-call | flops 1000 | bytes 1000 | tf_op jit(solution)/shard_map/pallas_call | solution.py:49
  548.4 7.9 add_convert_fusion.1
  556.2 16.9 %collective-permute-done.14 = bf16[4,2,256,256]{3,2,1,0:T(8,128)(2,1)S(1)} collective-permute-done((bf16[4,2,256,256]{3,2,1,0:T(8,128)(2,1)}, bf16[4,2,256,256]{3,2,1,0:T(8,128)(2,1)S(1)}, u32[]{:S(2)}, u32[]{:S(2)}) %collective-permute-start.14) | collective-permute-done | bytes 1048608 | tf_op jit(solution)/shard_map/ppermute | solution.py:776
  582.9 11.7 %collective-permute-done.16 = bf16[128,2048]{1,0:T(8,128)(2,1)S(1)} collective-permute-done((bf16[128,2048]{1,0:T(8,128)(2,1)}, bf16[128,2048]{1,0:T(8,128)(2,1)S(1)}, u32[]{:S(2)}, u32[]{:S(2)}) %collective-permute-start.16) | collective-permute-done | bytes 524320 | tf_op jit(solution)/shard_map/ppermute | solution.py:776
  600.4 15.8 %shard_map.274 = (f32[512,512]{1,0:T(8,128)}, f32[512,512]{1,0:T(8,128)}, bf16[512,512]{1,0:T(8,128)(2,1)}, f32[2,512]{1,0:T(2,128)}) custom-call(bf16[512,2048]{1,0:T(8,128)(2,1)} %copy-done.13, bf16[2048,2048]{1,0:T(8,128)(2,1)} %all-gather.4.cloned.1.call-done.weights.refs_8_.refs_1_, bf16[512,512]{1,0:T(8,128)(2,1)} %get-tuple-element.188.refs_2_, ...), custom_call_target="tpu_custom_call" | custom-call | flops 1000 | bytes 1000 | tf_op jit(solution)/shard_map/pallas_call | solution.py:49
  627.7 10.9 %all-to-all-start.6 = ((bf16[16,256,256]{2,1,0:T(8,128)(2,1)}), bf16[16,256,256]{2,1,0:T(8,128)(2,1)}, u32[]{:S(2)}, u32[]{:S(2)}) async-start(bf16[16,256,256]{2,1,0:T(8,128)(2,1)} %bitcast.114), calls=%async_computation.7 | async-start | bytes 4194304 | tf_op jit(solution)/shard_map/all_to_all | solution.py:852
  638.6 7.6 psum.15
  672.0 32.5 %collective-permute-done.20 = bf16[8,2,256,256]{3,2,1,0:T(8,128)(2,1)} collective-permute-done((bf16[8,2,256,256]{3,2,1,0:T(8,128)(2,1)}, bf16[8,2,256,256]{3,2,1,0:T(8,128)(2,1)}, u32[]{:S(2)}, u32[]{:S(2)}) %collective-permute-start.20) | collective-permute-done | bytes 2097184 | tf_op jit(solution)/shard_map/ppermute | solution.py:776
  717.1 16.5 %collective-permute-done.22 = bf16[4,256,1024]{2,1,0:T(8,128)(2,1)} collective-permute-done((bf16[4,256,1024]{2,1,0:T(8,128)(2,1)}, bf16[4,256,1024]{2,1,0:T(8,128)(2,1)}, u32[]{:S(2)}, u32[]{:S(2)}) %collective-permute-start.22) | collective-permute-done | bytes 2097184 | tf_op jit(solution)/shard_map/ppermute | solution.py:776
  741.4 36.0 %collective-permute-done.25 = f32[20,2048]{1,0:T(8,128)S(1)} collective-permute-done((f32[20,2048]{1,0:T(8,128)S(1)}, f32[20,2048]{1,0:T(8,128)S(1)}, u32[]{:S(2)}, u32[]{:S(2)}) %collective-permute-start.25) | collective-permute-done | bytes 163872 | tf_op jit(solution)/shard_map/ppermute | solution.py:776
  812.9 14.2 %collective-permute-done.28 = bf16[256,1024]{1,0:T(8,128)(2,1)} collective-permute-done((bf16[256,1024]{1,0:T(8,128)(2,1)S(1)}, bf16[256,1024]{1,0:T(8,128)(2,1)}, u32[]{:S(2)}, u32[]{:S(2)}) %collective-permute-start.28) | collective-permute-done | bytes 524320 | tf_op jit(solution)/shard_map/ppermute | solution.py:776
  (334 shorter events, 281.6 us)
Async XLA Ops:
  7.2 168.2 %all-gather.4.cloned.1.call-start = ((), (), s32[]{:S(2)}) async-start(), calls=%async_computation.11 | async-start | bytes 9437184 | tf_op jit(solution)/shard_map/all_gather | solution.py:884
  22.8 74.7 %all-to-all-start.1 = ((bf16[16,256,256]{2,1,0:T(8,128)(2,1)}), bf16[16,256,256]{2,1,0:T(8,128)(2,1)S(1)}, u32[]{:S(2)}, u32[]{:S(2)}) async-start(bf16[16,256,256]{2,1,0:T(8,128)(2,1)} %bitcast.115), calls=%async_computation.1 | async-start | bytes 4194304 | tf_op jit(solution)/shard_map/all_to_all | solution.py:823
  29.5 14.4 %collective-permute-start.1 = (bf16[512,512]{1,0:T(8,128)(2,1)S(1)}, bf16[512,512]{1,0:T(8,128)(2,1)}, u32[]{:S(2)}, u32[]{:S(2)}) collective-permute-start(bf16[512,512]{1,0:T(8,128)(2,1)S(1)} %copy-done.60), channel_id=1, source_target_pairs={{0,2},{2,0},{1,3},{3,1},{4,6},{6,4},{5,7},{7,5},{8,10},{10,8},{9,1... | collective-permute-start | bytes 1572872 | tf_op jit(solution)/shard_map/ppermute | solution.py:776
  30.0 28.2 %collective-permute-start = (bf16[512,512]{1,0:T(8,128)(2,1)S(1)}, bf16[512,512]{1,0:T(8,128)(2,1)}, u32[]{:S(2)}, u32[]{:S(2)}) collective-permute-start(bf16[512,512]{1,0:T(8,128)(2,1)S(1)} %copy-done.60), channel_id=1, source_target_pairs={{0,1},{1,0},{2,3},{3,2},{4,5},{5,4},{6,7},{7,6},{8,9},{9,8},{10,11... | collective-permute-start | bytes 1572872 | tf_op jit(solution)/shard_map/ppermute | solution.py:776
  44.0 18.1 %collective-permute-start.2 = (bf16[512,512]{1,0:T(8,128)(2,1)}, bf16[512,512]{1,0:T(8,128)(2,1)}, u32[]{:S(2)}, u32[]{:S(2)}) collective-permute-start(bf16[512,512]{1,0:T(8,128)(2,1)} %collective-permute-done.1), channel_id=1, source_target_pairs={{0,1},{1,0},{2,3},{3,2},{4,5},{5,4},{6,7},{7,6},{8,9},{9,8},{10,11... | collective-permute-start | bytes 1572872 | tf_op jit(solution)/shard_map/ppermute | solution.py:776
  97.5 47.6 %collective-permute-start.3 = (bf16[8,2,256,256]{3,2,1,0:T(8,128)(2,1)S(1)}, bf16[8,2,256,256]{3,2,1,0:T(8,128)(2,1)S(1)}, u32[]{:S(2)}, u32[]{:S(2)}) collective-permute-start(bf16[8,2,256,256]{3,2,1,0:T(8,128)(2,1)S(1)} %bitcast.106), channel_id=1, source_target_pairs={{0,2},{2,0},{1,3},{3,1},{4,6},{6,4},{5,7},{7,5},{8,10},{10,8},{9,1... | collective-permute-start | bytes 6291464 | tf_op jit(solution)/shard_map/ppermute | solution.py:776
  175.4 61.6 %all-to-all-start.2 = ((bf16[16,256,256]{2,1,0:T(8,128)(2,1)}), bf16[16,256,256]{2,1,0:T(8,128)(2,1)S(1)}, u32[]{:S(2)}, u32[]{:S(2)}) async-start(bf16[16,256,256]{2,1,0:T(8,128)(2,1)} %get-tuple-element.141), calls=%async_computation.2 | async-start | bytes 4194304 | tf_op jit(solution)/shard_map/all_to_all | solution.py:823
  179.1 134.1 %all-gather.6.cloned.1.call-start = ((), (), s32[]{:S(2)}) async-start(), calls=%async_computation.12 | async-start | bytes 4718592 | tf_op jit(solution)/shard_map/all_gather | solution.py:910
  237.0 79.2 %all-to-all-start.3 = ((bf16[16,256,256]{2,1,0:T(8,128)(2,1)}), bf16[16,256,256]{2,1,0:T(8,128)(2,1)}, u32[]{:S(2)}, u32[]{:S(2)}) async-start(bf16[16,256,256]{2,1,0:T(8,128)(2,1)} %get-tuple-element.148), calls=%async_computation.3 | async-start | bytes 4194304 | tf_op jit(solution)/shard_map/all_to_all | solution.py:823
  254.6 142.0 %all-gather.8.cloned.1.call-start = ((), (), s32[]{:S(2)}) async-start(), calls=%async_computation.13 | async-start | bytes 4718592 | tf_op jit(solution)/shard_map/all_gather | solution.py:935
  271.4 25.6 %collective-permute-start.5 = (bf16[4,2,256,256]{3,2,1,0:T(8,128)(2,1)}, bf16[4,2,256,256]{3,2,1,0:T(8,128)(2,1)}, u32[]{:S(2)}, u32[]{:S(2)}) collective-permute-start(bf16[4,2,256,256]{3,2,1,0:T(8,128)(2,1)} %slice.98), channel_id=1, source_target_pairs={{0,2},{2,0},{1,3},{3,1},{4,6},{6,4},{5,7},{7,5},{8,10},{10,8},{9,1... | collective-permute-start | bytes 3145736 | tf_op jit(solution)/shard_map/ppermute | solution.py:776
  316.3 260.5 %reduce-scatter.3.cloned.1.call-start = ((), (), s32[]{:S(2)}) async-start(), calls=%async_computation.14 | async-start | bytes 5013504 | tf_op jit(solution)/shard_map/reduce_scatter | solution.py:970
  316.4 23.0 %collective-permute-start.7 = (bf16[1024,2048]{1,0:T(8,128)(2,1)}, bf16[1024,2048]{1,0:T(8,128)(2,1)}, u32[]{:S(2)}, u32[]{:S(2)}) collective-permute-start(bf16[1024,2048]{1,0:T(8,128)(2,1)} %all-gather.6.cloned.1.call-done.refs_0_), channel_id=1, source_target_pairs={{0,1},{1,0},{2,3},{3,2},{4,5},{5,4},{6,7},{7,6},{8,9},{9,8},{10,11... | collective-permute-start | bytes 12582920 | tf_op jit(solution)/shard_map/ppermute | solution.py:776
  316.5 70.6 %collective-permute-start.8 = (bf16[8,2,256,256]{3,2,1,0:T(8,128)(2,1)}, bf16[8,2,256,256]{3,2,1,0:T(8,128)(2,1)}, u32[]{:S(2)}, u32[]{:S(2)}) collective-permute-start(bf16[8,2,256,256]{3,2,1,0:T(8,128)(2,1)} %bitcast.14.refs_4_), channel_id=1, source_target_pairs={{0,2},{2,0},{1,3},{3,1},{4,6},{6,4},{5,7},{7,5},{8,10},{10,8},{9,1... | collective-permute-start | bytes 6291464 | tf_op jit(solution)/shard_map/ppermute | solution.py:776
  319.1 68.1 %collective-permute-start.9 = (bf16[4,2,256,256]{3,2,1,0:T(8,128)(2,1)}, bf16[4,2,256,256]{3,2,1,0:T(8,128)(2,1)S(1)}, u32[]{:S(2)}, u32[]{:S(2)}) collective-permute-start(bf16[4,2,256,256]{3,2,1,0:T(8,128)(2,1)} %slice.100), channel_id=1, source_target_pairs={{0,2},{2,0},{1,3},{3,1},{4,6},{6,4},{5,7},{7,5},{8,10},{10,8},{9,1... | collective-permute-start | bytes 3145736 | tf_op jit(solution)/shard_map/ppermute | solution.py:776
  487.6 49.1 %collective-permute-start.12 = (bf16[8,2,256,256]{3,2,1,0:T(8,128)(2,1)S(1)}, bf16[8,2,256,256]{3,2,1,0:T(8,128)(2,1)}, u32[]{:S(2)}, u32[]{:S(2)}) collective-permute-start(bf16[8,2,256,256]{3,2,1,0:T(8,128)(2,1)S(1)} %get-tuple-element.174), channel_id=1, source_target_pairs={{0,2},{2,0},{1,3},{3,1},{4,6},{6,4},{5,7},{7,5},{8,10},{10,8},{9,1... | collective-permute-start | bytes 6291464 | tf_op jit(solution)/shard_map/ppermute | solution.py:776
  541.9 55.5 %all-to-all-start.5 = ((bf16[16,256,256]{2,1,0:T(8,128)(2,1)}), bf16[16,256,256]{2,1,0:T(8,128)(2,1)}, u32[]{:S(2)}, u32[]{:S(2)}) async-start(bf16[16,256,256]{2,1,0:T(8,128)(2,1)} %bitcast.113), calls=%async_computation.6 | async-start | bytes 4194304 | tf_op jit(solution)/shard_map/all_to_all | solution.py:852
  546.3 242.9 %reduce-scatter.5.cloned.1.call-start = ((), (), s32[]{:S(2)}) async-start(), calls=%async_computation.15 | async-start | bytes 4718592 | tf_op jit(solution)/shard_map/reduce_scatter | solution.py:989
  547.6 25.5 %collective-permute-start.14 = (bf16[4,2,256,256]{3,2,1,0:T(8,128)(2,1)}, bf16[4,2,256,256]{3,2,1,0:T(8,128)(2,1)S(1)}, u32[]{:S(2)}, u32[]{:S(2)}) collective-permute-start(bf16[4,2,256,256]{3,2,1,0:T(8,128)(2,1)} %slice.101), channel_id=1, source_target_pairs={{0,2},{2,0},{1,3},{3,1},{4,6},{6,4},{5,7},{7,5},{8,10},{10,8},{9,1... | collective-permute-start | bytes 3145736 | tf_op jit(solution)/shard_map/ppermute | solution.py:776
  598.7 25.7 %collective-permute-start.18 = (bf16[4,2,256,256]{3,2,1,0:T(8,128)(2,1)S(1)}, bf16[4,2,256,256]{3,2,1,0:T(8,128)(2,1)}, u32[]{:S(2)}, u32[]{:S(2)}) collective-permute-start(bf16[4,2,256,256]{3,2,1,0:T(8,128)(2,1)S(1)} %slice.104), channel_id=1, source_target_pairs={{0,2},{2,0},{1,3},{3,1},{4,6},{6,4},{5,7},{7,5},{8,10},{10,8},{9,1... | collective-permute-start | bytes 3145736 | tf_op jit(solution)/shard_map/ppermute | solution.py:776
  627.7 76.7 %all-to-all-start.6 = ((bf16[16,256,256]{2,1,0:T(8,128)(2,1)}), bf16[16,256,256]{2,1,0:T(8,128)(2,1)}, u32[]{:S(2)}, u32[]{:S(2)}) async-start(bf16[16,256,256]{2,1,0:T(8,128)(2,1)} %bitcast.114), calls=%async_computation.7 | async-start | bytes 4194304 | tf_op jit(solution)/shard_map/all_to_all | solution.py:852
  658.2 46.2 %collective-permute-start.20 = (bf16[8,2,256,256]{3,2,1,0:T(8,128)(2,1)}, bf16[8,2,256,256]{3,2,1,0:T(8,128)(2,1)}, u32[]{:S(2)}, u32[]{:S(2)}) collective-permute-start(bf16[8,2,256,256]{3,2,1,0:T(8,128)(2,1)} %get-tuple-element.206), channel_id=1, source_target_pairs={{0,2},{2,0},{1,3},{3,1},{4,6},{6,4},{5,7},{7,5},{8,10},{10,8},{9,1... | collective-permute-start | bytes 6291464 | tf_op jit(solution)/shard_map/ppermute | solution.py:776
  666.5 67.1 %collective-permute-start.22 = (bf16[4,256,1024]{2,1,0:T(8,128)(2,1)}, bf16[4,256,1024]{2,1,0:T(8,128)(2,1)}, u32[]{:S(2)}, u32[]{:S(2)}) collective-permute-start(bf16[4,256,1024]{2,1,0:T(8,128)(2,1)} %bitcast.22), channel_id=1, source_target_pairs={{0,4},{4,0},{1,5},{5,1},{2,6},{6,2},{3,7},{7,3},{8,12},{12,8},{9,1... | collective-permute-start | bytes 6291464 | tf_op jit(solution)/shard_map/ppermute | solution.py:776
  668.3 120.9 %collective-permute-start.24 = (bf16[4,256,1024]{2,1,0:T(8,128)(2,1)}, bf16[4,256,1024]{2,1,0:T(8,128)(2,1)}, u32[]{:S(2)}, u32[]{:S(2)}) collective-permute-start(bf16[4,256,1024]{2,1,0:T(8,128)(2,1)} %bitcast.25), channel_id=1, source_target_pairs={{0,4},{4,0},{1,5},{5,1},{2,6},{6,2},{3,7},{7,3},{8,12},{12,8},{9,1... | collective-permute-start | bytes 6291464 | tf_op jit(solution)/shard_map/ppermute | solution.py:776
  707.9 120.0 %all-to-all-start.7 = ((bf16[16,256,256]{2,1,0:T(8,128)(2,1)}), bf16[16,256,256]{2,1,0:T(8,128)(2,1)}, u32[]{:S(2)}, u32[]{:S(2)}) async-start(bf16[16,256,256]{2,1,0:T(8,128)(2,1)} %bitcast.112), calls=%async_computation.9 | async-start | bytes 4194304 | tf_op jit(solution)/shard_map/all_to_all | solution.py:852
  714.1 19.6 %collective-permute-start.21 = (bf16[128,2048]{1,0:T(8,128)(2,1)}, bf16[128,2048]{1,0:T(8,128)(2,1)S(1)}, u32[]{:S(2)}, u32[]{:S(2)}) collective-permute-start(bf16[128,2048]{1,0:T(8,128)(2,1)} %fusion.16), channel_id=1, source_target_pairs={{0,2},{2,0},{1,3},{3,1},{4,6},{6,4},{5,7},{7,5},{8,10},{10,8},{9,1... | collective-permute-start | bytes 1572872 | tf_op jit(solution)/shard_map/ppermute | solution.py:776
  737.6 51.6 %collective-permute-start.23 = (bf16[2,256,1024]{2,1,0:T(8,128)(2,1)}, bf16[2,256,1024]{2,1,0:T(8,128)(2,1)}, u32[]{:S(2)}, u32[]{:S(2)}) collective-permute-start(bf16[2,256,1024]{2,1,0:T(8,128)(2,1)} %slice.175), channel_id=1, source_target_pairs={{0,8},{8,0},{16,24},{24,16},{1,9},{9,1},{17,25},{25,17},{2,10},{10... | collective-permute-start | bytes 3145736 | tf_op jit(solution)/shard_map/ppermute | solution.py:776
  739.7 37.7 %collective-permute-start.25 = (f32[20,2048]{1,0:T(8,128)S(1)}, f32[20,2048]{1,0:T(8,128)S(1)}, u32[]{:S(2)}, u32[]{:S(2)}) collective-permute-start(f32[20,2048]{1,0:T(8,128)S(1)} %concatenate.32), channel_id=1, source_target_pairs={{0,8},{8,0},{16,24},{24,16},{1,9},{9,1},{17,25},{25,17},{2,10},{10... | collective-permute-start | bytes 491528 | tf_op jit(solution)/shard_map/ppermute | solution.py:776
  792.1 35.8 %collective-permute-start.27 = (bf16[2,256,1024]{2,1,0:T(8,128)(2,1)S(1)}, bf16[2,256,1024]{2,1,0:T(8,128)(2,1)S(1)}, u32[]{:S(2)}, u32[]{:S(2)}) collective-permute-start(bf16[2,256,1024]{2,1,0:T(8,128)(2,1)S(1)} %slice.174), channel_id=1, source_target_pairs={{0,8},{8,0},{16,24},{24,16},{1,9},{9,1},{17,25},{25,17},{2,10},{10... | collective-permute-start | bytes 3145736 | tf_op jit(solution)/shard_map/ppermute | solution.py:776
  795.2 31.9 %collective-permute-start.28 = (bf16[256,1024]{1,0:T(8,128)(2,1)S(1)}, bf16[256,1024]{1,0:T(8,128)(2,1)}, u32[]{:S(2)}, u32[]{:S(2)}) collective-permute-start(bf16[256,1024]{1,0:T(8,128)(2,1)S(1)} %fusion.17), channel_id=1, source_target_pairs={{0,16},{8,24},{16,0},{24,8},{1,17},{9,25},{17,1},{25,9},{2,18},{10... | collective-permute-start | bytes 1572872 | tf_op jit(solution)/shard_map/ppermute | solution.py:776
  831.3 25.6 %collective-permute-start.32 = (bf16[256,1024]{1,0:T(8,128)(2,1)}, bf16[256,1024]{1,0:T(8,128)(2,1)}, u32[]{:S(2)}, u32[]{:S(2)}) collective-permute-start(bf16[256,1024]{1,0:T(8,128)(2,1)} %fusion.18), channel_id=1, source_target_pairs={{0,16},{8,24},{16,0},{24,8},{1,17},{9,25},{17,1},{25,9},{2,18},{10... | collective-permute-start | bytes 1572872 | tf_op jit(solution)/shard_map/ppermute | solution.py:776
  848.1 18.0 %all-to-all-start.8 = ((bf16[4,2,128,512]{3,2,1,0:T(8,128)(2,1)}), bf16[4,2,128,512]{3,2,1,0:T(8,128)(2,1)S(1)}, u32[]{:S(2)}, u32[]{:S(2)}) async-start(bf16[4,2,128,512]{3,2,1,0:T(8,128)(2,1)} %maximum_bitcast_fusion), calls=%async_computation.10 | async-start | bytes 2097152 | tf_op jit(solution)/shard_map/all_to_all | solution.py:1070
  (82 other events, 1526.6 us)
Sparse Core Ops, SparseCore 0:
  10.7 164.6 all-gather.3
  182.1 130.1 all-gather.5
  316.4 80.0 all-gather.7
  470.3 106.4 reduce-scatter.2
  594.7 107.7 reduce-scatter.4

commit v6 on v5

--- a/solution.py
+++ b/solution.py
@@ -410,7 +410,7 @@
         + [pltpu.SemaphoreType.DMA((2,))] * bool(tail),
         [a for t in triples for a in t] + list(tail),
         2 * n * rows * model * hidden,
-        40,
+        58 if tail else 40,
         2 * (n * rows * hidden + n * model * hidden + rows * model),
     )
 

time: 884 us -> 882 us (level)
    unnamed x143 -> x127, local copies, waits for them, and re-layouts: 47.5 us -> 40 us
  transfers between devices with their start and end apart: 46 -> 46, of which waited for: 26 -> 25; matrix products, arithmetic and copies ran while one was open for 14% -> 14% of each run, Pallas kernels for 15% -> 15%
where the time goes in v6:
time: 882 us; the launch traced here: 874 us
  waiting for transfers between devices  388 us (44%)
  Pallas kernels  177 us (20%)
  starting transfers between devices  91.1 us (10%)
  local copies, waits for them, and re-layouts  79.5 us (9%)
  other arithmetic  76.5 us (9%)
  blocking collectives  37.7 us (4%)
  between operations  15.3 us (2%)
    ppermute x33, waiting for transfers between devices, swap(): return lax.ppermute(values, axis, [(i, i ^ step) for i in range(count)])  264 us
    pallas_call x13, Pallas kernels, call(): pl.pallas_call(body, out_shape=outs, in_specs=[place_of(a) for a in args]...  166 us
    all_to_all x3, waiting for transfers between devices, to_group(): got = lax.all_to_all(weight, GROUP, 0, 0, tiled=True)  66.9 us
    unnamed x127, local copies, waits for them, and re-layouts  40 us
    ppermute x33, starting transfers between devices, swap(): return lax.ppermute(values, axis, [(i, i ^ step) for i in range(count)])  32.7 us
    all_gather x1, waiting for transfers between devices, per_device(): lax.all_gather(jnp.concatenate([w_query, w_key, w_value, w_out], axis=1),...  28.9 us
    all_to_all x3, starting transfers between devices, to_group(): got = lax.all_to_all(weight, GROUP, 0, 0, tiled=True)  28.6 us
    all_to_all x3, starting transfers between devices, to_slices(): return lax.all_to_all(sent, GROUP, 0, 0, tiled=True)  21.4 us
  transfers between devices with their start and end apart: 46, of which 25 were waited for; matrix products, arithmetic and copies ran while one was open for 14% of the time, Pallas kernels for 15%

profile of v6, /device:TPU:0, one launch (start us, length us, event | category | flops | bytes accessed | tf_op | source)
XLA Modules:
  0.0 873.7 jit_solution(7512993617375662203)
XLA Ops:
  30.1 13.9 %collective-permute-done.1 = bf16[512,512]{1,0:T(8,128)(2,1)} collective-permute-done((bf16[512,512]{1,0:T(8,128)(2,1)S(1)}, bf16[512,512]{1,0:T(8,128)(2,1)}, u32[]{:S(2)}, u32[]{:S(2)}) %collective-permute-start.1) | collective-permute-done | bytes 524320 | tf_op jit(solution)/shard_map/ppermute | solution.py:776
  69.6 27.9 %all-to-all-done.1 = bf16[16,256,256]{2,1,0:T(8,128)(2,1)S(1)} async-done(((bf16[16,256,256]{2,1,0:T(8,128)(2,1)}), bf16[16,256,256]{2,1,0:T(8,128)(2,1)S(1)}, u32[]{:S(2)}, u32[]{:S(2)}) %all-to-all-start.1) | async-done | bytes 2097184 | tf_op jit(solution)/shard_map/all_to_all | solution.py:823
  98.9 46.2 %collective-permute-done.3.refs_3_.refs_2_ = bf16[8,2,256,256]{3,2,1,0:T(8,128)(2,1)S(1)} collective-permute-done((bf16[8,2,256,256]{3,2,1,0:T(8,128)(2,1)S(1)}, bf16[8,2,256,256]{3,2,1,0:T(8,128)(2,1)S(1)}, u32[]{:S(2)}, u32[]{:S(2)}) %collective-permute-start.3) | collective-permute-done | bytes 2097184 | tf_op jit(solution)/shard_map/ppermute | solution.py:776
  146.5 28.9 %all-gather.4.cloned.1.call-done.weights.refs_8_.refs_1_ = bf16[2048,2048]{1,0:T(8,128)(2,1)} async-done(((bf16[256,2048]{1,0:T(8,128)(2,1)}), bf16[2048,2048]{1,0:T(8,128)(2,1)}) %all-gather.4.cloned.1.call-update) | async-done | bytes 8388624 | tf_op jit(solution)/shard_map/all_gather | solution.py:884
  183.3 9.1 %shard_map.263 = (f32[512,512]{1,0:T(8,128)}, f32[512,512]{1,0:T(8,128)}, bf16[512,512]{1,0:T(8,128)(2,1)}, f32[2,512]{1,0:T(2,128)}) custom-call(bf16[512,2048]{1,0:T(8,128)(2,1)} %fusion.4.normed.refs_2_.refs_0_, bf16[2048,2048]{1,0:T(8,128)(2,1)} %all-gather.4.cloned.1.call-done.weights.refs_8_.refs_1_), custom_call_target="tpu_custom_call" | custom-call | flops 1000 | bytes 1000 | tf_op jit(solution)/shard_map/pallas_call | solution.py:49
  192.4 7.5 psum.14
  200.5 37.3 %all-to-all-done.2 = bf16[16,256,256]{2,1,0:T(8,128)(2,1)} async-done(((bf16[16,256,256]{2,1,0:T(8,128)(2,1)}), bf16[16,256,256]{2,1,0:T(8,128)(2,1)}, u32[]{:S(2)}, u32[]{:S(2)}) %all-to-all-start.2) | async-done | bytes 2097184 | tf_op jit(solution)/shard_map/all_to_all | solution.py:823
  237.8 17.5 %all-to-all-start.3 = ((bf16[16,256,256]{2,1,0:T(8,128)(2,1)}), bf16[16,256,256]{2,1,0:T(8,128)(2,1)}, u32[]{:S(2)}, u32[]{:S(2)}) async-start(bf16[16,256,256]{2,1,0:T(8,128)(2,1)} %get-tuple-element.148), calls=%async_computation.3 | async-start | bytes 4194304 | tf_op jit(solution)/shard_map/all_to_all | solution.py:823
  256.2 12.3 %shard_map.264 = (bf16[512,512]{1,0:T(8,128)(2,1)}, bf16[512,512]{1,0:T(8,128)(2,1)}, bf16[512,512]{1,0:T(8,128)(2,1)}, f32[4,512]{1,0:T(4,128)}, bf16[512,2048]{1,0:T(8,128)(2,1)}) custom-call(f32[512,512]{1,0:T(8,128)} %get-tuple-element.137.refs_0_.refs_10_.refs_2_, f32[512,512]{1,0:T(8,128)} %get-tuple-element.138.refs_1_.refs_11_.refs_3_, ...), custom_call_target="tpu_custom_call" | custom-call | flops 1000 | bytes 1000 | tf_op jit(solution)/shard_map/pallas_call | solution.py:49
  277.5 21.5 %collective-permute-done.5 = bf16[4,2,256,256]{3,2,1,0:T(8,128)(2,1)} collective-permute-done((bf16[4,2,256,256]{3,2,1,0:T(8,128)(2,1)}, bf16[4,2,256,256]{3,2,1,0:T(8,128)(2,1)}, u32[]{:S(2)}, u32[]{:S(2)}) %collective-permute-start.5) | collective-permute-done | bytes 1048608 | tf_op jit(solution)/shard_map/ppermute | solution.py:776
  300.3 11.9 %collective-permute-done.6 = bf16[128,2048]{1,0:T(8,128)(2,1)} collective-permute-done((bf16[128,2048]{1,0:T(8,128)(2,1)S(1)}, bf16[128,2048]{1,0:T(8,128)(2,1)}, u32[]{:S(2)}, u32[]{:S(2)}) %collective-permute-start.6) | collective-permute-done | bytes 524320 | tf_op jit(solution)/shard_map/ppermute | solution.py:776
  323.1 17.6 %all_to_all.49 = f32[16,1,128]{2,1,0:T(1,128)S(1)} all-to-all(f32[16,1,128]{2,1,0:T(1,128)S(1)} %copy.78), channel_id=1, replica_groups=mesh['t'=1,'g'=4,'p'=2,'y'=2,'c'=2] {'g','p','c'}, dimensions={0} | all-to-all | bytes 16384 | tf_op jit(solution)/shard_map/all_to_all | solution.py:814
  345.1 10.6 %shard_map.265.refs_6_ = bf16[2048,1024]{1,0:T(8,128)(2,1)S(1)} custom-call(bf16[1024,2048]{1,0:T(8,128)(2,1)S(1)} %copy-done.12, bf16[1024,2048]{1,0:T(8,128)(2,1)} %collective-permute-done.7.refs_1_, bf16[8,2,256,256]{3,2,1,0:T(8,128)(2,1)S(1)} %bitcast.102, bf16[8,2,256,256]{3,2,1,0:T(8,128)(2,1)S(1)} %copy-done.8), custom_call_target="tpu_custom_call" | custom-call | flops 1000 | bytes 1000 | tf_op jit(solution)/shard_map/pallas_call | solution.py:49
  357.8 30.2 %collective-permute-done.9 = bf16[4,2,256,256]{3,2,1,0:T(8,128)(2,1)} collective-permute-done((bf16[4,2,256,256]{3,2,1,0:T(8,128)(2,1)}, bf16[4,2,256,256]{3,2,1,0:T(8,128)(2,1)}, u32[]{:S(2)}, u32[]{:S(2)}) %collective-permute-start.9) | collective-permute-done | bytes 1048608 | tf_op jit(solution)/shard_map/ppermute | solution.py:776
  387.9 9.2 %all-gather.8.cloned.1.call-done.refs_0_ = bf16[1024,2048]{1,0:T(8,128)(2,1)} async-done(((bf16[128,2048]{1,0:T(8,128)(2,1)}), bf16[1024,2048]{1,0:T(8,128)(2,1)}) %all-gather.8.cloned.1.call-update) | async-done | bytes 4194320 | tf_op jit(solution)/shard_map/all_gather | solution.py:935
  404.6 29.7 %shard_map.266 = (bf16[2048,1024]{1,0:T(8,128)(2,1)}, bf16[2048,1024]{1,0:T(8,128)(2,1)}, bf16[2048,1024]{1,0:T(8,128)(2,1)}, f32[16,128]{1,0:T(8,128)}) custom-call(bf16[1024,2048]{1,0:T(8,128)(2,1)} %all-gather.8.cloned.1.call-done.refs_0_, bf16[1024,2048]{1,0:T(8,128)(2,1)} %collective-permute-done.10.refs_1_, ...), custom_call_target="tpu_custom_call" | custom-call | flops 1000 | bytes 1000 | tf_op jit(solution)/shard_map/pallas_call | solution.py:49
  434.3 13.8 %shard_map.267 = bf16[1024,2176]{1,0:T(8,128)(2,1)} custom-call(bf16[2048,1024]{1,0:T(8,128)(2,1)} %get-tuple-element.175.refs_0_.refs_2_, bf16[8,2,256,256]{3,2,1,0:T(8,128)(2,1)} %bitcast.7.refs_2_.refs_1_, bf16[8,2,256,256]{3,2,1,0:T(8,128)(2,1)} %copy-done.33, bf16[2048,1024]{1,0:T(8,128)(2,1)} %get-tuple-element.177.refs_3_.refs_2_, ...), custom_call_target="tpu_custom_call" | custom-call | flops 1000 | bytes 1000 | tf_op jit(solution)/shard_map/pallas_call | solution.py:49
  448.3 13.7 %shard_map.268 = bf16[1024,2176]{1,0:T(8,128)(2,1)} custom-call(bf16[2048,1024]{1,0:T(8,128)(2,1)} %get-tuple-element.175.refs_0_.refs_2_, bf16[8,2,256,256]{3,2,1,0:T(8,128)(2,1)} %bitcast.7.refs_2_.refs_1_, bf16[8,2,256,256]{3,2,1,0:T(8,128)(2,1)} %copy-done.33, bf16[2048,1024]{1,0:T(8,128)(2,1)} %get-tuple-element.177.refs_3_.refs_2_, ...), custom_call_target="tpu_custom_call" | custom-call | flops 1000 | bytes 1000 | tf_op jit(solution)/shard_map/pallas_call | solution.py:49
  471.1 15.2 %shard_map.269 = (bf16[8,2,256,256]{3,2,1,0:T(8,128)(2,1)S(1)}, bf16[8,2,256,256]{3,2,1,0:T(8,128)(2,1)S(1)}) custom-call(bf16[1024,2048]{1,0:T(8,128)(2,1)S(1)} %copy-done.13, bf16[1024,2048]{1,0:T(8,128)(2,1)} %collective-permute-done.7.refs_1_, bf16[2048,1024]{1,0:T(8,128)(2,1)} %get-tuple-element.179.refs_2_.refs_0_), custom_call_target="tpu_custom_call" | custom-call | flops 1000 | bytes 1000 | tf_op jit(solution)/shard_map/pallas_call | solution.py:49
  487.5 7.1 shard_map.273
  503.8 15.3 %shard_map.271 = (bf16[8,2,256,256]{3,2,1,0:T(8,128)(2,1)S(1)}, bf16[8,2,256,256]{3,2,1,0:T(8,128)(2,1)}) custom-call(bf16[1024,2048]{1,0:T(8,128)(2,1)S(1)} %copy-done.2, bf16[1024,2048]{1,0:T(8,128)(2,1)} %collective-permute-done.10.refs_1_, bf16[2048,1024]{1,0:T(8,128)(2,1)} %get-tuple-element.177.refs_3_.refs_2_), custom_call_target="tpu_custom_call" | custom-call | flops 1000 | bytes 1000 | tf_op jit(solution)/shard_map/pallas_call | solution.py:49
  520.4 14.9 %shard_map.270 = (bf16[8,2,256,256]{3,2,1,0:T(8,128)(2,1)S(1)}, bf16[8,2,256,256]{3,2,1,0:T(8,128)(2,1)S(1)}) custom-call(bf16[1024,2048]{1,0:T(8,128)(2,1)S(1)} %copy-done.2, bf16[1024,2048]{1,0:T(8,128)(2,1)} %collective-permute-done.10.refs_1_, bf16[2048,1024]{1,0:T(8,128)(2,1)} %get-tuple-element.175.refs_0_.refs_2_), custom_call_target="tpu_custom_call" | custom-call | flops 1000 | bytes 1000 | tf_op jit(solution)/shard_map/pallas_call | solution.py:49
  546.9 7.9 add_convert_fusion.1
  554.8 17.0 %collective-permute-done.14 = bf16[4,2,256,256]{3,2,1,0:T(8,128)(2,1)S(1)} collective-permute-done((bf16[4,2,256,256]{3,2,1,0:T(8,128)(2,1)}, bf16[4,2,256,256]{3,2,1,0:T(8,128)(2,1)S(1)}, u32[]{:S(2)}, u32[]{:S(2)}) %collective-permute-start.14) | collective-permute-done | bytes 1048608 | tf_op jit(solution)/shard_map/ppermute | solution.py:776
  581.7 11.7 %collective-permute-done.16 = bf16[128,2048]{1,0:T(8,128)(2,1)S(1)} collective-permute-done((bf16[128,2048]{1,0:T(8,128)(2,1)}, bf16[128,2048]{1,0:T(8,128)(2,1)S(1)}, u32[]{:S(2)}, u32[]{:S(2)}) %collective-permute-start.16) | collective-permute-done | bytes 524320 | tf_op jit(solution)/shard_map/ppermute | solution.py:776
  599.2 15.9 %shard_map.274 = (f32[512,512]{1,0:T(8,128)}, f32[512,512]{1,0:T(8,128)}, bf16[512,512]{1,0:T(8,128)(2,1)}, f32[2,512]{1,0:T(2,128)}) custom-call(bf16[512,2048]{1,0:T(8,128)(2,1)} %copy-done.5, bf16[2048,2048]{1,0:T(8,128)(2,1)} %all-gather.4.cloned.1.call-done.weights.refs_8_.refs_1_, bf16[512,512]{1,0:T(8,128)(2,1)} %get-tuple-element.188.refs_2_, ...), custom_call_target="tpu_custom_call" | custom-call | flops 1000 | bytes 1000 | tf_op jit(solution)/shard_map/pallas_call | solution.py:49
  626.6 10.8 %all-to-all-start.6 = ((bf16[16,256,256]{2,1,0:T(8,128)(2,1)}), bf16[16,256,256]{2,1,0:T(8,128)(2,1)}, u32[]{:S(2)}, u32[]{:S(2)}) async-start(bf16[16,256,256]{2,1,0:T(8,128)(2,1)} %bitcast.109), calls=%async_computation.7 | async-start | bytes 4194304 | tf_op jit(solution)/shard_map/all_to_all | solution.py:852
  637.4 7.4 psum.15
  670.7 32.5 %collective-permute-done.20 = bf16[8,2,256,256]{3,2,1,0:T(8,128)(2,1)} collective-permute-done((bf16[8,2,256,256]{3,2,1,0:T(8,128)(2,1)}, bf16[8,2,256,256]{3,2,1,0:T(8,128)(2,1)}, u32[]{:S(2)}, u32[]{:S(2)}) %collective-permute-start.20) | collective-permute-done | bytes 2097184 | tf_op jit(solution)/shard_map/ppermute | solution.py:776
  715.7 16.6 %collective-permute-done.22 = bf16[4,256,1024]{2,1,0:T(8,128)(2,1)} collective-permute-done((bf16[4,256,1024]{2,1,0:T(8,128)(2,1)}, bf16[4,256,1024]{2,1,0:T(8,128)(2,1)}, u32[]{:S(2)}, u32[]{:S(2)}) %collective-permute-start.22) | collective-permute-done | bytes 2097184 | tf_op jit(solution)/shard_map/ppermute | solution.py:776
  740.1 36.0 %collective-permute-done.25 = f32[20,2048]{1,0:T(8,128)S(1)} collective-permute-done((f32[20,2048]{1,0:T(8,128)S(1)}, f32[20,2048]{1,0:T(8,128)S(1)}, u32[]{:S(2)}, u32[]{:S(2)}) %collective-permute-start.25) | collective-permute-done | bytes 163872 | tf_op jit(solution)/shard_map/ppermute | solution.py:776
  811.7 14.2 %collective-permute-done.28 = bf16[256,1024]{1,0:T(8,128)(2,1)} collective-permute-done((bf16[256,1024]{1,0:T(8,128)(2,1)S(1)}, bf16[256,1024]{1,0:T(8,128)(2,1)}, u32[]{:S(2)}, u32[]{:S(2)}) %collective-permute-start.28) | collective-permute-done | bytes 524320 | tf_op jit(solution)/shard_map/ppermute | solution.py:776
  (318 shorter events, 277.1 us)
Async XLA Ops:
  7.2 168.2 %all-gather.4.cloned.1.call-start = ((), (), s32[]{:S(2)}) async-start(), calls=%async_computation.11 | async-start | bytes 9437184 | tf_op jit(solution)/shard_map/all_gather | solution.py:884
  22.8 74.7 %all-to-all-start.1 = ((bf16[16,256,256]{2,1,0:T(8,128)(2,1)}), bf16[16,256,256]{2,1,0:T(8,128)(2,1)S(1)}, u32[]{:S(2)}, u32[]{:S(2)}) async-start(bf16[16,256,256]{2,1,0:T(8,128)(2,1)} %bitcast.110), calls=%async_computation.1 | async-start | bytes 4194304 | tf_op jit(solution)/shard_map/all_to_all | solution.py:823
  29.5 14.4 %collective-permute-start.1 = (bf16[512,512]{1,0:T(8,128)(2,1)S(1)}, bf16[512,512]{1,0:T(8,128)(2,1)}, u32[]{:S(2)}, u32[]{:S(2)}) collective-permute-start(bf16[512,512]{1,0:T(8,128)(2,1)S(1)} %copy-done.52), channel_id=1, source_target_pairs={{0,2},{2,0},{1,3},{3,1},{4,6},{6,4},{5,7},{7,5},{8,10},{10,8},{9,1... | collective-permute-start | bytes 1572872 | tf_op jit(solution)/shard_map/ppermute | solution.py:776
  30.0 28.3 %collective-permute-start = (bf16[512,512]{1,0:T(8,128)(2,1)S(1)}, bf16[512,512]{1,0:T(8,128)(2,1)}, u32[]{:S(2)}, u32[]{:S(2)}) collective-permute-start(bf16[512,512]{1,0:T(8,128)(2,1)S(1)} %copy-done.52), channel_id=1, source_target_pairs={{0,1},{1,0},{2,3},{3,2},{4,5},{5,4},{6,7},{7,6},{8,9},{9,8},{10,11... | collective-permute-start | bytes 1572872 | tf_op jit(solution)/shard_map/ppermute | solution.py:776
  44.0 18.1 %collective-permute-start.2 = (bf16[512,512]{1,0:T(8,128)(2,1)}, bf16[512,512]{1,0:T(8,128)(2,1)}, u32[]{:S(2)}, u32[]{:S(2)}) collective-permute-start(bf16[512,512]{1,0:T(8,128)(2,1)} %collective-permute-done.1), channel_id=1, source_target_pairs={{0,1},{1,0},{2,3},{3,2},{4,5},{5,4},{6,7},{7,6},{8,9},{9,8},{10,11... | collective-permute-start | bytes 1572872 | tf_op jit(solution)/shard_map/ppermute | solution.py:776
  97.5 47.6 %collective-permute-start.3 = (bf16[8,2,256,256]{3,2,1,0:T(8,128)(2,1)S(1)}, bf16[8,2,256,256]{3,2,1,0:T(8,128)(2,1)S(1)}, u32[]{:S(2)}, u32[]{:S(2)}) collective-permute-start(bf16[8,2,256,256]{3,2,1,0:T(8,128)(2,1)S(1)} %bitcast.101), channel_id=1, source_target_pairs={{0,2},{2,0},{1,3},{3,1},{4,6},{6,4},{5,7},{7,5},{8,10},{10,8},{9,1... | collective-permute-start | bytes 6291464 | tf_op jit(solution)/shard_map/ppermute | solution.py:776
  175.4 62.4 %all-to-all-start.2 = ((bf16[16,256,256]{2,1,0:T(8,128)(2,1)}), bf16[16,256,256]{2,1,0:T(8,128)(2,1)}, u32[]{:S(2)}, u32[]{:S(2)}) async-start(bf16[16,256,256]{2,1,0:T(8,128)(2,1)} %get-tuple-element.141), calls=%async_computation.2 | async-start | bytes 4194304 | tf_op jit(solution)/shard_map/all_to_all | solution.py:823
  179.8 135.4 %all-gather.6.cloned.1.call-start = ((), (), s32[]{:S(2)}) async-start(), calls=%async_computation.12 | async-start | bytes 4718592 | tf_op jit(solution)/shard_map/all_gather | solution.py:910
  237.8 79.2 %all-to-all-start.3 = ((bf16[16,256,256]{2,1,0:T(8,128)(2,1)}), bf16[16,256,256]{2,1,0:T(8,128)(2,1)}, u32[]{:S(2)}, u32[]{:S(2)}) async-start(bf16[16,256,256]{2,1,0:T(8,128)(2,1)} %get-tuple-element.148), calls=%async_computation.3 | async-start | bytes 4194304 | tf_op jit(solution)/shard_map/all_to_all | solution.py:823
  255.3 141.8 %all-gather.8.cloned.1.call-start = ((), (), s32[]{:S(2)}) async-start(), calls=%async_computation.13 | async-start | bytes 4718592 | tf_op jit(solution)/shard_map/all_gather | solution.py:935
  273.4 25.6 %collective-permute-start.5 = (bf16[4,2,256,256]{3,2,1,0:T(8,128)(2,1)}, bf16[4,2,256,256]{3,2,1,0:T(8,128)(2,1)}, u32[]{:S(2)}, u32[]{:S(2)}) collective-permute-start(bf16[4,2,256,256]{3,2,1,0:T(8,128)(2,1)} %slice.98), channel_id=1, source_target_pairs={{0,2},{2,0},{1,3},{3,1},{4,6},{6,4},{5,7},{7,5},{8,10},{10,8},{9,1... | collective-permute-start | bytes 3145736 | tf_op jit(solution)/shard_map/ppermute | solution.py:776
  317.0 258.6 %reduce-scatter.3.cloned.1.call-start = ((), (), s32[]{:S(2)}) async-start(), calls=%async_computation.14 | async-start | bytes 5013504 | tf_op jit(solution)/shard_map/reduce_scatter | solution.py:970
  317.0 24.3 %collective-permute-start.7 = (bf16[1024,2048]{1,0:T(8,128)(2,1)}, bf16[1024,2048]{1,0:T(8,128)(2,1)}, u32[]{:S(2)}, u32[]{:S(2)}) collective-permute-start(bf16[1024,2048]{1,0:T(8,128)(2,1)} %all-gather.6.cloned.1.call-done.refs_0_), channel_id=1, source_target_pairs={{0,1},{1,0},{2,3},{3,2},{4,5},{5,4},{6,7},{7,6},{8,9},{9,8},{10,11... | collective-permute-start | bytes 12582920 | tf_op jit(solution)/shard_map/ppermute | solution.py:776
  317.2 70.7 %collective-permute-start.8 = (bf16[8,2,256,256]{3,2,1,0:T(8,128)(2,1)}, bf16[8,2,256,256]{3,2,1,0:T(8,128)(2,1)}, u32[]{:S(2)}, u32[]{:S(2)}) collective-permute-start(bf16[8,2,256,256]{3,2,1,0:T(8,128)(2,1)} %bitcast.14.refs_4_), channel_id=1, source_target_pairs={{0,2},{2,0},{1,3},{3,1},{4,6},{6,4},{5,7},{7,5},{8,10},{10,8},{9,1... | collective-permute-start | bytes 6291464 | tf_op jit(solution)/shard_map/ppermute | solution.py:776
  321.0 67.0 %collective-permute-start.9 = (bf16[4,2,256,256]{3,2,1,0:T(8,128)(2,1)}, bf16[4,2,256,256]{3,2,1,0:T(8,128)(2,1)}, u32[]{:S(2)}, u32[]{:S(2)}) collective-permute-start(bf16[4,2,256,256]{3,2,1,0:T(8,128)(2,1)} %slice.100), channel_id=1, source_target_pairs={{0,2},{2,0},{1,3},{3,1},{4,6},{6,4},{5,7},{7,5},{8,10},{10,8},{9,1... | collective-permute-start | bytes 3145736 | tf_op jit(solution)/shard_map/ppermute | solution.py:776
  486.3 49.1 %collective-permute-start.12 = (bf16[8,2,256,256]{3,2,1,0:T(8,128)(2,1)S(1)}, bf16[8,2,256,256]{3,2,1,0:T(8,128)(2,1)}, u32[]{:S(2)}, u32[]{:S(2)}) collective-permute-start(bf16[8,2,256,256]{3,2,1,0:T(8,128)(2,1)S(1)} %get-tuple-element.174), channel_id=1, source_target_pairs={{0,2},{2,0},{1,3},{3,1},{4,6},{6,4},{5,7},{7,5},{8,10},{10,8},{9,1... | collective-permute-start | bytes 6291464 | tf_op jit(solution)/shard_map/ppermute | solution.py:776
  540.5 55.6 %all-to-all-start.5 = ((bf16[16,256,256]{2,1,0:T(8,128)(2,1)}), bf16[16,256,256]{2,1,0:T(8,128)(2,1)}, u32[]{:S(2)}, u32[]{:S(2)}) async-start(bf16[16,256,256]{2,1,0:T(8,128)(2,1)} %bitcast.108), calls=%async_computation.6 | async-start | bytes 4194304 | tf_op jit(solution)/shard_map/all_to_all | solution.py:852
  544.9 243.0 %reduce-scatter.5.cloned.1.call-start = ((), (), s32[]{:S(2)}) async-start(), calls=%async_computation.15 | async-start | bytes 4718592 | tf_op jit(solution)/shard_map/reduce_scatter | solution.py:989
  546.2 25.5 %collective-permute-start.14 = (bf16[4,2,256,256]{3,2,1,0:T(8,128)(2,1)}, bf16[4,2,256,256]{3,2,1,0:T(8,128)(2,1)S(1)}, u32[]{:S(2)}, u32[]{:S(2)}) collective-permute-start(bf16[4,2,256,256]{3,2,1,0:T(8,128)(2,1)} %slice.101), channel_id=1, source_target_pairs={{0,2},{2,0},{1,3},{3,1},{4,6},{6,4},{5,7},{7,5},{8,10},{10,8},{9,1... | collective-permute-start | bytes 3145736 | tf_op jit(solution)/shard_map/ppermute | solution.py:776
  597.4 26.0 %collective-permute-start.18 = (bf16[4,2,256,256]{3,2,1,0:T(8,128)(2,1)S(1)}, bf16[4,2,256,256]{3,2,1,0:T(8,128)(2,1)}, u32[]{:S(2)}, u32[]{:S(2)}) collective-permute-start(bf16[4,2,256,256]{3,2,1,0:T(8,128)(2,1)S(1)} %slice.104), channel_id=1, source_target_pairs={{0,2},{2,0},{1,3},{3,1},{4,6},{6,4},{5,7},{7,5},{8,10},{10,8},{9,1... | collective-permute-start | bytes 3145736 | tf_op jit(solution)/shard_map/ppermute | solution.py:776
  626.6 76.6 %all-to-all-start.6 = ((bf16[16,256,256]{2,1,0:T(8,128)(2,1)}), bf16[16,256,256]{2,1,0:T(8,128)(2,1)}, u32[]{:S(2)}, u32[]{:S(2)}) async-start(bf16[16,256,256]{2,1,0:T(8,128)(2,1)} %bitcast.109), calls=%async_computation.7 | async-start | bytes 4194304 | tf_op jit(solution)/shard_map/all_to_all | solution.py:852
  656.8 46.3 %collective-permute-start.20 = (bf16[8,2,256,256]{3,2,1,0:T(8,128)(2,1)}, bf16[8,2,256,256]{3,2,1,0:T(8,128)(2,1)}, u32[]{:S(2)}, u32[]{:S(2)}) collective-permute-start(bf16[8,2,256,256]{3,2,1,0:T(8,128)(2,1)} %get-tuple-element.206), channel_id=1, source_target_pairs={{0,2},{2,0},{1,3},{3,1},{4,6},{6,4},{5,7},{7,5},{8,10},{10,8},{9,1... | collective-permute-start | bytes 6291464 | tf_op jit(solution)/shard_map/ppermute | solution.py:776
  665.2 67.1 %collective-permute-start.22 = (bf16[4,256,1024]{2,1,0:T(8,128)(2,1)}, bf16[4,256,1024]{2,1,0:T(8,128)(2,1)}, u32[]{:S(2)}, u32[]{:S(2)}) collective-permute-start(bf16[4,256,1024]{2,1,0:T(8,128)(2,1)} %bitcast.22), channel_id=1, source_target_pairs={{0,4},{4,0},{1,5},{5,1},{2,6},{6,2},{3,7},{7,3},{8,12},{12,8},{9,1... | collective-permute-start | bytes 6291464 | tf_op jit(solution)/shard_map/ppermute | solution.py:776
  667.0 120.9 %collective-permute-start.24 = (bf16[4,256,1024]{2,1,0:T(8,128)(2,1)}, bf16[4,256,1024]{2,1,0:T(8,128)(2,1)}, u32[]{:S(2)}, u32[]{:S(2)}) collective-permute-start(bf16[4,256,1024]{2,1,0:T(8,128)(2,1)} %bitcast.25), channel_id=1, source_target_pairs={{0,4},{4,0},{1,5},{5,1},{2,6},{6,2},{3,7},{7,3},{8,12},{12,8},{9,1... | collective-permute-start | bytes 6291464 | tf_op jit(solution)/shard_map/ppermute | solution.py:776
  706.7 120.0 %all-to-all-start.7 = ((bf16[16,256,256]{2,1,0:T(8,128)(2,1)}), bf16[16,256,256]{2,1,0:T(8,128)(2,1)}, u32[]{:S(2)}, u32[]{:S(2)}) async-start(bf16[16,256,256]{2,1,0:T(8,128)(2,1)} %bitcast.107), calls=%async_computation.9 | async-start | bytes 4194304 | tf_op jit(solution)/shard_map/all_to_all | solution.py:852
  712.8 19.5 %collective-permute-start.21 = (bf16[128,2048]{1,0:T(8,128)(2,1)}, bf16[128,2048]{1,0:T(8,128)(2,1)S(1)}, u32[]{:S(2)}, u32[]{:S(2)}) collective-permute-start(bf16[128,2048]{1,0:T(8,128)(2,1)} %fusion.16), channel_id=1, source_target_pairs={{0,2},{2,0},{1,3},{3,1},{4,6},{6,4},{5,7},{7,5},{8,10},{10,8},{9,1... | collective-permute-start | bytes 1572872 | tf_op jit(solution)/shard_map/ppermute | solution.py:776
  736.3 51.6 %collective-permute-start.23 = (bf16[2,256,1024]{2,1,0:T(8,128)(2,1)}, bf16[2,256,1024]{2,1,0:T(8,128)(2,1)}, u32[]{:S(2)}, u32[]{:S(2)}) collective-permute-start(bf16[2,256,1024]{2,1,0:T(8,128)(2,1)} %slice.175), channel_id=1, source_target_pairs={{0,8},{8,0},{16,24},{24,16},{1,9},{9,1},{17,25},{25,17},{2,10},{10... | collective-permute-start | bytes 3145736 | tf_op jit(solution)/shard_map/ppermute | solution.py:776
  738.4 37.7 %collective-permute-start.25 = (f32[20,2048]{1,0:T(8,128)S(1)}, f32[20,2048]{1,0:T(8,128)S(1)}, u32[]{:S(2)}, u32[]{:S(2)}) collective-permute-start(f32[20,2048]{1,0:T(8,128)S(1)} %concatenate.32), channel_id=1, source_target_pairs={{0,8},{8,0},{16,24},{24,16},{1,9},{9,1},{17,25},{25,17},{2,10},{10... | collective-permute-start | bytes 491528 | tf_op jit(solution)/shard_map/ppermute | solution.py:776
  790.8 35.8 %collective-permute-start.27 = (bf16[2,256,1024]{2,1,0:T(8,128)(2,1)S(1)}, bf16[2,256,1024]{2,1,0:T(8,128)(2,1)S(1)}, u32[]{:S(2)}, u32[]{:S(2)}) collective-permute-start(bf16[2,256,1024]{2,1,0:T(8,128)(2,1)S(1)} %slice.174), channel_id=1, source_target_pairs={{0,8},{8,0},{16,24},{24,16},{1,9},{9,1},{17,25},{25,17},{2,10},{10... | collective-permute-start | bytes 3145736 | tf_op jit(solution)/shard_map/ppermute | solution.py:776
  793.9 32.0 %collective-permute-start.28 = (bf16[256,1024]{1,0:T(8,128)(2,1)S(1)}, bf16[256,1024]{1,0:T(8,128)(2,1)}, u32[]{:S(2)}, u32[]{:S(2)}) collective-permute-start(bf16[256,1024]{1,0:T(8,128)(2,1)S(1)} %fusion.17), channel_id=1, source_target_pairs={{0,16},{8,24},{16,0},{24,8},{1,17},{9,25},{17,1},{25,9},{2,18},{10... | collective-permute-start | bytes 1572872 | tf_op jit(solution)/shard_map/ppermute | solution.py:776
  830.1 25.6 %collective-permute-start.32 = (bf16[256,1024]{1,0:T(8,128)(2,1)}, bf16[256,1024]{1,0:T(8,128)(2,1)}, u32[]{:S(2)}, u32[]{:S(2)}) collective-permute-start(bf16[256,1024]{1,0:T(8,128)(2,1)} %fusion.18), channel_id=1, source_target_pairs={{0,16},{8,24},{16,0},{24,8},{1,17},{9,25},{17,1},{25,9},{2,18},{10... | collective-permute-start | bytes 1572872 | tf_op jit(solution)/shard_map/ppermute | solution.py:776
  846.8 18.0 %all-to-all-start.8 = ((bf16[4,2,128,512]{3,2,1,0:T(8,128)(2,1)}), bf16[4,2,128,512]{3,2,1,0:T(8,128)(2,1)S(1)}, u32[]{:S(2)}, u32[]{:S(2)}) async-start(bf16[4,2,128,512]{3,2,1,0:T(8,128)(2,1)} %maximum_bitcast_fusion), calls=%async_computation.10 | async-start | bytes 2097152 | tf_op jit(solution)/shard_map/all_to_all | solution.py:1070
  (74 other events, 1386.8 us)
Sparse Core Ops, SparseCore 0:
  10.7 164.6 all-gather.3
  182.8 130.0 all-gather.5
  317.1 80.0 all-gather.7
  469.0 106.5 reduce-scatter.2
  593.5 107.9 reduce-scatter.4
